TPU v7x, 32 devices: a whole 2x2x4 slice. The times are simulated.
32 devices in a mesh: dp: 8 (over z, x), tensor: 4 (over y, core).
Axes of the slice: x: 2, y: 2, z: 4, core: 2. Of those that a mesh axis runs over, the one named last changes fastest.
Arguments:
- tokens_in: bfloat16 [8192, 1024], P(('dp', 'tensor')), may hold values from -6 to 6
- cotangent: bfloat16 [8192, 1024], P(('dp', 'tensor')), may hold values from -6 to 6
- routes: int32 [2, 8192, 8], P(None, 'dp'), may hold values from 0 to 15, all different within a row
- attn_gain: bfloat16 [2, 1024], P(None, 'dp'), may hold values from 0.5 to 1.5
- w_query: bfloat16 [2, 1024, 1024], P(None, 'dp', 'tensor'), may hold values from -0.1875 to 0.1875
- key_projection: bfloat16 [2, 1024, 512], P(None, 'dp', 'tensor'), may hold values from -0.1875 to 0.1875
- value_projection: bfloat16 [2, 1024, 512], P(None, 'dp', 'tensor'), may hold values from -0.1875 to 0.1875
- w_out: bfloat16 [2, 1024, 1024], P(None, 'tensor', 'dp'), may hold values from -0.75 to 0.75
- moe_gain: bfloat16 [2, 1024], P(None, 'dp'), may hold values from 0.5 to 1.5
- w_router: bfloat16 [2, 1024, 16], P(None, 'dp'), may hold values from -0.09375 to 0.09375
- w_gate: bfloat16 [2, 16, 1024, 512], P(None, None, 'dp', 'tensor'), may hold values from -0.1875 to 0.1875
- w_up: bfloat16 [2, 16, 1024, 512], P(None, None, 'dp', 'tensor'), may hold values from -0.1875 to 0.1875
- w_down: bfloat16 [2, 16, 512, 1024], P(None, None, 'tensor', 'dp'), may hold values from -1 to 1
Outputs:
- result: float32 [8192, 1024], P(('dp', 'tensor'))
- input_grad: float32 [8192, 1024], P(('dp', 'tensor'))
- grad_attn_gain: float32 [2, 1024], P(None, 'dp')
- grad_w_query: float32 [2, 1024, 1024], P(None, 'dp', 'tensor')
- grad_w_key: float32 [2, 1024, 512], P(None, 'dp', 'tensor')
- grad_w_value: float32 [2, 1024, 512], P(None, 'dp', 'tensor')
- grad_w_out: float32 [2, 1024, 1024], P(None, 'tensor', 'dp')
- grad_moe_gain: float32 [2, 1024], P(None, 'dp')
- grad_w_router: float32 [2, 1024, 16], P(None, 'dp')
- grad_w_gate: float32 [2, 16, 1024, 512], P(None, None, 'dp', 'tensor')
- grad_w_up: float32 [2, 16, 1024, 512], P(None, None, 'dp', 'tensor')
- grad_w_down: float32 [2, 16, 512, 1024], P(None, None, 'tensor', 'dp')
Inputs may be any that keep to these rules, and one draw needn't show every extreme that they name: `routes`: each row names 8 different experts, and every expert is named by some row.
All inputs are finite; a program needn't handle non-finite values.
Results may differ from a plain program's by a relative error of at most 0.03.
Values may be sent and summed in bfloat16 or wider, within the bound.
No kernel may reach another device: no remote copies, remote signals or barrier semaphores. Data moves between devices by JAX's collectives and lax.ppermute only.
A program may use at most 256 MiB of HBM per device.

v0:
```python
import jax
import jax.numpy as jnp
from jax import lax
from jax.sharding import PartitionSpec as P

HEAD_SIZE = 64
TOPK = 8
EXPERTS = 16
LAYER_COUNT = 2
SEQUENCE_LENGTH = 1024
CAP = 512


epsilon = 1e-06
rope_base = 10000.0
masked_score = -1e30


def times_transposed(left_side, right_side):
    return lax.dot_general(
        left_side, right_side, (((1,), (1,)), ((), ())), preferred_element_type=jnp.float32
    )


def inner_rows(left_side, right_side):
    return lax.dot_general(
        left_side, right_side, (((0,), (0,)), ((), ())), preferred_element_type=jnp.float32
    )


def normalize(residual, norm_gain):
    root_scale = lax.rsqrt(jnp.mean(residual * residual, axis=-1, keepdims=True) + epsilon)
    normed = residual * root_scale
    return (normed, root_scale, (normed * norm_gain.astype(jnp.float32)).astype(jnp.bfloat16))


def normalize_back(grad_hidden, normed, root_scale, norm_gain):
    grad_gain = jnp.sum(grad_hidden * normed, axis=0)
    grad_normed = grad_hidden * norm_gain.astype(jnp.float32)
    inner_mean = jnp.mean(grad_normed * normed, axis=-1, keepdims=True)
    return (root_scale * (grad_normed - normed * inner_mean), grad_gain)


def rope_tables(row_count):
    positions = (jnp.arange(row_count, dtype=jnp.int32) % SEQUENCE_LENGTH).astype(jnp.float32)
    frequency = rope_base ** (-jnp.arange(0, HEAD_SIZE // 2, dtype=jnp.float32) * 2.0 / HEAD_SIZE)
    angles = positions[:, None] * frequency[None, :]
    return (jnp.cos(angles)[:, None, :], jnp.sin(angles)[:, None, :])


def apply_rotation(heads, cosine_table, sine_values):
    half_width = heads.shape[-1] // 2
    front_half = heads[..., :half_width]
    back_half = heads[..., half_width:]
    return jnp.concatenate(
        [
            front_half * cosine_table - back_half * sine_values,
            back_half * cosine_table + front_half * sine_values,
        ],
        axis=-1,
    )


def unrotate(heads, cosine_table, sine_values):
    half_width = heads.shape[-1] // 2
    front_half = heads[..., :half_width]
    back_half = heads[..., half_width:]
    return jnp.concatenate(
        [
            front_half * cosine_table + back_half * sine_values,
            back_half * cosine_table - front_half * sine_values,
        ],
        axis=-1,
    )


def score_block(query_block, key_block, row_start):
    block_rows = query_block.shape[0]
    scores = jnp.einsum(
        "qkgd,ckd->kgqc", query_block, key_block, preferred_element_type=jnp.float32
    ) * HEAD_SIZE ** (-0.5)
    causal = (row_start + jnp.arange(block_rows))[:, None] >= jnp.arange(SEQUENCE_LENGTH)[None, :]
    return jnp.where(causal, scores, masked_score)


def attend_forward(hidden_state, query_weight, key_matrix, value_matrix, cosine_table, sine_values):
    row_count = hidden_state.shape[0]
    query_heads = query_weight.shape[1] // HEAD_SIZE
    kv_heads = key_matrix.shape[1] // HEAD_SIZE
    query_rows = apply_rotation(
        jnp.dot(hidden_state, query_weight, preferred_element_type=jnp.float32).reshape(
            row_count, query_heads, HEAD_SIZE
        ),
        cosine_table,
        sine_values,
    ).astype(jnp.bfloat16)
    key_head_rows = apply_rotation(
        jnp.dot(hidden_state, key_matrix, preferred_element_type=jnp.float32).reshape(
            row_count, kv_heads, HEAD_SIZE
        ),
        cosine_table,
        sine_values,
    ).astype(jnp.bfloat16)
    value_head_rows = (
        jnp.dot(hidden_state, value_matrix, preferred_element_type=jnp.float32)
        .astype(jnp.bfloat16)
        .reshape(row_count, kv_heads, HEAD_SIZE)
    )
    block_rows = min(512, SEQUENCE_LENGTH)
    per_sequence = SEQUENCE_LENGTH // block_rows
    block_total = row_count // block_rows
    grouped_heads = query_rows.reshape(
        block_total, block_rows, kv_heads, query_heads // kv_heads, HEAD_SIZE
    )
    seq_keys = key_head_rows.reshape(
        row_count // SEQUENCE_LENGTH, SEQUENCE_LENGTH, kv_heads, HEAD_SIZE
    )
    seq_values = value_head_rows.reshape(
        row_count // SEQUENCE_LENGTH, SEQUENCE_LENGTH, kv_heads, HEAD_SIZE
    )

    def one_block(pieces):
        query_block, block_index = pieces
        sequence = block_index // per_sequence
        row_start = block_index % per_sequence * block_rows
        key_block = lax.dynamic_index_in_dim(seq_keys, sequence, 0, keepdims=False)
        value_block = lax.dynamic_index_in_dim(seq_values, sequence, 0, keepdims=False)
        scores = score_block(query_block, key_block, row_start)
        row_max = jnp.max(scores, axis=-1, keepdims=True)
        logsum = row_max + jnp.log(jnp.sum(jnp.exp(scores - row_max), axis=-1, keepdims=True))
        probs_low = jnp.exp(scores - logsum).astype(jnp.bfloat16)
        mixed = jnp.einsum(
            "kgqc,ckd->qkgd", probs_low, value_block, preferred_element_type=jnp.float32
        )
        return (mixed.astype(jnp.bfloat16), logsum)

    mixed, logsum = lax.map(one_block, (grouped_heads, jnp.arange(block_total, dtype=jnp.int32)))
    return (
        mixed.reshape(row_count, query_heads * HEAD_SIZE),
        logsum,
        query_rows,
        key_head_rows,
        value_head_rows,
    )


def attend_backward(
    grad_full,
    hidden_state,
    query_weight,
    key_matrix,
    value_matrix,
    out_weight,
    mixed,
    logsum,
    query_rows,
    key_head_rows,
    value_head_rows,
    cosine_table,
    sine_values,
):
    row_count = hidden_state.shape[0]
    query_heads = query_weight.shape[1] // HEAD_SIZE
    kv_heads = key_matrix.shape[1] // HEAD_SIZE
    query_group_width = query_heads // kv_heads
    grad_out_weight = inner_rows(mixed, grad_full)
    grad_mixed = times_transposed(grad_full, out_weight).astype(jnp.bfloat16)
    block_rows = min(512, SEQUENCE_LENGTH)
    per_sequence = SEQUENCE_LENGTH // block_rows
    block_total = row_count // block_rows
    sequences = row_count // SEQUENCE_LENGTH
    grouped_heads = query_rows.reshape(
        block_total, block_rows, kv_heads, query_group_width, HEAD_SIZE
    )
    grad_grouped = grad_mixed.reshape(
        block_total, block_rows, kv_heads, query_group_width, HEAD_SIZE
    )
    seq_keys = key_head_rows.reshape(sequences, SEQUENCE_LENGTH, kv_heads, HEAD_SIZE)
    seq_values = value_head_rows.reshape(sequences, SEQUENCE_LENGTH, kv_heads, HEAD_SIZE)

    def one_block(carried, pieces):
        key_grads, value_grads = carried
        query_block, grad_block, logsum_block, block_index = pieces
        sequence = block_index // per_sequence
        row_start = block_index % per_sequence * block_rows
        key_block = lax.dynamic_index_in_dim(seq_keys, sequence, 0, keepdims=False)
        value_block = lax.dynamic_index_in_dim(seq_values, sequence, 0, keepdims=False)
        probs = jnp.exp(score_block(query_block, key_block, row_start) - logsum_block)
        grad_probs = jnp.einsum(
            "qkgd,ckd->kgqc", grad_block, value_block, preferred_element_type=jnp.float32
        )
        grad_scores = (
            probs * (grad_probs - jnp.sum(probs * grad_probs, axis=-1, keepdims=True))
        ).astype(jnp.bfloat16)
        grad_query = jnp.einsum(
            "kgqc,ckd->qkgd", grad_scores, key_block, preferred_element_type=jnp.float32
        ) * HEAD_SIZE ** (-0.5)
        grad_key = jnp.einsum(
            "kgqc,qkgd->ckd", grad_scores, query_block, preferred_element_type=jnp.float32
        ) * HEAD_SIZE ** (-0.5)
        grad_value = jnp.einsum(
            "kgqc,qkgd->ckd",
            probs.astype(jnp.bfloat16),
            grad_block,
            preferred_element_type=jnp.float32,
        )
        return (
            (key_grads.at[sequence].add(grad_key), value_grads.at[sequence].add(grad_value)),
            grad_query,
        )

    empty_grads = jnp.zeros((sequences, SEQUENCE_LENGTH, kv_heads, HEAD_SIZE), jnp.float32)
    (key_grads, value_grads), query_grads = lax.scan(
        one_block,
        (empty_grads, empty_grads),
        (grouped_heads, grad_grouped, logsum, jnp.arange(block_total, dtype=jnp.int32)),
    )
    grad_query_low = (
        unrotate(query_grads.reshape(row_count, query_heads, HEAD_SIZE), cosine_table, sine_values)
        .reshape(row_count, query_heads * HEAD_SIZE)
        .astype(jnp.bfloat16)
    )
    grad_key_low = (
        unrotate(key_grads.reshape(row_count, kv_heads, HEAD_SIZE), cosine_table, sine_values)
        .reshape(row_count, kv_heads * HEAD_SIZE)
        .astype(jnp.bfloat16)
    )
    grad_value_low = value_grads.reshape(row_count, kv_heads * HEAD_SIZE).astype(jnp.bfloat16)
    grad_hidden = (
        times_transposed(grad_query_low, query_weight)
        + times_transposed(grad_key_low, key_matrix)
        + times_transposed(grad_value_low, value_matrix)
    )
    return (
        grad_hidden,
        inner_rows(hidden_state, grad_query_low),
        inner_rows(hidden_state, grad_key_low),
        inner_rows(hidden_state, grad_value_low),
        grad_out_weight,
    )


def gate_probs_of(hidden_state, router_weight, route_rows):
    logits = jnp.dot(hidden_state, router_weight, preferred_element_type=jnp.float32)
    onehot = (route_rows[:, :, None] == jnp.arange(EXPERTS, dtype=jnp.int32)[None, None, :]).astype(
        jnp.float32
    )
    chosen = jnp.sum(onehot * logits[:, None, :], axis=-1)
    return (jax.nn.softmax(chosen, axis=-1), onehot)


def plan_slots(route_rows, gate_probs):
    row_count = route_rows.shape[0]
    sequences = row_count // SEQUENCE_LENGTH
    slot_width = sequences * CAP
    flat_routes = route_rows.reshape(sequences, SEQUENCE_LENGTH * TOPK)
    onehot = (
        flat_routes[:, :, None] == jnp.arange(EXPERTS, dtype=jnp.int32)[None, None, :]
    ).astype(jnp.int32)
    before = jnp.cumsum(onehot, axis=1) - onehot
    slot_place = jnp.sum(before * onehot, axis=-1)
    offsets = jnp.arange(sequences, dtype=jnp.int32)[:, None] * CAP
    target = jnp.where(
        slot_place < CAP, flat_routes * slot_width + offsets + slot_place, EXPERTS * slot_width
    ).reshape(-1)
    token_index = jnp.arange(row_count * TOPK, dtype=jnp.int32) // TOPK
    source = (
        jnp.full((EXPERTS * slot_width,), row_count, jnp.int32)
        .at[target]
        .set(token_index, mode="drop")
    )
    slot_gate = (
        jnp.zeros((EXPERTS * slot_width,), jnp.float32)
        .at[target]
        .set(gate_probs.reshape(-1), mode="drop")
    )
    return (target, source.reshape(EXPERTS, slot_width), slot_gate.reshape(EXPERTS, slot_width))


def experts_forward(hidden_state, source, slot_gate, gate_weight, up_weight, down_weight):
    row_count = hidden_state.shape[0]
    padded = jnp.concatenate(
        [hidden_state, jnp.zeros((1, hidden_state.shape[1]), hidden_state.dtype)], axis=0
    )

    def one_expert(accumulated, pieces):
        slot_source, gate_column, gate_matrix, up_matrix, down_matrix = pieces
        buffer = padded[slot_source]
        gate_part = jnp.dot(buffer, gate_matrix, preferred_element_type=jnp.float32)
        up_part = jnp.dot(buffer, up_matrix, preferred_element_type=jnp.float32)
        active = (gate_column[:, None] * jax.nn.silu(gate_part) * up_part).astype(jnp.bfloat16)
        produced = jnp.dot(active, down_matrix, preferred_element_type=jnp.float32)
        return (accumulated.at[slot_source].add(produced, mode="drop"), (gate_part, up_part))

    empty_rows = jnp.zeros((row_count, hidden_state.shape[1]), jnp.float32)
    return lax.scan(
        one_expert, empty_rows, (source, slot_gate, gate_weight, up_weight, down_weight)
    )


def experts_backward(
    hidden_state, grad_full, source, slot_gate, saved_parts, gate_weight, up_weight, down_weight
):
    row_count = hidden_state.shape[0]
    padded = jnp.concatenate(
        [hidden_state, jnp.zeros((1, hidden_state.shape[1]), hidden_state.dtype)], axis=0
    )
    padded_grad = jnp.concatenate(
        [grad_full, jnp.zeros((1, grad_full.shape[1]), grad_full.dtype)], axis=0
    )

    def one_expert(accumulated, pieces):
        slot_source, gate_column, gate_part, up_part, gate_matrix, up_matrix, down_matrix = pieces
        buffer = padded[slot_source]
        grad_rows = padded_grad[slot_source]
        logistic = jax.nn.sigmoid(gate_part)
        swished = jax.nn.silu(gate_part)
        active = (gate_column[:, None] * swished * up_part).astype(jnp.bfloat16)
        grad_down = inner_rows(active, grad_rows)
        grad_active = times_transposed(grad_rows, down_matrix)
        grad_slot = jnp.sum(grad_active * swished * up_part, axis=-1)
        grad_product = gate_column[:, None] * grad_active
        grad_gate_part = (
            grad_product * up_part * logistic * (1.0 + gate_part * (1.0 - logistic))
        ).astype(jnp.bfloat16)
        grad_up_part = (grad_product * swished).astype(jnp.bfloat16)
        grad_buffer = times_transposed(grad_gate_part, gate_matrix) + times_transposed(
            grad_up_part, up_matrix
        )
        outputs = (
            grad_slot,
            inner_rows(buffer, grad_gate_part),
            inner_rows(buffer, grad_up_part),
            grad_down,
        )
        return (accumulated.at[slot_source].add(grad_buffer, mode="drop"), outputs)

    empty_rows = jnp.zeros((row_count, hidden_state.shape[1]), jnp.float32)
    gate_parts, up_parts = saved_parts
    accumulated, outputs = lax.scan(
        one_expert,
        empty_rows,
        (source, slot_gate, gate_parts, up_parts, gate_weight, up_weight, down_weight),
    )
    return (accumulated, outputs[0], outputs[1], outputs[2], outputs[3])


def local(
    tokens_in,
    cotangent,
    routes,
    attn_gain,
    w_query,
    key_projection,
    value_projection,
    w_out,
    moe_gain,
    w_router,
    w_gate,
    w_up,
    w_down,
):
    rows_own = tokens_in.shape[0]
    group_rows = rows_own * lax.axis_size("tensor")
    cosine_table, sine_values = rope_tables(group_rows)
    own_start = lax.axis_index("tensor") * rows_own

    def widen(values):
        return lax.all_gather(values, "tensor", axis=0, tiled=True)

    def narrow(values):
        return lax.psum_scatter(
            values.astype(jnp.bfloat16), "tensor", scatter_dimension=0, tiled=True
        ).astype(jnp.float32)

    def widen_grad(values):
        return lax.all_gather(values.astype(jnp.bfloat16), "tensor", axis=0, tiled=True)

    residual = tokens_in.astype(jnp.float32)
    records = []
    for layer_index in range(LAYER_COUNT):
        fetched = (
            lax.all_gather(attn_gain[layer_index], "dp", axis=0, tiled=True),
            lax.all_gather(w_query[layer_index], "dp", axis=0, tiled=True),
            lax.all_gather(key_projection[layer_index], "dp", axis=0, tiled=True),
            lax.all_gather(value_projection[layer_index], "dp", axis=0, tiled=True),
            lax.all_gather(w_out[layer_index], "dp", axis=1, tiled=True),
            lax.all_gather(moe_gain[layer_index], "dp", axis=0, tiled=True),
            lax.all_gather(w_router[layer_index], "dp", axis=0, tiled=True),
            lax.all_gather(w_gate[layer_index], "dp", axis=1, tiled=True),
            lax.all_gather(w_up[layer_index], "dp", axis=1, tiled=True),
            lax.all_gather(w_down[layer_index], "dp", axis=2, tiled=True),
        )
        (
            gain_attn,
            query_weight,
            key_matrix,
            value_matrix,
            out_weight,
            gain_moe,
            router_weight,
            gate_weight,
            up_weight,
            down_weight,
        ) = fetched
        normed_attn, scale_attn, low_attn = normalize(residual, gain_attn)
        hidden_attn = widen(low_attn)
        mixed, logsum, query_rows, key_head_rows, value_head_rows = attend_forward(
            hidden_attn, query_weight, key_matrix, value_matrix, cosine_table, sine_values
        )
        residual = residual + narrow(jnp.dot(mixed, out_weight, preferred_element_type=jnp.float32))
        normed_moe, scale_moe, low_moe = normalize(residual, gain_moe)
        hidden_moe = widen(low_moe)
        gate_probs, onehot = gate_probs_of(hidden_moe, router_weight, routes[layer_index])
        target, source, slot_gate = plan_slots(routes[layer_index], gate_probs)
        moe_out, saved_parts = experts_forward(
            hidden_moe, source, slot_gate, gate_weight, up_weight, down_weight
        )
        residual = residual + narrow(moe_out)
        kept_weights = None
        records.append(
            (
                normed_attn,
                scale_attn,
                hidden_attn,
                mixed,
                logsum,
                query_rows,
                key_head_rows,
                value_head_rows,
                normed_moe,
                scale_moe,
                low_moe,
                hidden_moe,
                target,
                source,
                slot_gate,
                saved_parts,
                kept_weights,
            )
        )
    grad = cotangent.astype(jnp.float32)
    layer_terms = []
    for layer_index in reversed(range(LAYER_COUNT)):
        (
            normed_attn,
            scale_attn,
            hidden_attn,
            mixed,
            logsum,
            query_rows,
            key_head_rows,
            value_head_rows,
            normed_moe,
            scale_moe,
            low_moe,
            hidden_moe,
            target,
            source,
            slot_gate,
            saved_parts,
            kept_weights,
        ) = records[layer_index]
        fetched = (
            lax.all_gather(attn_gain[layer_index], "dp", axis=0, tiled=True),
            lax.all_gather(w_query[layer_index], "dp", axis=0, tiled=True),
            lax.all_gather(key_projection[layer_index], "dp", axis=0, tiled=True),
            lax.all_gather(value_projection[layer_index], "dp", axis=0, tiled=True),
            lax.all_gather(w_out[layer_index], "dp", axis=1, tiled=True),
            lax.all_gather(moe_gain[layer_index], "dp", axis=0, tiled=True),
            lax.all_gather(w_router[layer_index], "dp", axis=0, tiled=True),
            lax.all_gather(w_gate[layer_index], "dp", axis=1, tiled=True),
            lax.all_gather(w_up[layer_index], "dp", axis=1, tiled=True),
            lax.all_gather(w_down[layer_index], "dp", axis=2, tiled=True),
        )
        (
            gain_attn,
            query_weight,
            key_matrix,
            value_matrix,
            out_weight,
            gain_moe,
            router_weight,
            gate_weight,
            up_weight,
            down_weight,
        ) = fetched
        grad_full = widen_grad(grad)
        grad_moe_hidden, grad_slots, grad_gate_weight, grad_up_weight, grad_down_weight = (
            experts_backward(
                hidden_moe,
                grad_full,
                source,
                slot_gate,
                saved_parts,
                gate_weight,
                up_weight,
                down_weight,
            )
        )
        slot_total = grad_slots.shape[0] * grad_slots.shape[1]
        flat_slots = grad_slots.reshape(-1)
        pair_grad = jnp.where(
            target < slot_total, flat_slots[jnp.minimum(target, slot_total - 1)], 0.0
        ).reshape(-1, TOPK)
        grad_moe_own, pair_own = (
            lax.psum_scatter(
                grad_moe_hidden.astype(jnp.bfloat16), "tensor", scatter_dimension=0, tiled=True
            ).astype(jnp.float32),
            lax.psum_scatter(
                pair_grad.astype(jnp.bfloat16), "tensor", scatter_dimension=0, tiled=True
            ).astype(jnp.float32),
        )
        own_routes = lax.dynamic_slice_in_dim(routes[layer_index], own_start, rows_own, 0)
        own_probs, own_onehot = gate_probs_of(low_moe, router_weight, own_routes)
        grad_chosen = own_probs * (pair_own - jnp.sum(own_probs * pair_own, axis=-1, keepdims=True))
        grad_logits = jnp.sum(own_onehot * grad_chosen[:, :, None], axis=1).astype(jnp.bfloat16)
        grad_router = inner_rows(low_moe, grad_logits)
        grad_moe_own = grad_moe_own + times_transposed(grad_logits, router_weight)
        grad_residual, grad_gain_moe = normalize_back(grad_moe_own, normed_moe, scale_moe, gain_moe)
        grad = grad + grad_residual
        grad_full = widen_grad(grad)
        grad_attn_hidden, grad_query_weight, grad_key_weight, grad_value_weight, grad_out_weight = (
            attend_backward(
                grad_full,
                hidden_attn,
                query_weight,
                key_matrix,
                value_matrix,
                out_weight,
                mixed,
                logsum,
                query_rows,
                key_head_rows,
                value_head_rows,
                cosine_table,
                sine_values,
            )
        )
        grad_attn_own = lax.psum_scatter(
            grad_attn_hidden.astype(jnp.bfloat16), "tensor", scatter_dimension=0, tiled=True
        ).astype(jnp.float32)
        grad_residual, grad_gain_attn = normalize_back(
            grad_attn_own, normed_attn, scale_attn, gain_attn
        )
        grad = grad + grad_residual
        gain_attn_sum, gain_moe_sum, router_sum = (
            lax.psum(grad_gain_attn.astype(jnp.bfloat16), "tensor").astype(jnp.float32),
            lax.psum(grad_gain_moe.astype(jnp.bfloat16), "tensor").astype(jnp.float32),
            lax.psum(grad_router.astype(jnp.bfloat16), "tensor").astype(jnp.float32),
        )
        grad_terms = (
            lax.psum_scatter(gain_attn_sum, "dp", scatter_dimension=0, tiled=True),
            lax.psum_scatter(grad_query_weight, "dp", scatter_dimension=0, tiled=True),
            lax.psum_scatter(grad_key_weight, "dp", scatter_dimension=0, tiled=True),
            lax.psum_scatter(grad_value_weight, "dp", scatter_dimension=0, tiled=True),
            lax.psum_scatter(grad_out_weight, "dp", scatter_dimension=1, tiled=True),
            lax.psum_scatter(gain_moe_sum, "dp", scatter_dimension=0, tiled=True),
            lax.psum_scatter(router_sum, "dp", scatter_dimension=0, tiled=True),
            lax.psum_scatter(grad_gate_weight, "dp", scatter_dimension=1, tiled=True),
            lax.psum_scatter(grad_up_weight, "dp", scatter_dimension=1, tiled=True),
            lax.psum_scatter(grad_down_weight, "dp", scatter_dimension=2, tiled=True),
        )
        layer_terms.insert(0, grad_terms)
    stacked = tuple(
        (jnp.stack([grad_terms[member] for grad_terms in layer_terms]) for member in range(10))
    )
    return (
        residual,
        grad,
        stacked[0],
        stacked[1],
        stacked[2],
        stacked[3],
        stacked[4],
        stacked[5],
        stacked[6],
        stacked[7],
        stacked[8],
        stacked[9],
    )


def solution(mesh):
    placed = (
        P(("dp", "tensor"), None),
        P(("dp", "tensor"), None),
        P(None, "dp", None),
        P(None, "dp"),
        P(None, "dp", "tensor"),
        P(None, "dp", "tensor"),
        P(None, "dp", "tensor"),
        P(None, "tensor", "dp"),
        P(None, "dp"),
        P(None, "dp", None),
        P(None, None, "dp", "tensor"),
        P(None, None, "dp", "tensor"),
        P(None, None, "tensor", "dp"),
    )
    return jax.shard_map(
        local,
        mesh=mesh,
        in_specs=placed,
        out_specs=(
            P(("dp", "tensor"), None),
            P(("dp", "tensor"), None),
            P(None, "dp"),
            P(None, "dp", "tensor"),
            P(None, "dp", "tensor"),
            P(None, "dp", "tensor"),
            P(None, "tensor", "dp"),
            P(None, "dp"),
            P(None, "dp", None),
            P(None, None, "dp", "tensor"),
            P(None, None, "dp", "tensor"),
            P(None, None, "tensor", "dp"),
        ),
        check_vma=False,
    )
```

profile of v0, /device:TPU:0, one launch (start us, length us, event | category | flops | bytes accessed | tf_op | source)
XLA Modules:
  0.0 4948.6 jit_solution(8551181332845144494)
XLA Ops:
  344.2 58.3 %all-gather.53.cloned.1.call-done = bf16[1,16,1024,128]{3,2,1,0:T(8,128)(2,1)} async-done(((bf16[1,16,128,128]{3,2,1,0:T(8,128)(2,1)}), bf16[1,16,1024,128]{3,2,1,0:T(8,128)(2,1)}) %all-gather.53.cloned.1.call-update) | async-done | bytes 4194320 | tf_op jit(solution)/shard_map/all_gather | solution.py:391
  402.6 75.4 %all-gather.55.cloned.1.call-done = bf16[1,16,128,1024]{3,2,1,0:T(8,128)(2,1)} async-done(((bf16[1,16,128,128]{3,2,1,0:T(8,128)(2,1)}), bf16[1,16,128,1024]{3,2,1,0:T(8,128)(2,1)}) %all-gather.55.cloned.1.call-update) | async-done | bytes 4194320 | tf_op jit(solution)/shard_map/all_gather | solution.py:392
  485.2 312.4 %while.131 = (s32[]{:T(128)}, f32[1024,1024]{1,0:T(8,128)}, f32[16,512,128]{2,1,0:T(8,128)}, f32[16,512,128]{2,1,0:T(8,128)}, s32[16,512]{1,0:T(8,128)S(1)}, /*i...) while((s32[]{:T(128)}, f32[1024,1024]{1,0:T(8,128)}, ...), condition=%wide.region_17.18_spmd, body=%wide.region_15.17_spmd.sunk | while | flops 403639808 | bytes 14967413 | solution.py:296
  1155.6 74.7 %all-gather.59.cloned.1.call-done = bf16[1,16,1024,128]{3,2,1,0:T(8,128)(2,1)} async-done(((bf16[1,16,128,128]{3,2,1,0:T(8,128)(2,1)}), bf16[1,16,1024,128]{3,2,1,0:T(8,128)(2,1)}) %all-gather.59.cloned.1.call-update) | async-done | bytes 4194320 | tf_op jit(solution)/shard_map/all_gather | solution.py:391
  1230.2 75.4 %all-gather.61.cloned.1.call-done = bf16[1,16,128,1024]{3,2,1,0:T(8,128)(2,1)} async-done(((bf16[1,16,128,128]{3,2,1,0:T(8,128)(2,1)}), bf16[1,16,128,1024]{3,2,1,0:T(8,128)(2,1)}) %all-gather.61.cloned.1.call-update) | async-done | bytes 4194320 | tf_op jit(solution)/shard_map/all_gather | solution.py:392
  1313.3 304.5 %while.133 = (s32[]{:T(128)}, f32[1024,1024]{1,0:T(8,128)}, f32[16,512,128]{2,1,0:T(8,128)}, f32[16,512,128]{2,1,0:T(8,128)}, s32[16,512]{1,0:T(8,128)S(1)}, /*i...) while((s32[]{:T(128)}, f32[1024,1024]{1,0:T(8,128)}, ...), condition=%wide.region_36.37_spmd, body=%wide.region_34.36_spmd.sunk | while | flops 403639808 | bytes 14967413 | solution.py:296
  1633.0 551.4 %while.134 = (s32[]{:T(128)}, f32[1024,1024]{1,0:T(8,128)}, bf16[16,512]{1,0:T(8,128)(2,1)S(1)}, f32[16,1024,128]{2,1,0:T(8,128)}, f32[16,1024,128]{2,1,0:T(8,12...) while((s32[]{:T(128)}, f32[1024,1024]{1,0:T(8,128)}, ...), condition=%wide.region_41.42_spmd, body=%wide.region_38.41_spmd.sunk | while | flops 807930880 | bytes 31491272 | solution.py:340
  2324.9 74.2 %while.136 = (s32[]{:T(128)}, f32[1,1024,2,64]{1,3,2,0:T(8,128)S(1)}, f32[1,1024,2,64]{1,3,2,0:T(8,128)}, f32[2,512,2,2,64]{1,0,4,3,2:T(2,128)}, s32[2]{0:T(128)...) while((s32[]{:T(128)}, ...), condition=%wide.region_53.54_spmd.clone, body=%wide.region_50.53_spmd.clone.sunk | while | flops 1375205888 | bytes 127201864 | solution.py:213
  2522.1 575.0 %while.135 = (s32[]{:T(128)}, f32[1024,1024]{1,0:T(8,128)}, bf16[16,512]{1,0:T(8,128)(2,1)S(1)}, f32[16,1024,128]{2,1,0:T(8,128)}, f32[16,1024,128]{2,1,0:T(8,12...) while((s32[]{:T(128)}, f32[1024,1024]{1,0:T(8,128)}, ...), condition=%wide.region_59.60_spmd, body=%wide.region_56.59_spmd.sunk | while | flops 807930880 | bytes 31491272 | solution.py:340
  3238.0 71.8 %while.137 = (s32[]{:T(128)}, f32[1,1024,2,64]{1,3,2,0:T(8,128)S(1)}, f32[1,1024,2,64]{1,3,2,0:T(8,128)}, f32[2,512,2,2,64]{1,0,4,3,2:T(2,128)}, s32[2]{0:T(128)...) while((s32[]{:T(128)}, ...), condition=%wide.region_71.72_spmd.clone, body=%wide.region_68.71_spmd.clone.sunk | while | flops 1375205888 | bytes 126153256 | solution.py:213
  3394.6 59.1 %reduce-scatter.57.cloned.1.call-done = f32[128,128]{1,0:T(8,128)} async-done(((f32[1024,128]{1,0:T(8,128)}), f32[128,128]{1,0:T(8,128)}) %reduce-scatter.57.cloned.1.call-update) | async-done | bytes 65552 | tf_op jit(solution)/shard_map/reduce_scatter | solution.py:556
  3453.6 64.2 %reduce-scatter.55.cloned.1.call-done = f32[128,128]{1,0:T(8,128)} async-done(((f32[1024,128]{1,0:T(8,128)}), f32[128,128]{1,0:T(8,128)}) %reduce-scatter.55.cloned.1.call-update) | async-done | bytes 65552 | tf_op jit(solution)/shard_map/reduce_scatter | solution.py:556
  3519.3 63.2 %reduce-scatter.53.cloned.1.call-done = f32[128,128]{1,0:T(8,128)} async-done(((f32[1024,128]{1,0:T(8,128)}), f32[128,128]{1,0:T(8,128)}) %reduce-scatter.53.cloned.1.call-update) | async-done | bytes 65552 | tf_op jit(solution)/shard_map/reduce_scatter | solution.py:555
  3582.5 64.3 %reduce-scatter.51.cloned.1.call-done = f32[128,128]{1,0:T(8,128)} async-done(((f32[1024,128]{1,0:T(8,128)}), f32[128,128]{1,0:T(8,128)}) %reduce-scatter.51.cloned.1.call-update) | async-done | bytes 65552 | tf_op jit(solution)/shard_map/reduce_scatter | solution.py:555
  3648.3 65.1 %reduce-scatter.61.cloned.1.call-done = f32[256,128]{1,0:T(8,128)} async-done(((f32[256,1024]{1,0:T(8,128)}), f32[256,128]{1,0:T(8,128)}) %reduce-scatter.61.cloned.1.call-update) | async-done | bytes 131088 | tf_op jit(solution)/shard_map/reduce_scatter | solution.py:557
  3713.4 66.3 %reduce-scatter.59.cloned.1.call-done = f32[256,128]{1,0:T(8,128)} async-done(((f32[256,1024]{1,0:T(8,128)}), f32[256,128]{1,0:T(8,128)}) %reduce-scatter.59.cloned.1.call-update) | async-done | bytes 131088 | tf_op jit(solution)/shard_map/reduce_scatter | solution.py:557
  3781.4 65.2 %reduce-scatter.49.cloned.1.call-done = f32[128,256]{1,0:T(8,128)} async-done(((f32[1024,256]{1,0:T(8,128)}), f32[128,256]{1,0:T(8,128)}) %reduce-scatter.49.cloned.1.call-update) | async-done | bytes 131088 | tf_op jit(solution)/shard_map/reduce_scatter | solution.py:554
  3846.6 66.2 %reduce-scatter.47.cloned.1.call-done = f32[128,256]{1,0:T(8,128)} async-done(((f32[1024,256]{1,0:T(8,128)}), f32[128,256]{1,0:T(8,128)}) %reduce-scatter.47.cloned.1.call-update) | async-done | bytes 131088 | tf_op jit(solution)/shard_map/reduce_scatter | solution.py:554
  4026.5 151.1 %reduce-scatter.77.cloned.1.call-done = f32[16,128,128]{2,1,0:T(8,128)} async-done(((f32[16,128,1024]{2,1,0:T(8,128)}), f32[16,128,128]{2,1,0:T(8,128)}) %reduce-scatter.77.cloned.1.call-update) | async-done | bytes 1048592 | tf_op jit(solution)/shard_map/reduce_scatter | solution.py:562
  4177.6 151.9 %reduce-scatter.75.cloned.1.call-done = f32[16,128,128]{2,1,0:T(8,128)} async-done(((f32[16,128,1024]{2,1,0:T(8,128)}), f32[16,128,128]{2,1,0:T(8,128)}) %reduce-scatter.75.cloned.1.call-update) | async-done | bytes 1048592 | tf_op jit(solution)/shard_map/reduce_scatter | solution.py:562
  4332.6 149.4 %reduce-scatter.73.cloned.1.call-done = f32[16,128,128]{2,1,0:T(8,128)} async-done(((f32[16,1024,128]{2,1,0:T(8,128)}), f32[16,128,128]{2,1,0:T(8,128)}) %reduce-scatter.73.cloned.1.call-update) | async-done | bytes 1048592 | tf_op jit(solution)/shard_map/reduce_scatter | solution.py:561
  4481.9 152.0 %reduce-scatter.71.cloned.1.call-done = f32[16,128,128]{2,1,0:T(8,128)} async-done(((f32[16,1024,128]{2,1,0:T(8,128)}), f32[16,128,128]{2,1,0:T(8,128)}) %reduce-scatter.71.cloned.1.call-update) | async-done | bytes 1048592 | tf_op jit(solution)/shard_map/reduce_scatter | solution.py:561
  4637.0 149.4 %reduce-scatter.69.cloned.1.call-done = f32[16,128,128]{2,1,0:T(8,128)} async-done(((f32[16,1024,128]{2,1,0:T(8,128)}), f32[16,128,128]{2,1,0:T(8,128)}) %reduce-scatter.69.cloned.1.call-update) | async-done | bytes 1048592 | tf_op jit(solution)/shard_map/reduce_scatter | solution.py:560
  4786.4 152.1 %reduce-scatter.67.cloned.1.call-done = f32[16,128,128]{2,1,0:T(8,128)} async-done(((f32[16,1024,128]{2,1,0:T(8,128)}), f32[16,128,128]{2,1,0:T(8,128)}) %reduce-scatter.67.cloned.1.call-update) | async-done | bytes 1048592 | tf_op jit(solution)/shard_map/reduce_scatter | solution.py:560
  (1552 shorter events, 3244.7 us)
Async XLA Ops:
  34.4 190.7 %reduce-scatter.27.cloned.1.call-start = ((), (), s32[]{:S(2)}) async-start(), calls=%async_computation.27 | async-start | bytes 2621440 | tf_op jit(solution)/shard_map/reduce_scatter | solution.py:372
  229.7 172.8 %all-gather.53.cloned.1.call-start = ((), (), s32[]{:S(2)}) async-start(), calls=%async_computation.61 | async-start | bytes 4718592 | tf_op jit(solution)/shard_map/all_gather | solution.py:391
  230.9 247.1 %all-gather.55.cloned.1.call-start = ((), (), s32[]{:S(2)}) async-start(), calls=%async_computation.62 | async-start | bytes 4718592 | tf_op jit(solution)/shard_map/all_gather | solution.py:392
  241.7 590.3 %reduce-scatter.29.cloned.1.call-start = ((), (), s32[]{:S(2)}) async-start(), calls=%async_computation.29 | async-start | bytes 2621440 | tf_op jit(solution)/shard_map/reduce_scatter | solution.py:372
  834.9 195.9 %reduce-scatter.31.cloned.1.call-start = ((), (), s32[]{:S(2)}) async-start(), calls=%async_computation.31 | async-start | bytes 2621440 | tf_op jit(solution)/shard_map/reduce_scatter | solution.py:372
  1034.7 195.5 %all-gather.59.cloned.1.call-start = ((), (), s32[]{:S(2)}) async-start(), calls=%async_computation.64 | async-start | bytes 4718592 | tf_op jit(solution)/shard_map/all_gather | solution.py:391
  1035.5 270.2 %all-gather.61.cloned.1.call-start = ((), (), s32[]{:S(2)}) async-start(), calls=%async_computation.65 | async-start | bytes 4718592 | tf_op jit(solution)/shard_map/all_gather | solution.py:392
  1036.0 1217.8 %reduce-scatter.37.cloned.1.call-start = ((), (), s32[]{:S(2)}) async-start(), calls=%async_computation.36 | async-start | bytes 20480 | tf_op jit(solution)/shard_map/reduce_scatter | solution.py:510
  2481.1 687.3 %reduce-scatter.43.cloned.1.call-start = ((), (), s32[]{:S(2)}) async-start(), calls=%async_computation.41 | async-start | bytes 20480 | tf_op jit(solution)/shard_map/reduce_scatter | solution.py:510
  3357.8 160.0 %reduce-scatter.55.cloned.1.call-start = ((), (), s32[]{:S(2)}) async-start(), calls=%async_computation.48 | async-start | bytes 589824 | tf_op jit(solution)/shard_map/reduce_scatter | solution.py:556
  3359.4 223.0 %reduce-scatter.53.cloned.1.call-start = ((), (), s32[]{:S(2)}) async-start(), calls=%async_computation.47 | async-start | bytes 589824 | tf_op jit(solution)/shard_map/reduce_scatter | solution.py:555
  3362.7 284.1 %reduce-scatter.51.cloned.1.call-start = ((), (), s32[]{:S(2)}) async-start(), calls=%async_computation.46 | async-start | bytes 589824 | tf_op jit(solution)/shard_map/reduce_scatter | solution.py:555
  3364.3 349.0 %reduce-scatter.61.cloned.1.call-start = ((), (), s32[]{:S(2)}) async-start(), calls=%async_computation.51 | async-start | bytes 1179648 | tf_op jit(solution)/shard_map/reduce_scatter | solution.py:557
  3367.9 411.8 %reduce-scatter.59.cloned.1.call-start = ((), (), s32[]{:S(2)}) async-start(), calls=%async_computation.50 | async-start | bytes 1179648 | tf_op jit(solution)/shard_map/reduce_scatter | solution.py:557
  3371.4 475.1 %reduce-scatter.49.cloned.1.call-start = ((), (), s32[]{:S(2)}) async-start(), calls=%async_computation.45 | async-start | bytes 1179648 | tf_op jit(solution)/shard_map/reduce_scatter | solution.py:554
  3374.8 538.0 %reduce-scatter.47.cloned.1.call-start = ((), (), s32[]{:S(2)}) async-start(), calls=%async_computation.44 | async-start | bytes 1179648 | tf_op jit(solution)/shard_map/reduce_scatter | solution.py:554
  3377.7 591.3 %reduce-scatter.63.cloned.1.call-start = ((), (), s32[]{:S(2)}) async-start(), calls=%async_computation.52 | async-start | bytes 73728 | tf_op jit(solution)/shard_map/reduce_scatter | solution.py:559
  3387.8 637.4 %reduce-scatter.65.cloned.1.call-start = ((), (), s32[]{:S(2)}) async-start(), calls=%async_computation.53 | async-start | bytes 73728 | tf_op jit(solution)/shard_map/reduce_scatter | solution.py:559
  3389.3 788.3 %reduce-scatter.77.cloned.1.call-start = ((), (), s32[]{:S(2)}) async-start(), calls=%async_computation.59 | async-start | bytes 9437184 | tf_op jit(solution)/shard_map/reduce_scatter | solution.py:562
  3389.9 939.6 %reduce-scatter.75.cloned.1.call-start = ((), (), s32[]{:S(2)}) async-start(), calls=%async_computation.58 | async-start | bytes 9437184 | tf_op jit(solution)/shard_map/reduce_scatter | solution.py:562
  3390.5 1091.5 %reduce-scatter.73.cloned.1.call-start = ((), (), s32[]{:S(2)}) async-start(), calls=%async_computation.57 | async-start | bytes 9437184 | tf_op jit(solution)/shard_map/reduce_scatter | solution.py:561
  3391.2 1242.7 %reduce-scatter.71.cloned.1.call-start = ((), (), s32[]{:S(2)}) async-start(), calls=%async_computation.56 | async-start | bytes 9437184 | tf_op jit(solution)/shard_map/reduce_scatter | solution.py:561
  3391.8 1394.6 %reduce-scatter.69.cloned.1.call-start = ((), (), s32[]{:S(2)}) async-start(), calls=%async_computation.55 | async-start | bytes 9437184 | tf_op jit(solution)/shard_map/reduce_scatter | solution.py:560
  3392.5 1545.9 %reduce-scatter.67.cloned.1.call-start = ((), (), s32[]{:S(2)}) async-start(), calls=%async_computation.54 | async-start | bytes 9437184 | tf_op jit(solution)/shard_map/reduce_scatter | solution.py:560
  (187 other events, 10832.6 us)
Sparse Core Ops, SparseCore 0:
  254.2 73.7 all-gather.50
  330.8 71.6 all-gather.52
  404.7 73.2 all-gather.54
  1082.0 73.4 all-gather.56
  1158.5 71.6 all-gather.58
  1232.3 73.2 all-gather.60
  2411.7 31.4 reduce-scatter.38
  3320.9 31.4 reduce-scatter.44
  3390.0 63.5 reduce-scatter.56
  3456.8 60.9 reduce-scatter.54
  3521.5 60.9 reduce-scatter.52
  3585.8 60.8 reduce-scatter.50
  3650.4 62.9 reduce-scatter.60
  3716.8 62.8 reduce-scatter.58
  3784.1 62.4 reduce-scatter.48
  3850.4 62.3 reduce-scatter.46
  3916.2 52.7 reduce-scatter.62
  3972.4 52.6 reduce-scatter.64
  4029.1 148.4 reduce-scatter.76
  4181.1 148.3 reduce-scatter.74
  4333.5 148.3 reduce-scatter.72
  4485.4 148.4 reduce-scatter.70
  4638.0 148.3 reduce-scatter.68
  4790.0 148.4 reduce-scatter.66
  (17 shorter events, 427.0 us)
where the time goes:
time: 4980 us; the launch traced here: 4950 us
  waiting for transfers between devices  2090 us (42%)
  local copies, waits for them, and re-layouts  845 us (17%)
  other arithmetic  787 us (16%)
  matrix products  764 us (15%)
  blocking collectives  412 us (8%)
    scatter-add x32, other arithmetic, one_expert(): return (accumulated.at[slot_source].add(grad_buffer, mode='drop'), outputs)  343 us
    scatter-add x32, other arithmetic, one_expert(): accumulated.at[slot_source].add(produced, mode='drop')  316 us
    reduce_scatter x2, waiting for transfers between devices, local(): lax.psum_scatter(grad_down_weight, 'dp', scatter_dimension=2, tiled=True)  303 us
    reduce_scatter x2, waiting for transfers between devices, local(): lax.psum_scatter(grad_gate_weight, 'dp', scatter_dimension=1, tiled=True)  301 us
    reduce_scatter x2, waiting for transfers between devices, local(): lax.psum_scatter(grad_up_weight, 'dp', scatter_dimension=1, tiled=True)  301 us
    dot_general x106, matrix products, times_transposed(): lax.dot_general(left_side, right_side, (((1,), (1,)), ((), ())), preferre...  250 us
    dot_general x106, matrix products, inner_rows(): lax.dot_general(left_side, right_side, (((0,), (0,)), ((), ())), preferre...  188 us
    dynamic_slice x96, local copies, waits for them, and re-layouts, experts_backward(): lax.scan(one_expert, empty_rows, (source, slot_gate, gate_parts, up_parts...  153 us
  transfers between devices with their start and end apart: 41, of which 35 were waited for; matrix products, arithmetic and copies ran while one was open for 5% of the time, Pallas kernels for 0%

commit v1 on v0

v1 whole, which is shorter than its diff:
```python
import jax
import jax.numpy as jnp
from jax import lax
from jax.experimental import pallas as pl
from jax.experimental.pallas import tpu as pltpu
from jax.sharding import PartitionSpec as P

HEAD_SIZE = 64
TOPK = 8
EXPERTS = 16
LAYER_COUNT = 2
SEQUENCE_LENGTH = 1024
CAP = 512

EPSILON = 1e-06
ROPE_BASE = 10000.0
MASKED = -1e30
LANES = 128
BLOCK = 256
F32 = jnp.float32
BF16 = jnp.bfloat16
MIB = 1 << 20


def dot_nn(a, b):
    return lax.dot_general(a, b, (((1,), (0,)), ((), ())), preferred_element_type=F32)


def dot_nt(a, b):
    return lax.dot_general(a, b, (((1,), (1,)), ((), ())), preferred_element_type=F32)


def dot_tn(a, b):
    return lax.dot_general(a, b, (((0,), (0,)), ((), ())), preferred_element_type=F32)


def half_mask(rows):
    return lax.broadcasted_iota(jnp.int32, (rows, LANES), 1) < HEAD_SIZE


def swap_halves(t):
    lane = lax.broadcasted_iota(jnp.int32, t.shape, 1) % HEAD_SIZE
    return jnp.where(
        lane < HEAD_SIZE // 2,
        pltpu.roll(t, LANES - HEAD_SIZE // 2, 1),
        pltpu.roll(t, HEAD_SIZE // 2, 1),
    )


def both_halves(t, low):
    turned = pltpu.roll(t, HEAD_SIZE, 1)
    return jnp.where(low, t, turned), jnp.where(low, turned, t)


def diagonal_mask(scores, row_block):
    rows = lax.broadcasted_iota(jnp.int32, scores.shape, 0) % BLOCK + row_block * BLOCK
    columns = lax.broadcasted_iota(jnp.int32, scores.shape, 1)
    return jnp.where(rows >= columns, scores, MASKED)


def attention_forward_kernel(
    x_ref, w_ref, cos_ref, sin_ref, wo_ref, q_ref, k_ref, v_ref, o_ref, lse_ref, out_ref, kd, vd
):
    rows = x_ref.shape[0]
    low = half_mask(BLOCK)
    lane = lax.broadcasted_iota(jnp.int32, (BLOCK, LANES), 1)
    for i in range(rows // BLOCK):
        here = pl.ds(i * BLOCK, BLOCK)
        qkv = dot_nn(x_ref[here, :], w_ref[...])
        cos, sin = cos_ref[here, :], sin_ref[here, :]

        def rope(t):
            return t * cos + swap_halves(t) * sin

        q = [(rope(qkv[:, j * LANES : (j + 1) * LANES]) * HEAD_SIZE ** (-0.5)).astype(BF16) for j in range(2)]
        k = rope(qkv[:, 2 * LANES : 3 * LANES])
        v = qkv[:, 3 * LANES :]
        k_ref[here, :] = k.astype(BF16)
        v_ref[here, :] = v.astype(BF16)
        for j, (kj, vj) in enumerate(zip(both_halves(k, low), both_halves(v, low))):
            kd[j, here, :] = kj.astype(BF16)
            vd[j, here, :] = vj.astype(BF16)
        context = (i + 1) * BLOCK
        lse_all = jnp.zeros((BLOCK, LANES), F32)
        for j in range(2):
            q_ref[here, j * LANES : (j + 1) * LANES] = q[j]
            zero = jnp.zeros_like(q[j])
            stacked = jnp.concatenate([jnp.where(low, q[j], zero), jnp.where(low, zero, q[j])], axis=0)
            scores = diagonal_mask(dot_nt(stacked, kd[j, :context, :]), i)
            row_max = jnp.max(scores, axis=1, keepdims=True)
            weights = jnp.exp(scores - row_max)
            total = jnp.sum(weights, axis=1, keepdims=True)
            lse = row_max + jnp.log(total)
            probs = (weights * (1.0 / total)).astype(BF16)
            mixed = dot_nn(probs, vd[j, :context, :])
            o_ref[here, j * LANES : (j + 1) * LANES] = jnp.where(low, mixed[:BLOCK], mixed[BLOCK:]).astype(BF16)
            lse_all = jnp.where(lane == 2 * j, lse[:BLOCK], lse_all)
            lse_all = jnp.where(lane == 2 * j + 1, lse[BLOCK:], lse_all)
        lse_ref[here, :] = lse_all
        out_ref[here, :] = dot_nt(o_ref[here, :], wo_ref[...]).astype(BF16)


def attention_forward(x, w, cos, sin, wo):
    rows, width = x.shape
    shapes = (
        jax.ShapeDtypeStruct((rows, 2 * LANES), BF16),
        jax.ShapeDtypeStruct((rows, LANES), BF16),
        jax.ShapeDtypeStruct((rows, LANES), BF16),
        jax.ShapeDtypeStruct((rows, 2 * LANES), BF16),
        jax.ShapeDtypeStruct((rows, LANES), F32),
        jax.ShapeDtypeStruct((rows, width), BF16),
    )
    return pl.pallas_call(
        attention_forward_kernel,
        out_shape=shapes,
        scratch_shapes=[pltpu.VMEM((2, rows, LANES), BF16)] * 2,
        compiler_params=pltpu.CompilerParams(vmem_limit_bytes=40 * MIB),
        cost_estimate=pl.CostEstimate(
            flops=2 * rows * width * 768 + 4 * rows * rows * 256, bytes_accessed=12 * MIB, transcendentals=rows * rows * 2
        ),
        name="attention_forward",
    )(x, w, cos, sin, wo)


def attention_backward_kernel(
    dy_ref, wo_ref, q_ref, k_ref, v_ref, lse_ref, w_ref, cos_ref, sin_ref, dqkv_ref, dx_ref, kd, vd, dk, dv
):
    rows = dy_ref.shape[0]
    low = half_mask(BLOCK)
    for i in range(rows // BLOCK):
        here = pl.ds(i * BLOCK, BLOCK)
        k, v = k_ref[here, :].astype(F32), v_ref[here, :].astype(F32)
        for j, (kj, vj) in enumerate(zip(both_halves(k, low), both_halves(v, low))):
            kd[j, here, :] = kj.astype(BF16)
            vd[j, here, :] = vj.astype(BF16)
    dk[...] = jnp.zeros_like(dk)
    dv[...] = jnp.zeros_like(dv)
    for i in range(rows // BLOCK):
        here = pl.ds(i * BLOCK, BLOCK)
        cos, sin = cos_ref[here, :], sin_ref[here, :]
        grad_mixed = dot_nn(dy_ref[here, :], wo_ref[...]).astype(BF16)
        lse_all = lse_ref[here, :]
        context = (i + 1) * BLOCK
        for j in range(2):
            qj = q_ref[here, j * LANES : (j + 1) * LANES]
            gj = grad_mixed[:, j * LANES : (j + 1) * LANES]
            zero = jnp.zeros_like(qj)
            q2 = jnp.concatenate([jnp.where(low, qj, zero), jnp.where(low, zero, qj)], axis=0)
            g2 = jnp.concatenate([jnp.where(low, gj, zero), jnp.where(low, zero, gj)], axis=0)
            lse = jnp.concatenate([lse_all[:, 2 * j : 2 * j + 1], lse_all[:, 2 * j + 1 : 2 * j + 2]], axis=0)
            scores = diagonal_mask(dot_nt(q2, kd[j, :context, :]), i)
            probs = jnp.exp(scores - lse)
            grad_probs = dot_nt(g2, vd[j, :context, :])
            inner = jnp.sum(probs * grad_probs, axis=1, keepdims=True)
            grad_scores = (probs * (grad_probs - inner)).astype(BF16)
            dk[j, :context, :] += dot_tn(grad_scores, q2)
            dv[j, :context, :] += dot_tn(probs.astype(BF16), g2)
            grad_q = dot_nn(grad_scores, kd[j, :context, :])
            grad_q = jnp.where(low, grad_q[:BLOCK], grad_q[BLOCK:]) * HEAD_SIZE ** (-0.5)
            dqkv_ref[here, j * LANES : (j + 1) * LANES] = (grad_q * cos - swap_halves(grad_q) * sin).astype(BF16)
    for i in range(rows // BLOCK):
        here = pl.ds(i * BLOCK, BLOCK)
        cos, sin = cos_ref[here, :], sin_ref[here, :]

        def folded(total):
            pair = [total[j, here, :] for j in range(2)]
            pair = [t + pltpu.roll(t, HEAD_SIZE, 1) for t in pair]
            return jnp.where(low, pair[0], pair[1])

        grad_k = folded(dk)
        dqkv_ref[here, 2 * LANES : 3 * LANES] = (grad_k * cos - swap_halves(grad_k) * sin).astype(BF16)
        dqkv_ref[here, 3 * LANES :] = folded(dv).astype(BF16)
        dx_ref[here, :] = dot_nt(dqkv_ref[here, :], w_ref[...]).astype(BF16)


def attention_backward(dy, wo, q, k, v, lse, w, cos, sin):
    rows, width = dy.shape
    return pl.pallas_call(
        attention_backward_kernel,
        out_shape=(jax.ShapeDtypeStruct((rows, 4 * LANES), BF16), jax.ShapeDtypeStruct((rows, width), BF16)),
        scratch_shapes=[pltpu.VMEM((2, rows, LANES), BF16)] * 2 + [pltpu.VMEM((2, rows, LANES), F32)] * 2,
        compiler_params=pltpu.CompilerParams(vmem_limit_bytes=48 * MIB),
        cost_estimate=pl.CostEstimate(
            flops=2 * rows * width * 768 + 10 * rows * rows * 256, bytes_accessed=12 * MIB, transcendentals=rows * rows * 2
        ),
        name="attention_backward",
    )(dy, wo, q, k, v, lse, w, cos, sin)


HIDDEN_STEP = 512


def spread_gates(gates, step, count):
    lane = lax.broadcasted_iota(jnp.int32, gates.shape, 1)
    return [
        jnp.sum(jnp.where(lane == step * count + n, gates, 0.0), axis=1, keepdims=True) for n in range(count)
    ]


def experts_forward_kernel(x_ref, wg_ref, wu_ref, wd_ref, gates_ref, g_ref, u_ref, out_ref, total):
    step = pl.program_id(0)
    count = g_ref.shape[1] // LANES
    columns = spread_gates(gates_ref[...], step, count)
    x = x_ref[...]
    parts = []
    for n in range(count // 2):
        at = slice(2 * n * LANES, (2 * n + 2) * LANES)
        g = dot_nn(x, wg_ref[:, at])
        u = dot_nn(x, wu_ref[:, at])
        g_ref[:, at] = g.astype(BF16)
        u_ref[:, at] = u.astype(BF16)
        shape = (x.shape[0], LANES)
        gate = jnp.concatenate(
            [jnp.broadcast_to(columns[2 * n], shape), jnp.broadcast_to(columns[2 * n + 1], shape)], axis=1
        )
        parts.append((gate * (g * jax.nn.sigmoid(g)) * u).astype(BF16))
    product = dot_nt(jnp.concatenate(parts, axis=1), wd_ref[...])

    @pl.when(step == 0)
    def _():
        total[...] = product

    @pl.when(step > 0)
    def _():
        total[...] += product

    @pl.when(step == pl.num_programs(0) - 1)
    def _():
        out_ref[...] = total[...].astype(BF16)


def experts_forward(x, wg, wu, wd, gates):
    rows, width = x.shape
    hidden = wg.shape[1]
    whole = lambda s: (0, 0)
    tile = lambda s: (0, s)
    weight = pl.BlockSpec((width, HIDDEN_STEP), tile)
    saved = pl.BlockSpec((rows, HIDDEN_STEP), tile)
    return pl.pallas_call(
        experts_forward_kernel,
        grid=(hidden // HIDDEN_STEP,),
        in_specs=[pl.BlockSpec((rows, width), whole), weight, weight, weight, pl.BlockSpec((rows, LANES), whole)],
        out_specs=[saved, saved, pl.BlockSpec((rows, width), whole)],
        out_shape=(
            jax.ShapeDtypeStruct((rows, hidden), BF16),
            jax.ShapeDtypeStruct((rows, hidden), BF16),
            jax.ShapeDtypeStruct((rows, width), BF16),
        ),
        scratch_shapes=[pltpu.VMEM((rows, width), F32)],
        compiler_params=pltpu.CompilerParams(vmem_limit_bytes=48 * MIB),
        cost_estimate=pl.CostEstimate(
            flops=6 * rows * width * hidden, bytes_accessed=26 * MIB, transcendentals=rows * hidden
        ),
        name="experts_forward",
    )(x, wg, wu, wd, gates)


def experts_backward_kernel(
    dy_ref, wg_ref, wu_ref, wd_ref, g_ref, u_ref, gates_ref, a_ref, dg_ref, du_ref, out_ref, total, slots
):
    step = pl.program_id(0)
    width = dy_ref.shape[1]
    rows = dy_ref.shape[0]
    count = g_ref.shape[1] // LANES
    columns = spread_gates(gates_ref[...], step, count)
    lane = lax.broadcasted_iota(jnp.int32, (rows, LANES), 1)
    dy = dy_ref[...]
    sums = jnp.zeros((rows, LANES), F32)
    for n in range(count // 2):
        at = slice(2 * n * LANES, (2 * n + 2) * LANES)
        shape = (rows, LANES)
        gate = jnp.concatenate(
            [jnp.broadcast_to(columns[2 * n], shape), jnp.broadcast_to(columns[2 * n + 1], shape)], axis=1
        )
        da = dot_nn(dy, wd_ref[:, at])
        g = g_ref[:, at].astype(F32)
        u = u_ref[:, at].astype(F32)
        logistic = jax.nn.sigmoid(g)
        swished = g * logistic
        product = swished * u
        a_ref[:, at] = (gate * product).astype(BF16)
        inner = da * product
        for m in range(2):
            total_slot = jnp.sum(inner[:, m * LANES : (m + 1) * LANES], axis=1, keepdims=True)
            sums = jnp.where(lane == step * count + 2 * n + m, total_slot, sums)
        scaled = gate * da
        dg_ref[:, at] = (scaled * u * logistic * (1.0 + g * (1.0 - logistic))).astype(BF16)
        du_ref[:, at] = (scaled * swished).astype(BF16)
    product = dot_nt(dg_ref[...], wg_ref[...]) + dot_nt(du_ref[...], wu_ref[...])

    @pl.when(step == 0)
    def _():
        total[...] = product
        slots[...] = sums

    @pl.when(step > 0)
    def _():
        total[...] += product
        slots[...] += sums

    @pl.when(step == pl.num_programs(0) - 1)
    def _():
        out_ref[:, :width] = total[...].astype(BF16)
        out_ref[:, width:] = slots[...].astype(BF16)


def experts_backward(dy, wg, wu, wd, g, u, gates):
    rows, width = dy.shape
    hidden = wg.shape[1]
    whole = lambda s: (0, 0)
    tile = lambda s: (0, s)
    weight = pl.BlockSpec((width, HIDDEN_STEP), tile)
    saved = pl.BlockSpec((rows, HIDDEN_STEP), tile)
    return pl.pallas_call(
        experts_backward_kernel,
        grid=(hidden // HIDDEN_STEP,),
        in_specs=[
            pl.BlockSpec((rows, width), whole),
            weight,
            weight,
            weight,
            saved,
            saved,
            pl.BlockSpec((rows, LANES), whole),
        ],
        out_specs=[saved, saved, saved, pl.BlockSpec((rows, width + LANES), whole)],
        out_shape=(
            jax.ShapeDtypeStruct((rows, hidden), BF16),
            jax.ShapeDtypeStruct((rows, hidden), BF16),
            jax.ShapeDtypeStruct((rows, hidden), BF16),
            jax.ShapeDtypeStruct((rows, width + LANES), BF16),
        ),
        scratch_shapes=[pltpu.VMEM((rows, width), F32), pltpu.VMEM((rows, LANES), F32)],
        compiler_params=pltpu.CompilerParams(vmem_limit_bytes=56 * MIB),
        cost_estimate=pl.CostEstimate(
            flops=6 * rows * width * hidden, bytes_accessed=38 * MIB, transcendentals=rows * hidden
        ),
        name="experts_backward",
    )(dy, wg, wu, wd, g, u, gates)


def normalize(residual, gain):
    scale = lax.rsqrt(jnp.mean(residual * residual, axis=-1, keepdims=True) + EPSILON)
    normed = residual * scale
    return normed, scale, (normed * gain).astype(BF16)


def normalize_back(grad_hidden, normed, scale, gain):
    grad_normed = grad_hidden * gain
    inner_mean = jnp.mean(grad_normed * normed, axis=-1, keepdims=True)
    return scale * (grad_normed - normed * inner_mean)


def rope_tables(row_count):
    positions = (jnp.arange(row_count, dtype=jnp.int32) % SEQUENCE_LENGTH).astype(F32)
    frequency = ROPE_BASE ** (-jnp.arange(0, HEAD_SIZE // 2, dtype=F32) * 2.0 / HEAD_SIZE)
    angles = positions[:, None] * frequency[None, :]
    cos, sin = jnp.cos(angles), jnp.sin(angles)
    return jnp.concatenate([cos] * 4, axis=1), jnp.concatenate([-sin, sin] * 2, axis=1)


def route_masks(routes):
    lane = lax.broadcasted_iota(jnp.int32, (routes.shape[0], LANES), 1)
    chosen = routes[:, 0:1] == lane
    for k in range(1, TOPK):
        chosen = chosen | (routes[:, k : k + 1] == lane)
    low = chosen.astype(BF16)
    rows = routes.shape[0]
    earlier = (
        lax.broadcasted_iota(jnp.int32, (rows, rows), 0) > lax.broadcasted_iota(jnp.int32, (rows, rows), 1)
    ).astype(BF16)
    before = dot_nn(earlier, low)
    kept = chosen & (before < CAP)
    return chosen.astype(F32), kept.astype(F32)


def gate_probs_of(hidden, router, chosen):
    logits = jnp.where(chosen > 0, dot_nn(hidden, router), MASKED)
    raised = jnp.exp(logits - jnp.max(logits, axis=-1, keepdims=True)) * chosen
    return raised / jnp.sum(raised, axis=-1, keepdims=True)


def swap_with(values, bit):
    size = lax.axis_size("tensor")
    return lax.ppermute(values, "tensor", [(i, i ^ bit) for i in range(size)])


def widen(values):
    rows = values.shape[0]
    size = lax.axis_size("tensor")
    me = lax.axis_index("tensor")
    pieces = [(0, values)]
    bit = size // 2
    while bit:
        pieces = pieces + [(code ^ bit, swap_with(piece, bit)) for code, piece in pieces]
        bit //= 2
    whole = jnp.zeros((rows * size, values.shape[1]), values.dtype)
    for code, piece in pieces:
        whole = lax.dynamic_update_slice(whole, piece, ((me ^ code) * rows, 0))
    return whole


def narrow(values):
    size = lax.axis_size("tensor")
    me = lax.axis_index("tensor")
    rows = values.shape[0] // size
    pieces = {
        code: lax.dynamic_slice_in_dim(values, (me ^ code) * rows, rows, 0).astype(F32) for code in range(size)
    }
    bit = 1
    while bit < size:
        kept = {}
        for code in sorted(pieces, reverse=True):
            if not code & bit:
                other = swap_with(pieces[code ^ bit].astype(BF16), bit)
                kept[code] = pieces[code] + other.astype(F32)
        pieces = kept
        bit *= 2
    return pieces[0]


def sum_over_tensor(values):
    bit = 1
    while bit < lax.axis_size("tensor"):
        values = values + swap_with(values, bit)
        bit *= 2
    return values


def local(
    tokens_in,
    cotangent,
    routes,
    attn_gain,
    w_query,
    key_projection,
    value_projection,
    w_out,
    moe_gain,
    w_router,
    w_gate,
    w_up,
    w_down,
):
    rows_own = tokens_in.shape[0]
    size = lax.axis_size("tensor")
    group_rows = rows_own * size
    own_start = lax.axis_index("tensor") * rows_own
    depth = w_query.shape[1]
    q_columns, kv_columns, o_columns = w_query.shape[2], key_projection.shape[2], w_out.shape[1]
    cos, sin = rope_tables(group_rows)
    masks = [route_masks(routes[layer]) for layer in range(LAYER_COUNT)]

    def gather(values):
        return lax.all_gather(values, "dp", axis=0, tiled=True)

    def scatter(values):
        return lax.psum_scatter(values.astype(BF16), "dp", scatter_dimension=0, tiled=True).astype(F32)

    def own_rows(values):
        return lax.dynamic_slice_in_dim(values, own_start, rows_own, 0)

    packs, shards = [], []
    for layer in range(LAYER_COUNT):
        small = jnp.concatenate(
            [
                w_router[layer],
                attn_gain[layer][:, None],
                moe_gain[layer][:, None],
                jnp.zeros((depth, LANES - EXPERTS - 2), BF16),
            ],
            axis=1,
        )
        pack = jnp.concatenate(
            [w_query[layer], key_projection[layer], value_projection[layer], w_out[layer].T, small], axis=1
        )
        gate_shard = w_gate[layer].transpose(1, 0, 2).reshape(depth, -1)
        up_shard = w_up[layer].transpose(1, 0, 2).reshape(depth, -1)
        down_shard = w_down[layer].reshape(-1, depth).T
        shards.append((pack, gate_shard, up_shard, down_shard))
    weights = []
    for layer in range(LAYER_COUNT):
        pack, gate_weight, up_weight, down_weight = (gather(shard) for shard in shards[layer])
        qkv_end = q_columns + 2 * kv_columns
        small = pack[:, qkv_end + o_columns :]
        lane = lax.broadcasted_iota(jnp.int32, (1, LANES), 1)
        weights.append(
            (
                pack[:, :qkv_end],
                pack[:, qkv_end : qkv_end + o_columns],
                jnp.where(lane < EXPERTS, small, jnp.zeros_like(small)),
                small[:, EXPERTS].astype(F32)[None, :],
                small[:, EXPERTS + 1].astype(F32)[None, :],
                gate_weight,
                up_weight,
                down_weight,
            )
        )

    residual = tokens_in.astype(F32)
    tokens_all = widen(tokens_in)
    grad_all = widen(cotangent)
    records = []
    for layer in range(LAYER_COUNT):
        qkv_weight, out_weight, router, gain_attn, gain_moe, gate_weight, up_weight, down_weight = weights[layer]
        chosen, kept = masks[layer]
        if layer == 0:
            hidden_attn = normalize(tokens_all.astype(F32), gain_attn)[2]
        else:
            hidden_attn = widen(normalize(residual, gain_attn)[2])
        before_attn = residual
        q, k, v, mixed, lse, attn_part = attention_forward(hidden_attn, qkv_weight, cos, sin, out_weight)
        residual = residual + narrow(attn_part)
        before_moe = residual
        low_moe = normalize(residual, gain_moe)[2]
        hidden_moe = widen(low_moe)
        probs = gate_probs_of(hidden_moe, router, chosen)
        gates = probs * kept
        g, u, moe_part = experts_forward(hidden_moe, gate_weight, up_weight, down_weight, gates)
        residual = residual + narrow(moe_part)
        records.append(
            (before_attn, hidden_attn, q, k, v, mixed, lse, before_moe, low_moe, hidden_moe, probs, gates, g, u)
        )
    grad = cotangent.astype(F32)
    outputs = []
    for layer in reversed(range(LAYER_COUNT)):
        qkv_weight, out_weight, router, gain_attn, gain_moe, gate_weight, up_weight, down_weight = weights[layer]
        before_attn, hidden_attn, q, k, v, mixed, lse, before_moe, low_moe, hidden_moe, probs, gates, g, u = records[
            layer
        ]
        kept = masks[layer][1]
        if layer < LAYER_COUNT - 1:
            grad_all = widen(grad.astype(BF16))
        active, grad_gate, grad_up, moe_part = experts_backward(
            grad_all, gate_weight, up_weight, down_weight, g, u, gates
        )
        grad_down_weight = scatter(dot_tn(grad_all, active))
        grad_gate_weight = scatter(dot_tn(hidden_moe, grad_gate))
        grad_up_weight = scatter(dot_tn(hidden_moe, grad_up))
        own = narrow(moe_part)
        width = residual.shape[1]
        grad_moe_own, grad_pairs = own[:, :width], own[:, width:] * own_rows(kept)
        own_probs = own_rows(probs)
        grad_chosen = own_probs * (grad_pairs - jnp.sum(own_probs * grad_pairs, axis=-1, keepdims=True))
        grad_logits = grad_chosen.astype(BF16)
        grad_router = dot_tn(low_moe, grad_logits)
        grad_moe_own = grad_moe_own + dot_nt(grad_logits, router)
        normed_moe, scale_moe, _ = normalize(before_moe, gain_moe)
        grad = grad + normalize_back(grad_moe_own, normed_moe, scale_moe, gain_moe)
        grad_all = widen(grad.astype(BF16))
        grad_qkv, attn_part = attention_backward(grad_all, out_weight, q, k, v, lse, qkv_weight, cos, sin)
        grad_pack = scatter(
            jnp.concatenate(
                [
                    dot_tn(hidden_attn, grad_qkv).astype(BF16),
                    dot_tn(grad_all, mixed).astype(BF16),
                    grad_router.astype(BF16),
                ],
                axis=1,
            )
        )
        normed_attn, scale_attn, _ = normalize(before_attn, gain_attn)
        grad = grad + normalize_back(narrow(attn_part), normed_attn, scale_attn, gain_attn)

        pack, gate_shard, up_shard, _ = shards[layer]
        pack = pack.astype(F32)
        qkv_end = q_columns + 2 * kv_columns
        attn_term = jnp.sum(pack[:, :qkv_end] * grad_pack[:, :qkv_end], axis=1, keepdims=True)
        moe_term = jnp.sum(
            gate_shard.astype(F32) * grad_gate_weight + up_shard.astype(F32) * grad_up_weight, axis=1, keepdims=True
        )
        lane = lax.broadcasted_iota(jnp.int32, (depth, LANES), 1)
        stats = grad_pack[:, qkv_end + o_columns :]
        stats = jnp.where(lane == EXPERTS, attn_term, jnp.where(lane == EXPERTS + 1, moe_term, stats))
        stats = sum_over_tensor(stats)
        router_grad = stats[:, :EXPERTS]
        router_own = pack[:, qkv_end + o_columns : qkv_end + o_columns + EXPERTS]
        attn_gain_grad = stats[:, EXPERTS] / attn_gain[layer].astype(F32)
        moe_gain_grad = (stats[:, EXPERTS + 1] + jnp.sum(router_own * router_grad, axis=1)) / moe_gain[layer].astype(
            F32
        )
        outputs.insert(
            0,
            (
                attn_gain_grad,
                grad_pack[:, :q_columns],
                grad_pack[:, q_columns : q_columns + kv_columns],
                grad_pack[:, q_columns + kv_columns : qkv_end],
                grad_pack[:, qkv_end : qkv_end + o_columns].T,
                moe_gain_grad,
                router_grad,
                grad_gate_weight.reshape(depth, EXPERTS, -1).transpose(1, 0, 2),
                grad_up_weight.reshape(depth, EXPERTS, -1).transpose(1, 0, 2),
                grad_down_weight.T.reshape(EXPERTS, -1, depth),
            ),
        )
    stacked = tuple(jnp.stack([terms[n] for terms in outputs]) for n in range(10))
    return (residual, grad) + stacked


def solution(mesh):
    placed = (
        P(("dp", "tensor"), None),
        P(("dp", "tensor"), None),
        P(None, "dp", None),
        P(None, "dp"),
        P(None, "dp", "tensor"),
        P(None, "dp", "tensor"),
        P(None, "dp", "tensor"),
        P(None, "tensor", "dp"),
        P(None, "dp"),
        P(None, "dp", None),
        P(None, None, "dp", "tensor"),
        P(None, None, "dp", "tensor"),
        P(None, None, "tensor", "dp"),
    )
    return jax.shard_map(
        local,
        mesh=mesh,
        in_specs=placed,
        out_specs=(
            P(("dp", "tensor"), None),
            P(("dp", "tensor"), None),
            P(None, "dp"),
            P(None, "dp", "tensor"),
            P(None, "dp", "tensor"),
            P(None, "dp", "tensor"),
            P(None, "tensor", "dp"),
            P(None, "dp"),
            P(None, "dp", None),
            P(None, None, "dp", "tensor"),
            P(None, None, "dp", "tensor"),
            P(None, None, "tensor", "dp"),
        ),
        check_vma=False,
    )
```

time: 4980 us -> 1390 us (0.28)
  waiting for transfers between devices: 2090 us -> 1000 us
  local copies, waits for them, and re-layouts: 845 us -> 61.4 us
  other arithmetic: 787 us -> 57.7 us
  matrix products: 764 us -> 69.4 us
  blocking collectives: 412 us -> 0 us
  Pallas kernels: 0 us -> 136 us
    reduce_scatter x26 -> x8, waiting for transfers between devices: 1710 us -> 469 us  [scatter(): lax.psum_scatter(values.astype(BF16), 'dp', scatter_dimension=0, tiled=True)]
    dot_general x348 -> x18, matrix products: 764 us -> 69.4 us  [the longest x12 55.4 us: dot_tn(): lax.dot_general(a, b, (((0,), (0,)), ((), ())), preferred_element_type=F32)]
    scatter-add x64 -> x0, other arithmetic: 659 us -> none  [the longest x32 343 us: one_expert(): return (accumulated.at[slot_source].add(grad_buffer, mode='drop'), outputs)]
    gather x102 -> x0, local copies, waits for them, and re-layouts: 381 us -> none  [the longest x32 147 us: one_expert(): grad_rows = padded_grad[slot_source]]
    all_gather x14 -> x0, blocking collectives: 377 us -> none  [the longest x2 65.8 us: local(): lax.all_gather(value_projection[layer_index], 'dp', axis=0, tiled=True)]
    ppermute x0 -> x52, waiting for transfers between devices: none -> 183 us  [swap_with(): return lax.ppermute(values, 'tensor', [(i, i ^ bit) for i in range(size)])]
    dynamic_slice x168 -> x8, local copies, waits for them, and re-layouts: 182 us -> 6.56 us  [narrow(): lax.dynamic_slice_in_dim(values, (me ^ code) * rows, rows, 0).astype(F32)]
    pallas_call x0 -> x8, Pallas kernels: none -> 136 us  [the longest x2 51.7 us: experts_backward(): pl.pallas_call(experts_backward_kernel, grid=(hidden // HIDDEN_STEP,), in...]
  transfers between devices with their start and end apart: 41 -> 68, of which waited for: 35 -> 41; matrix products, arithmetic and copies ran while one was open for 5% -> 11% of each run, Pallas kernels for 0% -> 6%
where the time goes in v1:
time: 1390 us; the launch traced here: 1380 us
  waiting for transfers between devices  1000 us (72%)
  Pallas kernels  136 us (10%)
  matrix products  69.4 us (5%)
  local copies, waits for them, and re-layouts  61.4 us (4%)
  other arithmetic  57.7 us (4%)
  starting transfers between devices  33.9 us (2%)
  between operations  16.5 us (1%)
    reduce_scatter x8, waiting for transfers between devices, scatter(): lax.psum_scatter(values.astype(BF16), 'dp', scatter_dimension=0, tiled=True)  469 us
    all_gather x8, waiting for transfers between devices, gather(): return lax.all_gather(values, 'dp', axis=0, tiled=True)  349 us
    ppermute x52, waiting for transfers between devices, swap_with(): return lax.ppermute(values, 'tensor', [(i, i ^ bit) for i in range(size)])  183 us
    dot_general x12, matrix products, dot_tn(): lax.dot_general(a, b, (((0,), (0,)), ((), ())), preferred_element_type=F32)  55.4 us
    pallas_call x2, Pallas kernels, experts_backward(): pl.pallas_call(experts_backward_kernel, grid=(hidden // HIDDEN_STEP,), in...  51.7 us
    pallas_call x2, Pallas kernels, experts_forward(): pl.pallas_call(experts_forward_kernel, grid=(hidden // HIDDEN_STEP,), in_...  37.5 us
    ppermute x52, starting transfers between devices, swap_with(): return lax.ppermute(values, 'tensor', [(i, i ^ bit) for i in range(size)])  32.7 us
    pallas_call x2, Pallas kernels, attention_backward(): pl.pallas_call(attention_backward_kernel, out_shape=(jax.ShapeDtypeStruct...  29.4 us
  transfers between devices with their start and end apart: 68, of which 41 were waited for; matrix products, arithmetic and copies ran while one was open for 11% of the time, Pallas kernels for 6%

profile of v1, /device:TPU:0, one launch (start us, length us, event | category | flops | bytes accessed | tf_op | source)
XLA Modules:
  0.0 1376.0 jit_solution(12978386330145108744)
XLA Ops:
  46.0 16.6 %all-gather.9.cloned.1.call-done = bf16[1024,896]{1,0:T(8,128)(2,1)} async-done(((bf16[128,896]{1,0:T(8,128)(2,1)}), bf16[1024,896]{1,0:T(8,128)(2,1)}) %all-gather.9.cloned.1.call-update) | async-done | bytes 1835024 | tf_op jit(solution)/shard_map/all_gather | solution.py:455
  80.2 12.5 collective-permute-done.5
  117.7 20.1 %all-gather.11.cloned.1.call-done.wg_ref = bf16[1024,2048]{1,0:T(8,128)(2,1)} async-done(((bf16[128,2048]{1,0:T(8,128)(2,1)}), bf16[1024,2048]{1,0:T(8,128)(2,1)}) %all-gather.11.cloned.1.call-update) | async-done | bytes 4194320 | tf_op jit(solution)/shard_map/all_gather | solution.py:455
  137.7 74.4 %all-gather.13.cloned.1.call-done.wu_ref = bf16[1024,2048]{1,0:T(8,128)(2,1)} async-done(((bf16[128,2048]{1,0:T(8,128)(2,1)}), bf16[1024,2048]{1,0:T(8,128)(2,1)}) %all-gather.13.cloned.1.call-update) | async-done | bytes 4194320 | tf_op jit(solution)/shard_map/all_gather | solution.py:455
  212.2 73.7 %all-gather.15.cloned.1.call-done.wd_ref = bf16[1024,2048]{1,0:T(8,128)(2,1)} async-done(((bf16[128,2048]{1,0:T(8,128)(2,1)}), bf16[1024,2048]{1,0:T(8,128)(2,1)}) %all-gather.15.cloned.1.call-update) | async-done | bytes 4194320 | tf_op jit(solution)/shard_map/all_gather | solution.py:455
  286.9 18.8 %experts_forward.2 = (bf16[1024,2048]{1,0:T(8,128)(2,1)}, bf16[1024,2048]{1,0:T(8,128)(2,1)}, bf16[1024,1024]{1,0:T(8,128)(2,1)S(1)}) custom-call(bf16[1024,1024]{1,0:T(8,128)(2,1)S(1)} %constant_dynamic-update-slice_fusion.24.x_ref, bf16[1024,2048]{1,0:T(8,128)(2,1)} %all-gather.11.cloned.1.call-done.wg_ref, ...), custom_call_target="tpu_custom_call" | custom-call | flops 12884901888 | bytes 27262976 | tf_op jit(solution)/shard_map/experts_forward/pallas_call | solution.py:239
  314.5 17.9 %all-gather.17.cloned.1.call-done = bf16[1024,896]{1,0:T(8,128)(2,1)} async-done(((bf16[128,896]{1,0:T(8,128)(2,1)}), bf16[1024,896]{1,0:T(8,128)(2,1)}) %all-gather.17.cloned.1.call-update) | async-done | bytes 1835024 | tf_op jit(solution)/shard_map/all_gather | solution.py:455
  364.1 12.7 collective-permute-done.17
  408.1 72.6 %all-gather.21.cloned.1.call-done.wu_ref = bf16[1024,2048]{1,0:T(8,128)(2,1)} async-done(((bf16[128,2048]{1,0:T(8,128)(2,1)}), bf16[1024,2048]{1,0:T(8,128)(2,1)}) %all-gather.21.cloned.1.call-update) | async-done | bytes 4194320 | tf_op jit(solution)/shard_map/all_gather | solution.py:455
  480.7 73.8 %all-gather.23.cloned.1.call-done.wd_ref = bf16[1024,2048]{1,0:T(8,128)(2,1)} async-done(((bf16[128,2048]{1,0:T(8,128)(2,1)}), bf16[1024,2048]{1,0:T(8,128)(2,1)}) %all-gather.23.cloned.1.call-update) | async-done | bytes 4194320 | tf_op jit(solution)/shard_map/all_gather | solution.py:455
  557.1 18.7 %experts_forward.3 = (bf16[1024,2048]{1,0:T(8,128)(2,1)}, bf16[1024,2048]{1,0:T(8,128)(2,1)}, bf16[1024,1024]{1,0:T(8,128)(2,1)S(1)}) custom-call(bf16[1024,1024]{1,0:T(8,128)(2,1)S(1)} %copy-done.3, bf16[1024,2048]{1,0:T(8,128)(2,1)} %all-gather.19.cloned.1.call-done.wg_ref, bf16[1024,2048]{1,0:T(8,128)(2,1)} %all-gather.21.cloned.1.call-done.wu_ref, ...), custom_call_target="tpu_custom_call" | custom-call | flops 12884901888 | bytes 27262976 | tf_op jit(solution)/shard_map/experts_forward/pallas_call | solution.py:239
  575.9 25.8 %experts_backward.2 = (bf16[1024,2048]{1,0:T(8,128)(2,1)}, bf16[1024,2048]{1,0:T(8,128)(2,1)}, bf16[1024,2048]{1,0:T(8,128)(2,1)}, bf16[1024,1152]{1,0:T(8,128)(2,1)}) custom-call(bf16[1024,1024]{1,0:T(8,128)(2,1)} %copy-done.76, bf16[1024,2048]{1,0:T(8,128)(2,1)} %all-gather.19.cloned.1.call-done.wg_ref, ...), custom_call_target="tpu_custom_call" | custom-call | flops 12884901888 | bytes 39845888 | tf_op jit(solution)/shard_map/experts_backward/pallas_call | solution.py:314
  608.7 13.0 collective-permute-done.29
  654.0 14.7 %attention_backward.2 = (bf16[1024,512]{1,0:T(8,128)(2,1)S(1)}, bf16[1024,1024]{1,0:T(8,128)(2,1)}) custom-call(bf16[1024,1024]{1,0:T(8,128)(2,1)} %copy-done.75, bf16[1024,256]{1,0:T(8,128)(2,1)S(1)} %copy-done.20, bf16[1024,256]{1,0:T(8,128)(2,1)S(1)} %copy-done.30, bf16[1024,128]{1,0:T(8,128)(2,1)S(1)} %copy-done.36, bf16[1024,128]{1,0:T(8,128)(2,1)S(1)} %copy-done.38, ...), custom_call_target="tpu_custom_call" | custom-call | flops 4294967296 | bytes 12582912 | tf_op jit(solution)/shard_map/attention_backward/pallas_call | solution.py:178
  697.3 12.5 collective-permute-done.35
  730.4 25.9 %experts_backward.3 = (bf16[1024,2048]{1,0:T(8,128)(2,1)}, bf16[1024,2048]{1,0:T(8,128)(2,1)}, bf16[1024,2048]{1,0:T(8,128)(2,1)}, bf16[1024,1152]{1,0:T(8,128)(2,1)}) custom-call(bf16[1024,1024]{1,0:T(8,128)(2,1)} %constant_dynamic-update-slice_fusion.4.dy_ref, bf16[1024,2048]{1,0:T(8,128)(2,1)} %all-gather.11.cloned.1.call-done.wg_ref, ...), custom_call_target="tpu_custom_call" | custom-call | flops 12884901888 | bytes 39845888 | tf_op jit(solution)/shard_map/experts_backward/pallas_call | solution.py:314
  761.7 14.1 %collective-permute-done.41 = bf16[256,1152]{1,0:T(8,128)(2,1)S(1)} collective-permute-done((bf16[256,1152]{1,0:T(8,128)(2,1)S(1)}, bf16[256,1152]{1,0:T(8,128)(2,1)S(1)}, u32[]{:S(2)}, u32[]{:S(2)}) %collective-permute-start.41) | collective-permute-done | bytes 589856 | tf_op jit(solution)/shard_map/ppermute | solution.py:385
  797.4 14.7 %attention_backward.3 = (bf16[1024,512]{1,0:T(8,128)(2,1)S(1)}, bf16[1024,1024]{1,0:T(8,128)(2,1)}) custom-call(bf16[1024,1024]{1,0:T(8,128)(2,1)} %copy-done.74, bf16[1024,256]{1,0:T(8,128)(2,1)S(1)} %copy-done.18, bf16[1024,256]{1,0:T(8,128)(2,1)S(1)} %copy-done.26, bf16[1024,128]{1,0:T(8,128)(2,1)S(1)} %get-tuple-element.58.k_ref, ...), custom_call_target="tpu_custom_call" | custom-call | flops 4294967296 | bytes 12582912 | tf_op jit(solution)/shard_map/attention_backward/pallas_call | solution.py:178
  866.1 52.4 %reduce-scatter.19.cloned.1.call-done = bf16[128,2048]{1,0:T(8,128)(2,1)} async-done(((bf16[1024,2048]{1,0:T(8,128)(2,1)}), bf16[128,2048]{1,0:T(8,128)(2,1)}) %reduce-scatter.19.cloned.1.call-update) | async-done | bytes 524304 | tf_op jit(solution)/shard_map/reduce_scatter | solution.py:458
  923.8 86.5 %reduce-scatter.23.cloned.1.call-done = bf16[128,2048]{1,0:T(8,128)(2,1)} async-done(((bf16[1024,2048]{1,0:T(8,128)(2,1)}), bf16[128,2048]{1,0:T(8,128)(2,1)}) %reduce-scatter.23.cloned.1.call-update) | async-done | bytes 524304 | tf_op jit(solution)/shard_map/reduce_scatter | solution.py:458
  1014.7 65.5 %reduce-scatter.9.cloned.1.call-done = bf16[128,896]{1,0:T(8,128)(2,1)} async-done(((bf16[1024,896]{1,0:T(8,128)(2,1)}), bf16[128,896]{1,0:T(8,128)(2,1)}) %reduce-scatter.9.cloned.1.call-update) | async-done | bytes 229392 | tf_op jit(solution)/shard_map/reduce_scatter | solution.py:458
  1087.2 83.9 %reduce-scatter.11.cloned.1.call-done = bf16[128,2048]{1,0:T(8,128)(2,1)} async-done(((bf16[1024,2048]{1,0:T(8,128)(2,1)}), bf16[128,2048]{1,0:T(8,128)(2,1)}) %reduce-scatter.11.cloned.1.call-update) | async-done | bytes 524304 | tf_op jit(solution)/shard_map/reduce_scatter | solution.py:458
  1171.1 91.2 %reduce-scatter.13.cloned.1.call-done = bf16[128,2048]{1,0:T(8,128)(2,1)} async-done(((bf16[1024,2048]{1,0:T(8,128)(2,1)}), bf16[128,2048]{1,0:T(8,128)(2,1)}) %reduce-scatter.13.cloned.1.call-update) | async-done | bytes 524304 | tf_op jit(solution)/shard_map/reduce_scatter | solution.py:458
  1264.9 89.0 %reduce-scatter.21.cloned.1.call-done = bf16[128,2048]{1,0:T(8,128)(2,1)} async-done(((bf16[1024,2048]{1,0:T(8,128)(2,1)}), bf16[128,2048]{1,0:T(8,128)(2,1)}) %reduce-scatter.21.cloned.1.call-update) | async-done | bytes 524304 | tf_op jit(solution)/shard_map/reduce_scatter | solution.py:458
  (566 shorter events, 358.6 us)
Async XLA Ops:
  7.2 55.4 %all-gather.9.cloned.1.call-start = ((), (), s32[]{:S(2)}) async-start(), calls=%async_computation.8 | async-start | bytes 2064384 | tf_op jit(solution)/shard_map/all_gather | solution.py:455
  13.5 124.3 %all-gather.11.cloned.1.call-start = ((), (), s32[]{:S(2)}) async-start(), calls=%async_computation.9 | async-start | bytes 4718592 | tf_op jit(solution)/shard_map/all_gather | solution.py:455
  16.7 195.5 %all-gather.13.cloned.1.call-start = ((), (), s32[]{:S(2)}) async-start(), calls=%async_computation.10 | async-start | bytes 4718592 | tf_op jit(solution)/shard_map/all_gather | solution.py:455
  17.7 268.1 %all-gather.15.cloned.1.call-start = ((), (), s32[]{:S(2)}) async-start(), calls=%async_computation.11 | async-start | bytes 4718592 | tf_op jit(solution)/shard_map/all_gather | solution.py:455
  19.7 312.7 %all-gather.17.cloned.1.call-start = ((), (), s32[]{:S(2)}) async-start(), calls=%async_computation.12 | async-start | bytes 2064384 | tf_op jit(solution)/shard_map/all_gather | solution.py:455
  21.1 387.0 %all-gather.19.cloned.1.call-start = ((), (), s32[]{:S(2)}) async-start(), calls=%async_computation.13 | async-start | bytes 4718592 | tf_op jit(solution)/shard_map/all_gather | solution.py:455
  22.1 458.6 %all-gather.21.cloned.1.call-start = ((), (), s32[]{:S(2)}) async-start(), calls=%async_computation.14 | async-start | bytes 4718592 | tf_op jit(solution)/shard_map/all_gather | solution.py:455
  26.2 528.4 %all-gather.23.cloned.1.call-start = ((), (), s32[]{:S(2)}) async-start(), calls=%async_computation.15 | async-start | bytes 4718592 | tf_op jit(solution)/shard_map/all_gather | solution.py:455
  310.1 538.7 %reduce-scatter.15.cloned.1.call-start = ((), (), s32[]{:S(2)}) async-start(), calls=%async_computation.19 | async-start | bytes 2064384 | tf_op jit(solution)/shard_map/reduce_scatter | solution.py:458
  310.3 23.5 %collective-permute-start.9 = (bf16[256,1024]{1,0:T(8,128)(2,1)}, bf16[256,1024]{1,0:T(8,128)(2,1)}, u32[]{:S(2)}, u32[]{:S(2)}) collective-permute-start(bf16[256,1024]{1,0:T(8,128)(2,1)} %get-tuple-element.165), channel_id=1, source_target_pairs={{0,1},{1,0},{2,3},{3,2},{4,5},{5,4},{6,7},{7,6},{8,9},{9,8},{10,11... | collective-permute-start | bytes 1572872 | tf_op jit(solution)/shard_map/ppermute | solution.py:385
  313.1 20.8 %collective-permute-start.11 = (bf16[256,1024]{1,0:T(8,128)(2,1)}, bf16[256,1024]{1,0:T(8,128)(2,1)}, u32[]{:S(2)}, u32[]{:S(2)}) collective-permute-start(bf16[256,1024]{1,0:T(8,128)(2,1)} %add_convert_fusion.6), channel_id=1, source_target_pairs={{0,2},{1,3},{2,0},{3,1},{4,6},{5,7},{6,4},{7,5},{8,10},{9,11},{10,... | collective-permute-start | bytes 1572872 | tf_op jit(solution)/shard_map/ppermute | solution.py:385
  363.6 24.5 %collective-permute-start.24 = (bf16[256,1024]{1,0:T(8,128)(2,1)S(1)}, bf16[256,1024]{1,0:T(8,128)(2,1)S(1)}, u32[]{:S(2)}, u32[]{:S(2)}) collective-permute-start(bf16[256,1024]{1,0:T(8,128)(2,1)S(1)} %copy-done.78), channel_id=1, source_target_pairs={{0,2},{1,3},{2,0},{3,1},{4,6},{5,7},{6,4},{7,5},{8,10},{9,11},{10,... | collective-permute-start | bytes 1572872 | tf_op jit(solution)/shard_map/ppermute | solution.py:385
  378.2 20.5 %collective-permute-start.18 = (bf16[256,1024]{1,0:T(8,128)(2,1)S(1)}, bf16[256,1024]{1,0:T(8,128)(2,1)S(1)}, u32[]{:S(2)}, u32[]{:S(2)}) collective-permute-start(bf16[256,1024]{1,0:T(8,128)(2,1)S(1)} %get-tuple-element.140), channel_id=1, source_target_pairs={{0,2},{1,3},{2,0},{3,1},{4,6},{5,7},{6,4},{7,5},{8,10},{9,11},{10,... | collective-permute-start | bytes 1572872 | tf_op jit(solution)/shard_map/ppermute | solution.py:385
  379.7 19.1 %collective-permute-start.25 = (bf16[256,1024]{1,0:T(8,128)(2,1)S(1)}, bf16[256,1024]{1,0:T(8,128)(2,1)S(1)}, u32[]{:S(2)}, u32[]{:S(2)}) collective-permute-start(bf16[256,1024]{1,0:T(8,128)(2,1)S(1)} %copy-done.78), channel_id=1, source_target_pairs={{0,1},{1,0},{2,3},{3,2},{4,5},{5,4},{6,7},{7,6},{8,9},{9,8},{10,11... | collective-permute-start | bytes 1572872 | tf_op jit(solution)/shard_map/ppermute | solution.py:385
  607.3 24.9 %collective-permute-start.23 = (bf16[256,1024]{1,0:T(8,128)(2,1)S(1)}, bf16[256,1024]{1,0:T(8,128)(2,1)S(1)}, u32[]{:S(2)}, u32[]{:S(2)}) collective-permute-start(bf16[256,1024]{1,0:T(8,128)(2,1)S(1)} %add_convert_fusion.4), channel_id=1, source_target_pairs={{0,2},{1,3},{2,0},{3,1},{4,6},{5,7},{6,4},{7,5},{8,10},{9,11},{10,... | collective-permute-start | bytes 1572872 | tf_op jit(solution)/shard_map/ppermute | solution.py:385
  671.4 194.7 %reduce-scatter.17.cloned.1.call-start = ((), (), s32[]{:S(2)}) async-start(), calls=%async_computation.20 | async-start | bytes 4718592 | tf_op jit(solution)/shard_map/reduce_scatter | solution.py:458
  681.0 237.6 %reduce-scatter.19.cloned.1.call-start = ((), (), s32[]{:S(2)}) async-start(), calls=%async_computation.21 | async-start | bytes 4718592 | tf_op jit(solution)/shard_map/reduce_scatter | solution.py:458
  691.0 319.3 %reduce-scatter.23.cloned.1.call-start = ((), (), s32[]{:S(2)}) async-start(), calls=%async_computation.23 | async-start | bytes 4718592 | tf_op jit(solution)/shard_map/reduce_scatter | solution.py:458
  721.1 359.1 %reduce-scatter.9.cloned.1.call-start = ((), (), s32[]{:S(2)}) async-start(), calls=%async_computation.16 | async-start | bytes 2064384 | tf_op jit(solution)/shard_map/reduce_scatter | solution.py:458
  814.8 356.3 %reduce-scatter.11.cloned.1.call-start = ((), (), s32[]{:S(2)}) async-start(), calls=%async_computation.17 | async-start | bytes 4718592 | tf_op jit(solution)/shard_map/reduce_scatter | solution.py:458
  823.2 439.0 %reduce-scatter.13.cloned.1.call-start = ((), (), s32[]{:S(2)}) async-start(), calls=%async_computation.18 | async-start | bytes 4718592 | tf_op jit(solution)/shard_map/reduce_scatter | solution.py:458
  831.7 522.1 %reduce-scatter.21.cloned.1.call-start = ((), (), s32[]{:S(2)}) async-start(), calls=%async_computation.22 | async-start | bytes 4718592 | tf_op jit(solution)/shard_map/reduce_scatter | solution.py:458
  922.1 90.3 %collective-permute-start.51 = (f32[128,128]{1,0:T(8,128)S(1)}, f32[128,128]{1,0:T(8,128)S(1)}, u32[]{:S(2)}, u32[]{:S(2)}) collective-permute-start(f32[128,128]{1,0:T(8,128)S(1)} %add.351), channel_id=1, source_target_pairs={{0,2},{1,3},{2,0},{3,1},{4,6},{5,7},{6,4},{7,5},{8,10},{9,11},{10,... | collective-permute-start | bytes 196616 | tf_op jit(solution)/shard_map/ppermute | solution.py:385
  1264.8 96.9 %collective-permute-start.48 = (f32[128,128]{1,0:T(8,128)S(1)}, f32[128,128]{1,0:T(8,128)S(1)}, u32[]{:S(2)}, u32[]{:S(2)}) collective-permute-start(f32[128,128]{1,0:T(8,128)S(1)} %get-tuple-element.184), channel_id=1, source_target_pairs={{0,1},{1,0},{2,3},{3,2},{4,5},{5,4},{6,7},{7,6},{8,9},{9,8},{10,11... | collective-permute-start | bytes 196616 | tf_op jit(solution)/shard_map/ppermute | solution.py:385
  (168 other events, 2160.6 us)
Sparse Core Ops, SparseCore 0:
  13.6 48.9 all-gather.8
  65.3 72.4 all-gather.10
  140.5 71.6 all-gather.12
  214.1 71.6 all-gather.14
  287.9 44.4 all-gather.16
  334.4 72.4 all-gather.18
  409.0 71.6 all-gather.20
  482.8 71.6 all-gather.22
  671.5 64.8 reduce-scatter.14
  740.3 86.6 reduce-scatter.16
  830.7 87.8 reduce-scatter.18
  922.5 87.7 reduce-scatter.22
  1014.3 65.8 reduce-scatter.8
  1084.2 86.8 reduce-scatter.10
  1174.5 87.6 reduce-scatter.12
  1266.2 87.6 reduce-scatter.20

commit v2 on v1

--- a/solution.py
+++ b/solution.py
@@ -197,39 +197,25 @@
     ]
 
 
-def experts_forward_kernel(x_ref, wg_ref, wu_ref, wd_ref, gates_ref, g_ref, u_ref, out_ref, total):
+def experts_up_kernel(x_ref, wg_ref, wu_ref, gates_ref, g_ref, u_ref, a_ref):
     step = pl.program_id(0)
     count = g_ref.shape[1] // LANES
     columns = spread_gates(gates_ref[...], step, count)
     x = x_ref[...]
-    parts = []
+    shape = (x.shape[0], LANES)
     for n in range(count // 2):
         at = slice(2 * n * LANES, (2 * n + 2) * LANES)
         g = dot_nn(x, wg_ref[:, at])
         u = dot_nn(x, wu_ref[:, at])
         g_ref[:, at] = g.astype(BF16)
         u_ref[:, at] = u.astype(BF16)
-        shape = (x.shape[0], LANES)
         gate = jnp.concatenate(
             [jnp.broadcast_to(columns[2 * n], shape), jnp.broadcast_to(columns[2 * n + 1], shape)], axis=1
         )
-        parts.append((gate * (g * jax.nn.sigmoid(g)) * u).astype(BF16))
-    product = dot_nt(jnp.concatenate(parts, axis=1), wd_ref[...])
-
-    @pl.when(step == 0)
-    def _():
-        total[...] = product
-
-    @pl.when(step > 0)
-    def _():
-        total[...] += product
-
-    @pl.when(step == pl.num_programs(0) - 1)
-    def _():
-        out_ref[...] = total[...].astype(BF16)
-
-
-def experts_forward(x, wg, wu, wd, gates):
+        a_ref[:, at] = (gate * (g * jax.nn.sigmoid(g)) * u).astype(BF16)
+
+
+def experts_up(x, wg, wu, gates):
     rows, width = x.shape
     hidden = wg.shape[1]
     whole = lambda s: (0, 0)
@@ -237,26 +223,21 @@
     weight = pl.BlockSpec((width, HIDDEN_STEP), tile)
     saved = pl.BlockSpec((rows, HIDDEN_STEP), tile)
     return pl.pallas_call(
-        experts_forward_kernel,
+        experts_up_kernel,
         grid=(hidden // HIDDEN_STEP,),
-        in_specs=[pl.BlockSpec((rows, width), whole), weight, weight, weight, pl.BlockSpec((rows, LANES), whole)],
-        out_specs=[saved, saved, pl.BlockSpec((rows, width), whole)],
-        out_shape=(
-            jax.ShapeDtypeStruct((rows, hidden), BF16),
-            jax.ShapeDtypeStruct((rows, hidden), BF16),
-            jax.ShapeDtypeStruct((rows, width), BF16),
-        ),
-        scratch_shapes=[pltpu.VMEM((rows, width), F32)],
+        in_specs=[pl.BlockSpec((rows, width), whole), weight, weight, pl.BlockSpec((rows, LANES), whole)],
+        out_specs=[saved] * 3,
+        out_shape=(jax.ShapeDtypeStruct((rows, hidden), BF16),) * 3,
         compiler_params=pltpu.CompilerParams(vmem_limit_bytes=48 * MIB),
         cost_estimate=pl.CostEstimate(
-            flops=6 * rows * width * hidden, bytes_accessed=26 * MIB, transcendentals=rows * hidden
+            flops=4 * rows * width * hidden, bytes_accessed=22 * MIB, transcendentals=rows * hidden
         ),
-        name="experts_forward",
-    )(x, wg, wu, wd, gates)
+        name="experts_up",
+    )(x, wg, wu, gates)
 
 
 def experts_backward_kernel(
-    dy_ref, wg_ref, wu_ref, wd_ref, g_ref, u_ref, gates_ref, a_ref, dg_ref, du_ref, out_ref, total, slots
+    dy_ref, wg_ref, wu_ref, wd_ref, g_ref, u_ref, gates_ref, dg_ref, du_ref, out_ref, total, slots
 ):
     step = pl.program_id(0)
     width = dy_ref.shape[1]
@@ -277,9 +258,7 @@
         u = u_ref[:, at].astype(F32)
         logistic = jax.nn.sigmoid(g)
         swished = g * logistic
-        product = swished * u
-        a_ref[:, at] = (gate * product).astype(BF16)
-        inner = da * product
+        inner = da * swished * u
         for m in range(2):
             total_slot = jnp.sum(inner[:, m * LANES : (m + 1) * LANES], axis=1, keepdims=True)
             sums = jnp.where(lane == step * count + 2 * n + m, total_slot, sums)
@@ -323,9 +302,8 @@
             saved,
             pl.BlockSpec((rows, LANES), whole),
         ],
-        out_specs=[saved, saved, saved, pl.BlockSpec((rows, width + LANES), whole)],
+        out_specs=[saved, saved, pl.BlockSpec((rows, width + LANES), whole)],
         out_shape=(
-            jax.ShapeDtypeStruct((rows, hidden), BF16),
             jax.ShapeDtypeStruct((rows, hidden), BF16),
             jax.ShapeDtypeStruct((rows, hidden), BF16),
             jax.ShapeDtypeStruct((rows, width + LANES), BF16),
@@ -425,6 +403,99 @@
         values = values + swap_with(values, bit)
         bit *= 2
     return values
+
+
+def after(values, *earlier):
+    return lax.optimization_barrier((values,) + earlier)[0]
+
+
+class Ring:
+    def __init__(self, depth):
+        self.size = lax.axis_size("dp")
+        self.native = self.size % 2 == 1 or depth % LANES != 0 or self.size > 8
+        self.depth = depth
+        size = self.size
+        order = list(range(0, size, 2)) + list(range(size - 1 - size % 2, 0, -2))
+        self.order = order
+        self.forward = [(order[i], order[(i + 1) % size]) for i in range(size)]
+        self.backward = [(b, a) for a, b in self.forward]
+        place = [order.index(i) for i in range(size)]
+        self.place = jnp.asarray(place, jnp.int32)[lax.axis_index("dp")]
+        self.chains = [None, None]
+        self.turn = 0
+
+    def send(self, values, way):
+        return lax.ppermute(values, "dp", self.forward if way > 0 else self.backward)
+
+    def queued(self, values):
+        token = self.chains[self.turn]
+        return values if token is None else after(values, *token)
+
+    def finished(self, *token):
+        self.chains[self.turn] = token
+        self.turn = 1 - self.turn
+
+    def gather(self, own):
+        if self.native:
+            return lax.all_gather(own, "dp", axis=0, tiled=True)
+        way = 1 if self.turn == 0 else -1
+        half = self.size // 2
+        own = self.queued(own)
+        blocks = {0: own}
+        near, far = own, own
+        for k in range(1, half + 1):
+            near = self.send(near, way)
+            blocks[(way * k) % self.size] = near
+            if k < half:
+                far = self.send(far, -way)
+                blocks[(-way * k) % self.size] = far
+        self.finished(near, far)
+        return jnp.concatenate([blocks[k] for k in range(self.size)], axis=0)
+
+    def scatter(self, values):
+        values = values.astype(BF16)
+        if self.native:
+            return lax.psum_scatter(values, "dp", scatter_dimension=0, tiled=True).astype(F32)
+        way = 1 if self.turn == 0 else -1
+        half = self.size // 2
+
+        def block(k):
+            at = (k % self.size) * self.depth
+            return values[at : at + self.depth]
+
+        near = self.send(self.queued(block(-way * half)), way)
+        far = self.send(self.queued(block(way * (half - 1))), -way)
+        for k in range(half - 1, 0, -1):
+            near = self.send((near.astype(F32) + block(-way * k).astype(F32)).astype(BF16), way)
+            if k > 1:
+                far = self.send((far.astype(F32) + block(way * (k - 1)).astype(F32)).astype(BF16), -way)
+        self.finished(near, far)
+        return block(0).astype(F32) + near.astype(F32) + far.astype(F32)
+
+    def relative(self, values):
+        if self.native:
+            return values
+        order = jnp.asarray(self.order, jnp.int32)
+        width = values.shape[1] // self.size
+        return jnp.concatenate(
+            [
+                lax.dynamic_slice_in_dim(values, order[(self.place - k) % self.size] * width, width, 1)
+                for k in range(self.size)
+            ],
+            axis=1,
+        )
+
+    def absolute(self, values):
+        if self.native:
+            return values
+        width = values.shape[1] // self.size
+        return jnp.concatenate(
+            [
+                lax.dynamic_slice_in_dim(values, ((self.place - self.order.index(i)) % self.size) * width, width, 1)
+                for i in range(self.size)
+            ],
+            axis=1,
+        )
 
 
 def local(
@@ -451,11 +522,7 @@
     cos, sin = rope_tables(group_rows)
     masks = [route_masks(routes[layer]) for layer in range(LAYER_COUNT)]
 
-    def gather(values):
-        return lax.all_gather(values, "dp", axis=0, tiled=True)
-
-    def scatter(values):
-        return lax.psum_scatter(values.astype(BF16), "dp", scatter_dimension=0, tiled=True).astype(F32)
+    ring = Ring(depth)
 
     def own_rows(values):
         return lax.dynamic_slice_in_dim(values, own_start, rows_own, 0)
@@ -480,7 +547,7 @@
         shards.append((pack, gate_shard, up_shard, down_shard))
     weights = []
     for layer in range(LAYER_COUNT):
-        pack, gate_weight, up_weight, down_weight = (gather(shard) for shard in shards[layer])
+        pack, gate_weight, up_weight, down_weight = (ring.gather(shard) for shard in shards[layer])
         qkv_end = q_columns + 2 * kv_columns
         small = pack[:, qkv_end + o_columns :]
         lane = lax.broadcasted_iota(jnp.int32, (1, LANES), 1)
@@ -497,6 +564,7 @@
             )
         )
 
+    tokens_in, cotangent = ring.relative(tokens_in), ring.relative(cotangent)
     residual = tokens_in.astype(F32)
     tokens_all = widen(tokens_in)
     grad_all = widen(cotangent)
@@ -516,27 +584,27 @@
         hidden_moe = widen(low_moe)
         probs = gate_probs_of(hidden_moe, router, chosen)
         gates = probs * kept
-        g, u, moe_part = experts_forward(hidden_moe, gate_weight, up_weight, down_weight, gates)
-        residual = residual + narrow(moe_part)
+        g, u, active = experts_up(hidden_moe, gate_weight, up_weight, gates)
+        residual = residual + narrow(dot_nt(active, down_weight).astype(BF16))
         records.append(
-            (before_attn, hidden_attn, q, k, v, mixed, lse, before_moe, low_moe, hidden_moe, probs, gates, g, u)
+            (before_attn, hidden_attn, q, k, v, mixed, lse, before_moe, low_moe, hidden_moe, probs, gates, g, u, active)
         )
     grad = cotangent.astype(F32)
     outputs = []
     for layer in reversed(range(LAYER_COUNT)):
         qkv_weight, out_weight, router, gain_attn, gain_moe, gate_weight, up_weight, down_weight = weights[layer]
-        before_attn, hidden_attn, q, k, v, mixed, lse, before_moe, low_moe, hidden_moe, probs, gates, g, u = records[
-            layer
-        ]
+        before_attn, hidden_attn, q, k, v, mixed, lse, before_moe, low_moe, hidden_moe, probs, gates, g, u, active = (
+            records[layer]
+        )
         kept = masks[layer][1]
         if layer < LAYER_COUNT - 1:
             grad_all = widen(grad.astype(BF16))
-        active, grad_gate, grad_up, moe_part = experts_backward(
+        grad_down_weight = ring.scatter(dot_tn(grad_all, active))
+        grad_gate, grad_up, moe_part = experts_backward(
             grad_all, gate_weight, up_weight, down_weight, g, u, gates
         )
-        grad_down_weight = scatter(dot_tn(grad_all, active))
-        grad_gate_weight = scatter(dot_tn(hidden_moe, grad_gate))
-        grad_up_weight = scatter(dot_tn(hidden_moe, grad_up))
+        grad_gate_weight = ring.scatter(dot_tn(hidden_moe, grad_gate))
+        grad_up_weight = ring.scatter(dot_tn(hidden_moe, grad_up))
         own = narrow(moe_part)
         width = residual.shape[1]
         grad_moe_own, grad_pairs = own[:, :width], own[:, width:] * own_rows(kept)
@@ -549,7 +617,7 @@
         grad = grad + normalize_back(grad_moe_own, normed_moe, scale_moe, gain_moe)
         grad_all = widen(grad.astype(BF16))
         grad_qkv, attn_part = attention_backward(grad_all, out_weight, q, k, v, lse, qkv_weight, cos, sin)
-        grad_pack = scatter(
+        grad_pack = ring.scatter(
             jnp.concatenate(
                 [
                     dot_tn(hidden_attn, grad_qkv).astype(BF16),
@@ -595,7 +663,7 @@
             ),
         )
     stacked = tuple(jnp.stack([terms[n] for terms in outputs]) for n in range(10))
-    return (residual, grad) + stacked
+    return (ring.absolute(residual), ring.absolute(grad)) + stacked
 
 
 def solution(mesh):

time: 1390 us -> 896 us (0.64)
  waiting for transfers between devices: 1000 us -> 343 us
  starting transfers between devices: 33.9 us -> 144 us
  local copies, waits for them, and re-layouts: 61.4 us -> 122 us
  other arithmetic: 57.7 us -> 72.2 us
    reduce_scatter x8 -> x0, waiting for transfers between devices: 469 us -> none  [scatter(): lax.psum_scatter(values.astype(BF16), 'dp', scatter_dimension=0, tiled=True)]
    all_gather x8 -> x0, waiting for transfers between devices: 349 us -> none  [gather(): return lax.all_gather(values, 'dp', axis=0, tiled=True)]
    ppermute x0 -> x112, waiting for transfers between devices: none -> 317 us  [send(): lax.ppermute(values, 'dp', self.forward if way > 0 else self.backward)]
    ppermute x52, waiting for transfers between devices: 183 us -> 26 us  [swap_with(): return lax.ppermute(values, 'tensor', [(i, i ^ bit) for i in range(size)])]
    ppermute x0 -> x112, starting transfers between devices: none -> 118 us  [send(): lax.ppermute(values, 'dp', self.forward if way > 0 else self.backward)]
    unnamed x254 -> x406, local copies, waits for them, and re-layouts: 20.9 us -> 54.9 us
    convert_element_type x2 -> x24, other arithmetic: 1.94 us -> 22.1 us  [the longest x16 13.5 us: scatter(): (near.astype(F32) + block(-way * k).astype(F32)).astype(BF16)]
  transfers between devices with their start and end apart: 68 -> 164, of which waited for: 41 -> 66; matrix products, arithmetic and copies ran while one was open for 11% -> 22% of each run, Pallas kernels for 6% -> 8%
where the time goes in v2:
time: 896 us; the launch traced here: 887 us
  waiting for transfers between devices  343 us (38%)
  starting transfers between devices  144 us (16%)
  Pallas kernels  124 us (14%)
  local copies, waits for them, and re-layouts  122 us (14%)
  other arithmetic  72.2 us (8%)
  matrix products  66.1 us (7%)
  between operations  15.9 us (2%)
    ppermute x112, waiting for transfers between devices, send(): lax.ppermute(values, 'dp', self.forward if way > 0 else self.backward)  317 us
    ppermute x112, starting transfers between devices, send(): lax.ppermute(values, 'dp', self.forward if way > 0 else self.backward)  118 us
    unnamed x406, local copies, waits for them, and re-layouts  54.9 us
    pallas_call x2, Pallas kernels, experts_backward(): pl.pallas_call(experts_backward_kernel, grid=(hidden // HIDDEN_STEP,), in...  51.2 us
    dot_general x12, matrix products, dot_tn(): lax.dot_general(a, b, (((0,), (0,)), ((), ())), preferred_element_type=F32)  42.6 us
    pallas_call x2, Pallas kernels, attention_backward(): pl.pallas_call(attention_backward_kernel, out_shape=(jax.ShapeDtypeStruct...  28.7 us
    pallas_call x2, Pallas kernels, experts_up(): pl.pallas_call(experts_up_kernel, grid=(hidden // HIDDEN_STEP,), in_specs...  26.4 us
    ppermute x52, waiting for transfers between devices, swap_with(): return lax.ppermute(values, 'tensor', [(i, i ^ bit) for i in range(size)])  26 us
  transfers between devices with their start and end apart: 164, of which 66 were waited for; matrix products, arithmetic and copies ran while one was open for 22% of the time, Pallas kernels for 8%

profile of v2, /device:TPU:0, one launch (start us, length us, event | category | flops | bytes accessed | tf_op | source)
XLA Modules:
  0.0 886.7 jit_solution(3685376889922118379)
XLA Ops:
  101.4 12.1 %collective-permute-done.6 = bf16[128,896]{1,0:T(8,128)(2,1)S(1)} collective-permute-done((bf16[128,896]{1,0:T(8,128)(2,1)S(1)}, bf16[128,896]{1,0:T(8,128)(2,1)S(1)}, u32[]{:S(2)}, u32[]{:S(2)}) %collective-permute-start.6) | collective-permute-done | bytes 229408 | tf_op jit(solution)/shard_map/ppermute | solution.py:428
  118.6 8.6 attention_forward.2
  144.4 9.2 %collective-permute-done.21 = bf16[128,2048]{1,0:T(8,128)(2,1)S(1)} collective-permute-done((bf16[128,2048]{1,0:T(8,128)(2,1)S(1)}, bf16[128,2048]{1,0:T(8,128)(2,1)S(1)}, u32[]{:S(2)}, u32[]{:S(2)}) %collective-permute-start.21) | collective-permute-done | bytes 524320 | tf_op jit(solution)/shard_map/ppermute | solution.py:428
  160.4 15.2 %collective-permute-done.22 = bf16[128,2048]{1,0:T(8,128)(2,1)S(1)} collective-permute-done((bf16[128,2048]{1,0:T(8,128)(2,1)S(1)}, bf16[128,2048]{1,0:T(8,128)(2,1)S(1)}, u32[]{:S(2)}, u32[]{:S(2)}) %collective-permute-start.22) | collective-permute-done | bytes 524320 | tf_op jit(solution)/shard_map/ppermute | solution.py:428
  196.1 10.7 %collective-permute-done.29 = bf16[128,2048]{1,0:T(8,128)(2,1)S(1)} collective-permute-done((bf16[128,2048]{1,0:T(8,128)(2,1)S(1)}, bf16[128,2048]{1,0:T(8,128)(2,1)S(1)}, u32[]{:S(2)}, u32[]{:S(2)}) %collective-permute-start.29) | collective-permute-done | bytes 524320 | tf_op jit(solution)/shard_map/ppermute | solution.py:428
  220.2 13.1 %experts_up.2 = (bf16[1024,2048]{1,0:T(8,128)(2,1)}, bf16[1024,2048]{1,0:T(8,128)(2,1)}, bf16[1024,2048]{1,0:T(8,128)(2,1)}) custom-call(bf16[1024,1024]{1,0:T(8,128)(2,1)S(1)} %constant_dynamic-update-slice_fusion.120.x_ref, bf16[1024,2048]{1,0:T(8,128)(2,1)} %constant_dynamic-update-slice_fusion.16.wg_ref, bf16[1024,2048]{1,0:T(8,128)(2,1)} %copy-done.108, ...), custom_call_target="tpu_custom_call" | custom-call | flops 8589934592 | bytes 23068672 | tf_op jit(solution)/shard_map/experts_up/pallas_call | solution.py:225
  275.7 8.8 collective-permute-done.56
  287.0 8.7 collective-permute-done.64
  309.3 8.9 collective-permute-done.65
  329.4 10.8 %collective-permute-done.66 = bf16[128,2048]{1,0:T(8,128)(2,1)S(1)} collective-permute-done((bf16[128,2048]{1,0:T(8,128)(2,1)S(1)}, bf16[128,2048]{1,0:T(8,128)(2,1)S(1)}, u32[]{:S(2)}, u32[]{:S(2)}) %collective-permute-start.66) | collective-permute-done | bytes 524320 | tf_op jit(solution)/shard_map/ppermute | solution.py:428
  342.4 8.6 attention_forward.3
  359.4 8.7 collective-permute-done.70
  374.4 9.4 %collective-permute-done.74 = bf16[128,2048]{1,0:T(8,128)(2,1)S(1)} collective-permute-done((bf16[128,2048]{1,0:T(8,128)(2,1)S(1)}, bf16[128,2048]{1,0:T(8,128)(2,1)S(1)}, u32[]{:S(2)}, u32[]{:S(2)}) %collective-permute-start.74) | collective-permute-done | bytes 524320 | tf_op jit(solution)/shard_map/ppermute | solution.py:428
  387.0 9.3 %collective-permute-done.75 = bf16[128,2048]{1,0:T(8,128)(2,1)S(1)} collective-permute-done((bf16[128,2048]{1,0:T(8,128)(2,1)S(1)}, bf16[128,2048]{1,0:T(8,128)(2,1)S(1)}, u32[]{:S(2)}, u32[]{:S(2)}) %collective-permute-start.75) | collective-permute-done | bytes 524320 | tf_op jit(solution)/shard_map/ppermute | solution.py:428
  407.2 13.3 %experts_up.3 = (bf16[1024,2048]{1,0:T(8,128)(2,1)}, bf16[1024,2048]{1,0:T(8,128)(2,1)}, bf16[1024,2048]{1,0:T(8,128)(2,1)}) custom-call(bf16[1024,1024]{1,0:T(8,128)(2,1)S(1)} %constant_dynamic-update-slice_fusion.112.x_ref, bf16[1024,2048]{1,0:T(8,128)(2,1)} %constant_dynamic-update-slice_fusion.48.wg_ref, ...), custom_call_target="tpu_custom_call" | custom-call | flops 8589934592 | bytes 23068672 | tf_op jit(solution)/shard_map/experts_up/pallas_call | solution.py:225
  437.8 24.9 %experts_backward.2 = (bf16[1024,2048]{1,0:T(8,128)(2,1)}, bf16[1024,2048]{1,0:T(8,128)(2,1)}, bf16[1024,1152]{1,0:T(8,128)(2,1)}) custom-call(bf16[1024,1024]{1,0:T(8,128)(2,1)} %constant_dynamic-update-slice_fusion.108.dy_ref, bf16[1024,2048]{1,0:T(8,128)(2,1)} %constant_dynamic-update-slice_fusion.48.wg_ref, ...), custom_call_target="tpu_custom_call" | custom-call | flops 12884901888 | bytes 39845888 | tf_op jit(solution)/shard_map/experts_backward/pallas_call | solution.py:293
  503.6 12.5 %collective-permute-done.105 = bf16[128,2048]{1,0:T(8,128)(2,1)S(1)} collective-permute-done((bf16[128,2048]{1,0:T(8,128)(2,1)S(1)}, bf16[128,2048]{1,0:T(8,128)(2,1)S(1)}, u32[]{:S(2)}, u32[]{:S(2)}) %collective-permute-start.105) | collective-permute-done | bytes 524320 | tf_op jit(solution)/shard_map/ppermute | solution.py:428
  521.2 11.3 %collective-permute-done.85 = bf16[256,1152]{1,0:T(8,128)(2,1)S(1)} collective-permute-done((bf16[256,1152]{1,0:T(8,128)(2,1)S(1)}, bf16[256,1152]{1,0:T(8,128)(2,1)S(1)}, u32[]{:S(2)}, u32[]{:S(2)}) %collective-permute-start.85) | collective-permute-done | bytes 589856 | tf_op jit(solution)/shard_map/ppermute | solution.py:363
  567.4 14.3 %attention_backward.2 = (bf16[1024,512]{1,0:T(8,128)(2,1)S(1)}, bf16[1024,1024]{1,0:T(8,128)(2,1)}) custom-call(bf16[1024,1024]{1,0:T(8,128)(2,1)} %copy-done.72, bf16[1024,256]{1,0:T(8,128)(2,1)S(1)} %copy-done.14, bf16[1024,256]{1,0:T(8,128)(2,1)S(1)} %copy-done.24, bf16[1024,128]{1,0:T(8,128)(2,1)S(1)} %copy-done.30, bf16[1024,128]{1,0:T(8,128)(2,1)S(1)} %copy-done.32, ...), custom_call_target="tpu_custom_call" | custom-call | flops 4294967296 | bytes 12582912 | tf_op jit(solution)/shard_map/attention_backward/pallas_call | solution.py:178
  659.8 26.2 %experts_backward.3 = (bf16[1024,2048]{1,0:T(8,128)(2,1)}, bf16[1024,2048]{1,0:T(8,128)(2,1)}, bf16[1024,1152]{1,0:T(8,128)(2,1)}) custom-call(bf16[1024,1024]{1,0:T(8,128)(2,1)} %copy-done.69, bf16[1024,2048]{1,0:T(8,128)(2,1)} %constant_dynamic-update-slice_fusion.16.wg_ref, bf16[1024,2048]{1,0:T(8,128)(2,1)} %copy-done.108, ...), custom_call_target="tpu_custom_call" | custom-call | flops 12884901888 | bytes 39845888 | tf_op jit(solution)/shard_map/experts_backward/pallas_call | solution.py:293
  728.1 9.2 %collective-permute-done.119 = bf16[128,2048]{1,0:T(8,128)(2,1)S(1)} collective-permute-done((bf16[128,2048]{1,0:T(8,128)(2,1)S(1)}, bf16[128,2048]{1,0:T(8,128)(2,1)S(1)}, u32[]{:S(2)}, u32[]{:S(2)}) %collective-permute-start.119) | collective-permute-done | bytes 524320 | tf_op jit(solution)/shard_map/ppermute | solution.py:428
  750.1 13.5 %collective-permute-done.151 = bf16[128,2048]{1,0:T(8,128)(2,1)S(1)} collective-permute-done((bf16[128,2048]{1,0:T(8,128)(2,1)S(1)}, bf16[128,2048]{1,0:T(8,128)(2,1)S(1)}, u32[]{:S(2)}, u32[]{:S(2)}) %collective-permute-start.151) | collective-permute-done | bytes 524320 | tf_op jit(solution)/shard_map/ppermute | solution.py:428
  791.5 14.4 %attention_backward.3 = (bf16[1024,512]{1,0:T(8,128)(2,1)S(1)}, bf16[1024,1024]{1,0:T(8,128)(2,1)}) custom-call(bf16[1024,1024]{1,0:T(8,128)(2,1)} %constant_dynamic-update-slice_fusion.96.dy_ref, bf16[1024,256]{1,0:T(8,128)(2,1)S(1)} %copy-done.12, bf16[1024,256]{1,0:T(8,128)(2,1)S(1)} %copy-done.20, bf16[1024,128]{1,0:T(8,128)(2,1)S(1)} %get-tuple-element.84.k_ref, ...), custom_call_target="tpu_custom_call" | custom-call | flops 4294967296 | bytes 12582912 | tf_op jit(solution)/shard_map/attention_backward/pallas_call | solution.py:178
  829.8 9.2 %collective-permute-done.130 = bf16[128,896]{1,0:T(8,128)(2,1)S(1)} collective-permute-done((bf16[128,896]{1,0:T(8,128)(2,1)S(1)}, bf16[128,896]{1,0:T(8,128)(2,1)S(1)}, u32[]{:S(2)}, u32[]{:S(2)}) %collective-permute-start.130) | collective-permute-done | bytes 229408 | tf_op jit(solution)/shard_map/ppermute | solution.py:428
  (944 shorter events, 579.9 us)
Async XLA Ops:
  27.6 53.9 %collective-permute-start = (bf16[256,1024]{1,0:T(8,128)(2,1)}, bf16[256,1024]{1,0:T(8,128)(2,1)}, u32[]{:S(2)}, u32[]{:S(2)}) collective-permute-start(bf16[256,1024]{1,0:T(8,128)(2,1)} %constant_dynamic-update-slice_fusion), channel_id=1, source_target_pairs={{0,2},{1,3},{2,0},{3,1},{4,6},{5,7},{6,4},{7,5},{8,10},{9,11},{10,... | collective-permute-start | bytes 1572872 | tf_op jit(solution)/shard_map/ppermute | solution.py:363
  30.5 61.2 %collective-permute-start.1 = (bf16[256,1024]{1,0:T(8,128)(2,1)}, bf16[256,1024]{1,0:T(8,128)(2,1)}, u32[]{:S(2)}, u32[]{:S(2)}) collective-permute-start(bf16[256,1024]{1,0:T(8,128)(2,1)} %constant_dynamic-update-slice_fusion), channel_id=1, source_target_pairs={{0,1},{1,0},{2,3},{3,2},{4,5},{5,4},{6,7},{7,6},{8,9},{9,8},{10,11... | collective-permute-start | bytes 1572872 | tf_op jit(solution)/shard_map/ppermute | solution.py:363
  37.5 44.0 %collective-permute-start.7 = (bf16[128,896]{1,0:T(8,128)(2,1)}, bf16[128,896]{1,0:T(8,128)(2,1)}, u32[]{:S(2)}, u32[]{:S(2)}) collective-permute-start(bf16[128,896]{1,0:T(8,128)(2,1)} %concatenate.55), channel_id=1, source_target_pairs={{8,0},{16,8},{24,16},{28,24},{20,28},{12,20},{4,12},{0,4},{9,1},{1... | collective-permute-start | bytes 688136 | tf_op jit(solution)/shard_map/ppermute | solution.py:428
  42.5 40.6 %collective-permute-start.80 = (bf16[256,1024]{1,0:T(8,128)(2,1)}, bf16[256,1024]{1,0:T(8,128)(2,1)}, u32[]{:S(2)}, u32[]{:S(2)}) collective-permute-start(bf16[256,1024]{1,0:T(8,128)(2,1)} %constant_dynamic-update-slice_fusion.80), channel_id=1, source_target_pairs={{0,2},{1,3},{2,0},{3,1},{4,6},{5,7},{6,4},{7,5},{8,10},{9,11},{10,... | collective-permute-start | bytes 1572872 | tf_op jit(solution)/shard_map/ppermute | solution.py:363
  94.2 33.3 %collective-permute-start.17 = (bf16[128,2048]{1,0:T(8,128)(2,1)S(1)}, bf16[128,2048]{1,0:T(8,128)(2,1)S(1)}, u32[]{:S(2)}, u32[]{:S(2)}) collective-permute-start(bf16[128,2048]{1,0:T(8,128)(2,1)S(1)} %collective-permute-done.16), channel_id=1, source_target_pairs={{0,8},{8,16},{16,24},{24,28},{28,20},{20,12},{12,4},{4,0},{1,9},{9... | collective-permute-start | bytes 1572872 | tf_op jit(solution)/shard_map/ppermute | solution.py:428
  143.9 36.8 %collective-permute-start.28 = (bf16[128,2048]{1,0:T(8,128)(2,1)S(1)}, bf16[128,2048]{1,0:T(8,128)(2,1)S(1)}, u32[]{:S(2)}, u32[]{:S(2)}) collective-permute-start(bf16[128,2048]{1,0:T(8,128)(2,1)S(1)} %collective-permute-done.27), channel_id=1, source_target_pairs={{8,0},{16,8},{24,16},{28,24},{20,28},{12,20},{4,12},{0,4},{9,1},{1... | collective-permute-start | bytes 1572872 | tf_op jit(solution)/shard_map/ppermute | solution.py:428
  213.0 38.0 %collective-permute-start.32 = (bf16[128,2048]{1,0:T(8,128)(2,1)S(1)}, bf16[128,2048]{1,0:T(8,128)(2,1)S(1)}, u32[]{:S(2)}, u32[]{:S(2)}) collective-permute-start(bf16[128,2048]{1,0:T(8,128)(2,1)S(1)} %collective-permute-done.31), channel_id=1, source_target_pairs={{0,8},{8,16},{16,24},{24,28},{28,20},{20,12},{12,4},{4,0},{1,9},{9... | collective-permute-start | bytes 1572872 | tf_op jit(solution)/shard_map/ppermute | solution.py:428
  319.4 31.9 %collective-permute-start.69 = (bf16[128,2048]{1,0:T(8,128)(2,1)S(1)}, bf16[128,2048]{1,0:T(8,128)(2,1)S(1)}, u32[]{:S(2)}, u32[]{:S(2)}) collective-permute-start(bf16[128,2048]{1,0:T(8,128)(2,1)S(1)} %collective-permute-done.68), channel_id=1, source_target_pairs={{8,0},{16,8},{24,16},{28,24},{20,28},{12,20},{4,12},{0,4},{9,1},{1... | collective-permute-start | bytes 1572872 | tf_op jit(solution)/shard_map/ppermute | solution.py:428
  321.7 32.1 %collective-permute-start.62 = (bf16[128,2048]{1,0:T(8,128)(2,1)S(1)}, bf16[128,2048]{1,0:T(8,128)(2,1)S(1)}, u32[]{:S(2)}, u32[]{:S(2)}) collective-permute-start(bf16[128,2048]{1,0:T(8,128)(2,1)S(1)} %collective-permute-done.61), channel_id=1, source_target_pairs={{8,0},{16,8},{24,16},{28,24},{20,28},{12,20},{4,12},{0,4},{9,1},{1... | collective-permute-start | bytes 1572872 | tf_op jit(solution)/shard_map/ppermute | solution.py:428
  464.2 31.0 %collective-permute-start.84 = (bf16[256,1152]{1,0:T(8,128)(2,1)S(1)}, bf16[256,1152]{1,0:T(8,128)(2,1)S(1)}, u32[]{:S(2)}, u32[]{:S(2)}) collective-permute-start(bf16[256,1152]{1,0:T(8,128)(2,1)S(1)} %get-tuple-element.238), channel_id=1, source_target_pairs={{0,1},{1,0},{2,3},{3,2},{4,5},{5,4},{6,7},{7,6},{8,9},{9,8},{10,11... | collective-permute-start | bytes 1769480 | tf_op jit(solution)/shard_map/ppermute | solution.py:363
  464.3 56.5 %collective-permute-start.83 = (bf16[256,1152]{1,0:T(8,128)(2,1)S(1)}, bf16[256,1152]{1,0:T(8,128)(2,1)S(1)}, u32[]{:S(2)}, u32[]{:S(2)}) collective-permute-start(bf16[256,1152]{1,0:T(8,128)(2,1)S(1)} %get-tuple-element.237), channel_id=1, source_target_pairs={{0,1},{1,0},{2,3},{3,2},{4,5},{5,4},{6,7},{7,6},{8,9},{9,8},{10,11... | collective-permute-start | bytes 1769480 | tf_op jit(solution)/shard_map/ppermute | solution.py:363
  503.6 31.2 %collective-permute-start.77 = (bf16[256,1024]{1,0:T(8,128)(2,1)S(1)}, bf16[256,1024]{1,0:T(8,128)(2,1)S(1)}, u32[]{:S(2)}, u32[]{:S(2)}) collective-permute-start(bf16[256,1024]{1,0:T(8,128)(2,1)S(1)} %get-tuple-element.243), channel_id=1, source_target_pairs={{0,1},{1,0},{2,3},{3,2},{4,5},{5,4},{6,7},{7,6},{8,9},{9,8},{10,11... | collective-permute-start | bytes 1572872 | tf_op jit(solution)/shard_map/ppermute | solution.py:363
  520.8 33.8 %collective-permute-start.106 = (bf16[128,2048]{1,0:T(8,128)(2,1)S(1)}, bf16[128,2048]{1,0:T(8,128)(2,1)S(1)}, u32[]{:S(2)}, u32[]{:S(2)}) collective-permute-start(bf16[128,2048]{1,0:T(8,128)(2,1)S(1)} %get-tuple-element.232), channel_id=1, source_target_pairs={{8,0},{16,8},{24,16},{28,24},{20,28},{12,20},{4,12},{0,4},{9,1},{1... | collective-permute-start | bytes 1572872 | tf_op jit(solution)/shard_map/ppermute | solution.py:428
  556.0 30.5 %collective-permute-start.107 = (bf16[128,2048]{1,0:T(8,128)(2,1)}, bf16[128,2048]{1,0:T(8,128)(2,1)S(1)}, u32[]{:S(2)}, u32[]{:S(2)}) collective-permute-start(bf16[128,2048]{1,0:T(8,128)(2,1)} %get-tuple-element.230), channel_id=1, source_target_pairs={{8,0},{16,8},{24,16},{28,24},{20,28},{12,20},{4,12},{0,4},{9,1},{1... | collective-permute-start | bytes 1572872 | tf_op jit(solution)/shard_map/ppermute | solution.py:428
  563.6 32.7 %collective-permute-start.139 = (bf16[128,2048]{1,0:T(8,128)(2,1)}, bf16[128,2048]{1,0:T(8,128)(2,1)}, u32[]{:S(2)}, u32[]{:S(2)}) collective-permute-start(bf16[128,2048]{1,0:T(8,128)(2,1)} %get-tuple-element.106), channel_id=1, source_target_pairs={{0,8},{8,16},{16,24},{24,28},{28,20},{20,12},{12,4},{4,0},{1,9},{9... | collective-permute-start | bytes 1572872 | tf_op jit(solution)/shard_map/ppermute | solution.py:428
  565.3 51.3 %collective-permute-start.143 = (bf16[128,2048]{1,0:T(8,128)(2,1)}, bf16[128,2048]{1,0:T(8,128)(2,1)}, u32[]{:S(2)}, u32[]{:S(2)}) collective-permute-start(bf16[128,2048]{1,0:T(8,128)(2,1)} %get-tuple-element.107), channel_id=1, source_target_pairs={{8,0},{16,8},{24,16},{28,24},{20,28},{12,20},{4,12},{0,4},{9,1},{1... | collective-permute-start | bytes 1572872 | tf_op jit(solution)/shard_map/ppermute | solution.py:428
  591.0 31.4 %collective-permute-start.89 = (bf16[256,1024]{1,0:T(8,128)(2,1)S(1)}, bf16[256,1024]{1,0:T(8,128)(2,1)S(1)}, u32[]{:S(2)}, u32[]{:S(2)}) collective-permute-start(bf16[256,1024]{1,0:T(8,128)(2,1)S(1)} %get-tuple-element.241), channel_id=1, source_target_pairs={{0,1},{1,0},{2,3},{3,2},{4,5},{5,4},{6,7},{7,6},{8,9},{9,8},{10,11... | collective-permute-start | bytes 1572872 | tf_op jit(solution)/shard_map/ppermute | solution.py:363
  688.4 35.5 %collective-permute-start.96 = (bf16[256,1152]{1,0:T(8,128)(2,1)}, bf16[256,1152]{1,0:T(8,128)(2,1)}, u32[]{:S(2)}, u32[]{:S(2)}) collective-permute-start(bf16[256,1152]{1,0:T(8,128)(2,1)} %get-tuple-element.236), channel_id=1, source_target_pairs={{0,1},{1,0},{2,3},{3,2},{4,5},{5,4},{6,7},{7,6},{8,9},{9,8},{10,11... | collective-permute-start | bytes 1769480 | tf_op jit(solution)/shard_map/ppermute | solution.py:363
  688.4 54.4 %collective-permute-start.95 = (bf16[256,1152]{1,0:T(8,128)(2,1)}, bf16[256,1152]{1,0:T(8,128)(2,1)S(1)}, u32[]{:S(2)}, u32[]{:S(2)}) collective-permute-start(bf16[256,1152]{1,0:T(8,128)(2,1)} %get-tuple-element.235), channel_id=1, source_target_pairs={{0,1},{1,0},{2,3},{3,2},{4,5},{5,4},{6,7},{7,6},{8,9},{9,8},{10,11... | collective-permute-start | bytes 1769480 | tf_op jit(solution)/shard_map/ppermute | solution.py:363
  768.7 40.2 %collective-permute-start.121 = (bf16[128,2048]{1,0:T(8,128)(2,1)}, bf16[128,2048]{1,0:T(8,128)(2,1)}, u32[]{:S(2)}, u32[]{:S(2)}) collective-permute-start(bf16[128,2048]{1,0:T(8,128)(2,1)} %get-tuple-element.212), channel_id=1, source_target_pairs={{8,0},{16,8},{24,16},{28,24},{20,28},{12,20},{4,12},{0,4},{9,1},{1... | collective-permute-start | bytes 1572872 | tf_op jit(solution)/shard_map/ppermute | solution.py:428
  769.1 39.7 %collective-permute-start.124 = (bf16[128,2048]{1,0:T(8,128)(2,1)}, bf16[128,2048]{1,0:T(8,128)(2,1)}, u32[]{:S(2)}, u32[]{:S(2)}) collective-permute-start(bf16[128,2048]{1,0:T(8,128)(2,1)} %get-tuple-element.211), channel_id=1, source_target_pairs={{0,8},{8,16},{16,24},{24,28},{28,20},{20,12},{12,4},{4,0},{1,9},{9... | collective-permute-start | bytes 1572872 | tf_op jit(solution)/shard_map/ppermute | solution.py:428
  780.4 36.0 %collective-permute-start.153 = (bf16[128,2048]{1,0:T(8,128)(2,1)}, bf16[128,2048]{1,0:T(8,128)(2,1)}, u32[]{:S(2)}, u32[]{:S(2)}) collective-permute-start(bf16[128,2048]{1,0:T(8,128)(2,1)} %get-tuple-element.110), channel_id=1, source_target_pairs={{0,8},{8,16},{16,24},{24,28},{28,20},{20,12},{12,4},{4,0},{1,9},{9... | collective-permute-start | bytes 1572872 | tf_op jit(solution)/shard_map/ppermute | solution.py:428
  781.7 58.0 %collective-permute-start.157 = (bf16[128,2048]{1,0:T(8,128)(2,1)}, bf16[128,2048]{1,0:T(8,128)(2,1)}, u32[]{:S(2)}, u32[]{:S(2)}) collective-permute-start(bf16[128,2048]{1,0:T(8,128)(2,1)} %get-tuple-element.111), channel_id=1, source_target_pairs={{8,0},{16,8},{24,16},{28,24},{20,28},{12,20},{4,12},{0,4},{9,1},{1... | collective-permute-start | bytes 1572872 | tf_op jit(solution)/shard_map/ppermute | solution.py:428
  813.8 38.6 %collective-permute-start.101 = (bf16[256,1024]{1,0:T(8,128)(2,1)}, bf16[256,1024]{1,0:T(8,128)(2,1)}, u32[]{:S(2)}, u32[]{:S(2)}) collective-permute-start(bf16[256,1024]{1,0:T(8,128)(2,1)} %get-tuple-element.239), channel_id=1, source_target_pairs={{0,1},{1,0},{2,3},{3,2},{4,5},{5,4},{6,7},{7,6},{8,9},{9,8},{10,11... | collective-permute-start | bytes 1572872 | tf_op jit(solution)/shard_map/ppermute | solution.py:363
  (299 other events, 4610.8 us)

commit v3 on v1

v3 whole, which is shorter than its diff:
```python
import jax
import jax.numpy as jnp
from jax import lax
from jax.experimental import pallas as pl
from jax.experimental.pallas import tpu as pltpu
from jax.sharding import PartitionSpec as P

HEAD_SIZE = 64
TOPK = 8
EXPERTS = 16
LAYER_COUNT = 2
SEQUENCE_LENGTH = 1024
CAP = 512

EPSILON = 1e-06
ROPE_BASE = 10000.0
MASKED = -1e30
LANES = 128
BLOCK = 256
F32 = jnp.float32
BF16 = jnp.bfloat16
MIB = 1 << 20
QKV = 4 * LANES
OUT_END = 6 * LANES
PACK = 8 * LANES


def dot_nn(a, b):
    return lax.dot_general(a, b, (((1,), (0,)), ((), ())), preferred_element_type=F32)


def dot_nt(a, b):
    return lax.dot_general(a, b, (((1,), (1,)), ((), ())), preferred_element_type=F32)


def dot_tn(a, b):
    return lax.dot_general(a, b, (((0,), (0,)), ((), ())), preferred_element_type=F32)


def place_of(me, block):
    code = me ^ block
    return pl.multiple_of(((code & 1) * 2 + (code >> 1)) * BLOCK, BLOCK)


def half_mask(rows):
    return lax.broadcasted_iota(jnp.int32, (rows, LANES), 1) < HEAD_SIZE


def swap_halves(t):
    lane = lax.broadcasted_iota(jnp.int32, t.shape, 1) % HEAD_SIZE
    return jnp.where(
        lane < HEAD_SIZE // 2,
        pltpu.roll(t, LANES - HEAD_SIZE // 2, 1),
        pltpu.roll(t, HEAD_SIZE // 2, 1),
    )


def both_halves(t, low):
    turned = pltpu.roll(t, HEAD_SIZE, 1)
    return jnp.where(low, t, turned), jnp.where(low, turned, t)


def diagonal_mask(scores, row_block):
    rows = lax.broadcasted_iota(jnp.int32, scores.shape, 0) % BLOCK + row_block * BLOCK
    columns = lax.broadcasted_iota(jnp.int32, scores.shape, 1)
    return jnp.where(rows >= columns, scores, MASKED)


def attention_forward_kernel(
    me_ref, x_ref, pa_ref, pb_ref, cos_ref, sin_ref, q_ref, k_ref, v_ref, o_ref, lse_ref, out_ref, kd, vd
):
    rows, width = x_ref.shape
    half = width // 2
    low = half_mask(BLOCK)
    lane = lax.broadcasted_iota(jnp.int32, (BLOCK, LANES), 1)
    for i in range(rows // BLOCK):
        here = pl.ds(i * BLOCK, BLOCK)
        there = pl.ds(place_of(me_ref[0], i), BLOCK)
        qkv = dot_nn(x_ref[there, :half], pa_ref[:, :QKV]) + dot_nn(x_ref[there, half:], pb_ref[:, :QKV])
        cos, sin = cos_ref[here, :], sin_ref[here, :]

        def rope(t):
            return t * cos + swap_halves(t) * sin

        q = [(rope(qkv[:, j * LANES : (j + 1) * LANES]) * HEAD_SIZE ** (-0.5)).astype(BF16) for j in range(2)]
        k = rope(qkv[:, 2 * LANES : 3 * LANES])
        v = qkv[:, 3 * LANES :]
        k_ref[here, :] = k.astype(BF16)
        v_ref[here, :] = v.astype(BF16)
        for j, (kj, vj) in enumerate(zip(both_halves(k, low), both_halves(v, low))):
            kd[j, here, :] = kj.astype(BF16)
            vd[j, here, :] = vj.astype(BF16)
        context = (i + 1) * BLOCK
        lse_all = jnp.zeros((BLOCK, LANES), F32)
        outs = []
        for j in range(2):
            q_ref[here, j * LANES : (j + 1) * LANES] = q[j]
            zero = jnp.zeros_like(q[j])
            stacked = jnp.concatenate([jnp.where(low, q[j], zero), jnp.where(low, zero, q[j])], axis=0)
            scores = diagonal_mask(dot_nt(stacked, kd[j, :context, :]), i)
            row_max = jnp.max(scores, axis=1, keepdims=True)
            weights = jnp.exp(scores - row_max)
            total = jnp.sum(weights, axis=1, keepdims=True)
            lse = row_max + jnp.log(total)
            probs = (weights * (1.0 / total)).astype(BF16)
            mixed = dot_nn(probs, vd[j, :context, :])
            outs.append(jnp.where(low, mixed[:BLOCK], mixed[BLOCK:]).astype(BF16))
            lse_all = jnp.where(lane == 2 * j, lse[:BLOCK], lse_all)
            lse_all = jnp.where(lane == 2 * j + 1, lse[BLOCK:], lse_all)
        lse_ref[here, :] = lse_all
        mixed = jnp.concatenate(outs, axis=1)
        o_ref[there, :] = mixed
        out_ref[there, :half] = dot_nt(mixed, pa_ref[:, QKV:OUT_END]).astype(BF16)
        out_ref[there, half:] = dot_nt(mixed, pb_ref[:, QKV:OUT_END]).astype(BF16)


VMEM_SPEC = pl.BlockSpec(memory_space=pltpu.VMEM)
SMEM_SPEC = pl.BlockSpec(memory_space=pltpu.SMEM)


def attention_forward(me, x, pack, cos, sin):
    rows, width = x.shape
    shapes = (
        jax.ShapeDtypeStruct((rows, 2 * LANES), BF16),
        jax.ShapeDtypeStruct((rows, LANES), BF16),
        jax.ShapeDtypeStruct((rows, LANES), BF16),
        jax.ShapeDtypeStruct((rows, 2 * LANES), BF16),
        jax.ShapeDtypeStruct((rows, LANES), F32),
        jax.ShapeDtypeStruct((rows, width), BF16),
    )
    return pl.pallas_call(
        attention_forward_kernel,
        out_shape=shapes,
        in_specs=[SMEM_SPEC] + [VMEM_SPEC] * 5,
        scratch_shapes=[pltpu.VMEM((2, rows, LANES), BF16)] * 2,
        compiler_params=pltpu.CompilerParams(vmem_limit_bytes=40 * MIB),
        cost_estimate=pl.CostEstimate(
            flops=2 * rows * width * 768 + 4 * rows * rows * 256, bytes_accessed=12 * MIB, transcendentals=rows * rows * 2
        ),
        name="attention_forward",
    )(me, x, *pack, cos, sin)


def attention_backward_kernel(
    me_ref, dy_ref, pa_ref, pb_ref, q_ref, k_ref, v_ref, lse_ref, cos_ref, sin_ref, dqkv_ref, dx_ref, kd, vd, dk, dv
):
    rows, width = dy_ref.shape
    half = width // 2
    low = half_mask(BLOCK)
    for i in range(rows // BLOCK):
        here = pl.ds(i * BLOCK, BLOCK)
        k, v = k_ref[here, :].astype(F32), v_ref[here, :].astype(F32)
        for j, (kj, vj) in enumerate(zip(both_halves(k, low), both_halves(v, low))):
            kd[j, here, :] = kj.astype(BF16)
            vd[j, here, :] = vj.astype(BF16)
    dk[...] = jnp.zeros_like(dk)
    dv[...] = jnp.zeros_like(dv)
    for i in range(rows // BLOCK):
        here = pl.ds(i * BLOCK, BLOCK)
        there = pl.ds(place_of(me_ref[0], i), BLOCK)
        cos, sin = cos_ref[here, :], sin_ref[here, :]
        grad_mixed = (
            dot_nn(dy_ref[there, :half], pa_ref[:, QKV:OUT_END]) + dot_nn(dy_ref[there, half:], pb_ref[:, QKV:OUT_END])
        ).astype(BF16)
        lse_all = lse_ref[here, :]
        context = (i + 1) * BLOCK
        for j in range(2):
            qj = q_ref[here, j * LANES : (j + 1) * LANES]
            gj = grad_mixed[:, j * LANES : (j + 1) * LANES]
            zero = jnp.zeros_like(qj)
            q2 = jnp.concatenate([jnp.where(low, qj, zero), jnp.where(low, zero, qj)], axis=0)
            g2 = jnp.concatenate([jnp.where(low, gj, zero), jnp.where(low, zero, gj)], axis=0)
            lse = jnp.concatenate([lse_all[:, 2 * j : 2 * j + 1], lse_all[:, 2 * j + 1 : 2 * j + 2]], axis=0)
            scores = diagonal_mask(dot_nt(q2, kd[j, :context, :]), i)
            probs = jnp.exp(scores - lse)
            grad_probs = dot_nt(g2, vd[j, :context, :])
            inner = jnp.sum(probs * grad_probs, axis=1, keepdims=True)
            grad_scores = (probs * (grad_probs - inner)).astype(BF16)
            dk[j, :context, :] += dot_tn(grad_scores, q2)
            dv[j, :context, :] += dot_tn(probs.astype(BF16), g2)
            grad_q = dot_nn(grad_scores, kd[j, :context, :])
            grad_q = jnp.where(low, grad_q[:BLOCK], grad_q[BLOCK:]) * HEAD_SIZE ** (-0.5)
            dqkv_ref[there, j * LANES : (j + 1) * LANES] = (grad_q * cos - swap_halves(grad_q) * sin).astype(BF16)
    for i in range(rows // BLOCK):
        here = pl.ds(i * BLOCK, BLOCK)
        there = pl.ds(place_of(me_ref[0], i), BLOCK)
        cos, sin = cos_ref[here, :], sin_ref[here, :]

        def folded(total):
            pair = [total[j, here, :] for j in range(2)]
            pair = [t + pltpu.roll(t, HEAD_SIZE, 1) for t in pair]
            return jnp.where(low, pair[0], pair[1])

        grad_k = folded(dk)
        dqkv_ref[there, 2 * LANES : 3 * LANES] = (grad_k * cos - swap_halves(grad_k) * sin).astype(BF16)
        dqkv_ref[there, 3 * LANES :] = folded(dv).astype(BF16)
        grad_qkv = dqkv_ref[there, :]
        dx_ref[there, :half] = dot_nt(grad_qkv, pa_ref[:, :QKV]).astype(BF16)
        dx_ref[there, half:] = dot_nt(grad_qkv, pb_ref[:, :QKV]).astype(BF16)


def attention_backward(me, dy, pack, q, k, v, lse, cos, sin):
    rows, width = dy.shape
    return pl.pallas_call(
        attention_backward_kernel,
        out_shape=(jax.ShapeDtypeStruct((rows, QKV), BF16), jax.ShapeDtypeStruct((rows, width), BF16)),
        in_specs=[SMEM_SPEC] + [VMEM_SPEC] * 9,
        scratch_shapes=[pltpu.VMEM((2, rows, LANES), BF16)] * 2 + [pltpu.VMEM((2, rows, LANES), F32)] * 2,
        compiler_params=pltpu.CompilerParams(vmem_limit_bytes=48 * MIB),
        cost_estimate=pl.CostEstimate(
            flops=2 * rows * width * 768 + 10 * rows * rows * 256, bytes_accessed=12 * MIB, transcendentals=rows * rows * 2
        ),
        name="attention_backward",
    )(me, dy, *pack, q, k, v, lse, cos, sin)


def attention_weights_kernel(x_ref, dqkv_ref, dy_ref, o_ref, low_ref, dl_ref, out_ref):
    half = x_ref.shape[1] // 2
    count = OUT_END + LANES
    for n in range(2):
        at = slice(n * half, (n + 1) * half)
        to = n * count
        out_ref[:, to : to + QKV] = dot_tn(x_ref[:, at], dqkv_ref[...]).astype(BF16)
        out_ref[:, to + QKV : to + OUT_END] = dot_tn(dy_ref[:, at], o_ref[...]).astype(BF16)
        out_ref[:, to + OUT_END : to + count] = dot_tn(low_ref[:, at], dl_ref[...]).astype(BF16)


def attention_weights(x, dqkv, dy, o, low, dl):
    rows, width = x.shape
    return pl.pallas_call(
        attention_weights_kernel,
        out_shape=jax.ShapeDtypeStruct((width // 2, 2 * (OUT_END + LANES)), BF16),
        in_specs=[VMEM_SPEC] * 6,
        compiler_params=pltpu.CompilerParams(vmem_limit_bytes=32 * MIB),
        cost_estimate=pl.CostEstimate(flops=2 * rows * width * 800, bytes_accessed=9 * MIB, transcendentals=0),
        name="attention_weights",
    )(x, dqkv, dy, o, low, dl)


UP_STEP = 256
BACK_STEP = 512


def spread_gates(gates, first, count):
    lane = lax.broadcasted_iota(jnp.int32, gates.shape, 1)
    return [jnp.sum(jnp.where(lane == first + n, gates, 0.0), axis=1, keepdims=True) for n in range(count)]


def pair_columns(columns, n):
    shape = (columns[0].shape[0], LANES)
    return jnp.concatenate(
        [jnp.broadcast_to(columns[2 * n], shape), jnp.broadcast_to(columns[2 * n + 1], shape)], axis=1
    )


def experts_up_kernel(
    base_ref, x_ref, ga_ref, gb_ref, ua_ref, ub_ref, ra_ref, rb_ref, chosen_ref, kept_ref, g_ref, u_ref, a_ref, probs_ref, gates_ref
):
    step = pl.program_id(0)
    count = g_ref.shape[1] // LANES
    half = x_ref.shape[1] // 2
    xa, xb = x_ref[:, :half], x_ref[:, half:]

    @pl.when(step == 0)
    def _():
        chosen = chosen_ref[...]
        logits = jnp.where(chosen > 0, dot_nn(xa, ra_ref[...]) + dot_nn(xb, rb_ref[...]), MASKED)
        raised = jnp.exp(logits - jnp.max(logits, axis=1, keepdims=True)) * chosen
        probs = raised / jnp.sum(raised, axis=1, keepdims=True)
        probs_ref[...] = probs
        gates_ref[...] = probs * kept_ref[...]

    columns = spread_gates(gates_ref[...], base_ref[0] + step * count, count)
    for n in range(count // 2):
        at = slice(2 * n * LANES, (2 * n + 2) * LANES)
        g = dot_nn(xa, ga_ref[:, at]) + dot_nn(xb, gb_ref[:, at])
        u = dot_nn(xa, ua_ref[:, at]) + dot_nn(xb, ub_ref[:, at])
        g_ref[:, at] = g.astype(BF16)
        u_ref[:, at] = u.astype(BF16)
        a_ref[:, at] = (pair_columns(columns, n) * (g * jax.nn.sigmoid(g)) * u).astype(BF16)


def experts_up(base, x, gate_up, pack, chosen, kept):
    rows, width = x.shape
    hidden = gate_up.shape[1] // 4
    steps = hidden // UP_STEP
    whole = lambda s: (0, 0)
    weights = [pl.BlockSpec((width // 2, UP_STEP), lambda s, n=n: (0, s + n * steps)) for n in range(4)]
    saved = pl.BlockSpec((rows, UP_STEP), lambda s: (0, s))
    router = pl.BlockSpec((width // 2, LANES), lambda s: (0, OUT_END // LANES))
    wide = pl.BlockSpec((rows, LANES), whole)
    return pl.pallas_call(
        experts_up_kernel,
        grid=(steps,),
        in_specs=[SMEM_SPEC, pl.BlockSpec((rows, width), whole)] + weights + [router] * 2 + [wide] * 2,
        out_specs=[saved] * 3 + [wide] * 2,
        out_shape=(jax.ShapeDtypeStruct((rows, hidden), BF16),) * 3 + (jax.ShapeDtypeStruct((rows, LANES), F32),) * 2,
        compiler_params=pltpu.CompilerParams(vmem_limit_bytes=52 * MIB),
        cost_estimate=pl.CostEstimate(
            flops=4 * rows * width * hidden, bytes_accessed=22 * MIB, transcendentals=rows * hidden
        ),
        name="experts_up",
    )(base, x, gate_up, gate_up, gate_up, gate_up, *pack, chosen, kept)


def experts_down_kernel(a_ref, da_ref, db_ref, out_ref):
    half = out_ref.shape[1] // 2
    out_ref[:, :half] = dot_nt(a_ref[...], da_ref[...]).astype(BF16)
    out_ref[:, half:] = dot_nt(a_ref[...], db_ref[...]).astype(BF16)


def experts_down(active, down, part):
    rows, hidden = active.shape[0] // 2, active.shape[1]
    half = down.shape[0]
    steps = rows // (2 * BLOCK)
    weights = [pl.BlockSpec((half, hidden), lambda s, n=n: (0, n)) for n in range(2)]
    return pl.pallas_call(
        experts_down_kernel,
        grid=(steps,),
        in_specs=[pl.BlockSpec((2 * BLOCK, hidden), lambda s: (s + part * steps, 0))] + weights,
        out_specs=pl.BlockSpec((2 * BLOCK, 2 * half), lambda s: (s, 0)),
        out_shape=jax.ShapeDtypeStruct((rows, 2 * half), BF16),
        compiler_params=pltpu.CompilerParams(vmem_limit_bytes=32 * MIB),
        cost_estimate=pl.CostEstimate(flops=4 * rows * half * hidden, bytes_accessed=6 * MIB, transcendentals=0),
        name="experts_down",
    )(active, down, down)


def experts_backward_kernel(
    base_ref, dy_ref, ga_ref, gb_ref, ua_ref, ub_ref, da_ref, db_ref, g_ref, u_ref, gates_ref, dg_ref, du_ref, out_ref, total, slots
):
    step = pl.program_id(0)
    rows, width = dy_ref.shape
    half = width // 2
    count = g_ref.shape[1] // LANES
    first = base_ref[0] + step * count
    columns = spread_gates(gates_ref[...], first, count)
    lane = lax.broadcasted_iota(jnp.int32, (rows, LANES), 1)
    dya, dyb = dy_ref[:, :half], dy_ref[:, half:]
    sums = jnp.zeros((rows, LANES), F32)
    for n in range(count // 2):
        at = slice(2 * n * LANES, (2 * n + 2) * LANES)
        gate = pair_columns(columns, n)
        da = dot_nn(dya, da_ref[:, at]) + dot_nn(dyb, db_ref[:, at])
        g = g_ref[:, at].astype(F32)
        u = u_ref[:, at].astype(F32)
        logistic = jax.nn.sigmoid(g)
        swished = g * logistic
        inner = da * swished * u
        for m in range(2):
            total_slot = jnp.sum(inner[:, m * LANES : (m + 1) * LANES], axis=1, keepdims=True)
            sums = jnp.where(lane == first + 2 * n + m, total_slot, sums)
        scaled = gate * da
        dg_ref[:, at] = (scaled * u * logistic * (1.0 + g * (1.0 - logistic))).astype(BF16)
        du_ref[:, at] = (scaled * swished).astype(BF16)
    even = dot_nt(dg_ref[...], ga_ref[...]) + dot_nt(du_ref[...], ua_ref[...])
    odd = dot_nt(dg_ref[...], gb_ref[...]) + dot_nt(du_ref[...], ub_ref[...])

    @pl.when(step == 0)
    def _():
        total[:, :half] = even
        total[:, half:] = odd
        slots[...] = sums

    @pl.when(step == pl.num_programs(0) - 1)
    def _():
        out_ref[:, :half] = (total[:, :half] + even).astype(BF16)
        out_ref[:, half:width] = (total[:, half:] + odd).astype(BF16)
        out_ref[:, width:] = (slots[...] + sums).astype(BF16)


def experts_backward(base, dy, gate_up, down, g, u, gates):
    rows, width = dy.shape
    hidden = gate_up.shape[1] // 4
    steps = hidden // BACK_STEP
    whole = lambda s: (0, 0)
    weights = [pl.BlockSpec((width // 2, BACK_STEP), lambda s, n=n: (0, s + n * steps)) for n in range(4)]
    saved = pl.BlockSpec((rows, BACK_STEP), lambda s: (0, s))
    once = pl.Buffered(1)
    return pl.pallas_call(
        experts_backward_kernel,
        grid=(steps,),
        in_specs=[SMEM_SPEC, pl.BlockSpec((rows, width), whole, pipeline_mode=once)]
        + weights
        + weights[:2]
        + [saved] * 2
        + [pl.BlockSpec((rows, LANES), whole, pipeline_mode=once)],
        out_specs=[saved, saved, pl.BlockSpec((rows, width + LANES), whole, pipeline_mode=once)],
        out_shape=(
            jax.ShapeDtypeStruct((rows, hidden), BF16),
            jax.ShapeDtypeStruct((rows, hidden), BF16),
            jax.ShapeDtypeStruct((rows, width + LANES), BF16),
        ),
        scratch_shapes=[pltpu.VMEM((rows, width), F32), pltpu.VMEM((rows, LANES), F32)],
        compiler_params=pltpu.CompilerParams(vmem_limit_bytes=60 * MIB),
        cost_estimate=pl.CostEstimate(
            flops=6 * rows * width * hidden, bytes_accessed=38 * MIB, transcendentals=rows * hidden
        ),
        name="experts_backward",
    )(base, dy, gate_up, gate_up, gate_up, gate_up, down, down, g, u, gates)


def expert_weights_kernel(x_ref, r_ref, out_ref):
    out_ref[...] = dot_tn(x_ref[...], r_ref[...]).astype(BF16)


def expert_weights(x, rights):
    rows, width = x.shape
    hidden = rights[0].shape[1]
    steps = hidden // BACK_STEP
    outs = []
    for right in rights:
        outs.append(
            pl.pallas_call(
                expert_weights_kernel,
                grid=(2, steps),
                in_specs=[
                    pl.BlockSpec((rows, width // 2), lambda h, s: (0, h)),
                    pl.BlockSpec((rows, BACK_STEP), lambda h, s: (0, s)),
                ],
                out_specs=pl.BlockSpec((width // 2, BACK_STEP), lambda h, s: (0, h * steps + s)),
                out_shape=jax.ShapeDtypeStruct((width // 2, 2 * hidden), BF16),
                compiler_params=pltpu.CompilerParams(vmem_limit_bytes=40 * MIB),
                cost_estimate=pl.CostEstimate(
                    flops=2 * rows * width * hidden, bytes_accessed=12 * MIB, transcendentals=0
                ),
                name="expert_weights",
            )(x, right)
        )
    return outs


def normalize(residual, gain):
    scale = lax.rsqrt(jnp.mean(residual * residual, axis=-1, keepdims=True) + EPSILON)
    normed = residual * scale
    return normed, scale, (normed * gain).astype(BF16)


def normalize_back(grad_hidden, normed, scale, gain):
    grad_normed = grad_hidden * gain
    inner_mean = jnp.mean(grad_normed * normed, axis=-1, keepdims=True)
    return scale * (grad_normed - normed * inner_mean)


def rope_tables(row_count):
    positions = (jnp.arange(row_count, dtype=jnp.int32) % SEQUENCE_LENGTH).astype(F32)
    frequency = ROPE_BASE ** (-jnp.arange(0, HEAD_SIZE // 2, dtype=F32) * 2.0 / HEAD_SIZE)
    angles = positions[:, None] * frequency[None, :]
    cos, sin = jnp.cos(angles), jnp.sin(angles)
    return jnp.concatenate([cos] * 4, axis=1), jnp.concatenate([-sin, sin] * 2, axis=1)


def place_codes(size):
    return [(p % (size // 2)) * 2 + p // (size // 2) for p in range(size)]


def route_masks(routes, me):
    rows = routes.shape[0]
    size = lax.axis_size("tensor")
    own = rows // size
    starts = [(me ^ code) * own for code in place_codes(size)]
    routes = jnp.concatenate([lax.dynamic_slice_in_dim(routes, start, own, 0) for start in starts], axis=0)
    lane = lax.broadcasted_iota(jnp.int32, (rows, LANES), 1)
    chosen = routes[:, 0:1] == lane
    for k in range(1, TOPK):
        chosen = chosen | (routes[:, k : k + 1] == lane)
    position = jnp.concatenate([start + jnp.arange(own, dtype=jnp.int32) for start in starts])
    earlier = (position[:, None] > position[None, :]).astype(BF16)
    before = dot_nn(earlier, chosen.astype(BF16))
    kept = chosen & (before < CAP)
    return chosen.astype(F32), kept.astype(F32)


def swap(values, which):
    axis, bit = {"core": ("tensor", 1), "y": ("tensor", 2), "x": ("dp", 1)}[which]
    size = lax.axis_size(axis)
    return lax.ppermute(values, axis, [(i, i ^ bit) for i in range(size)])


def widen(values):
    other = swap(values, "y")
    near = [values, other]
    return jnp.concatenate(near + [swap(piece, "core") for piece in near], axis=0)


def widen_pair(values):
    half = values.shape[0] // 2
    by_y, by_x = swap(values, "y"), swap(values, "x")
    first, second = swap(by_y[:half], "x"), swap(by_x[half:], "y")
    near = [values, by_y, by_x, first, second]
    return jnp.concatenate(near + [swap(piece, "core") for piece in near], axis=0)


def added(left, right):
    return left.astype(F32) + right.astype(F32)


def narrow(values):
    rows = values.shape[0] // 4
    far, near = values[2 * rows :], values[: 2 * rows]
    out = added(near[rows:], swap(far[rows:], "core")).astype(BF16)
    out = swap(out, "y")
    return added(near[:rows], swap(far[:rows], "core")) + out.astype(F32)


def narrow_pair(near, far):
    rows = near.shape[0] // 4
    half = rows // 2
    received = swap(far, "core")

    def piece(n, lower):
        at = slice(n * rows + lower * half, n * rows + (lower + 1) * half)
        return added(near[at], received[at])

    def sent(*pieces):
        return jnp.concatenate([p.astype(BF16) for p in pieces], axis=0)

    x_first = swap(sent(piece(2, 0), piece(3, 0)), "x")
    y_first = swap(sent(piece(1, 1), piece(3, 1)), "y")
    y_second = swap(added(piece(1, 0), x_first[half:]).astype(BF16), "y")
    x_second = swap(added(piece(2, 1), y_first[half:]).astype(BF16), "x")
    upper = added(piece(0, 0), x_first[:half]) + y_second.astype(F32)
    lower = added(piece(0, 1), y_first[:half]) + x_second.astype(F32)
    return jnp.concatenate([upper, lower], axis=0)


def sum_over_tensor(values):
    for which in ("core", "y"):
        values = values + swap(values, which)
    return values


class Data:
    def __init__(self):
        size = lax.axis_size("dp")
        self.size = size
        self.groups = [list(range(0, size, 2)), list(range(1, size, 2))]
        self.odd = lax.axis_index("dp") % 2

    def by_parity(self, mine, other):
        even = self.odd == 0
        return jnp.where(even, mine, other), jnp.where(even, other, mine)

    def gather(self, own):
        return lax.all_gather(own, "dp", axis=0, tiled=True, axis_index_groups=self.groups)

    def scatter(self, values):
        total = lax.psum_scatter(values, "dp", scatter_dimension=0, tiled=True, axis_index_groups=self.groups)
        n = total.shape[1] // 2
        even, odd = total[:, :n], total[:, n:]
        return self.by_parity(even, odd)

    def relative(self, values):
        depth = values.shape[1] // self.size
        return jnp.concatenate(
            [values[:, i * depth : (i + 1) * depth] for group in self.groups for i in group], axis=1
        )

    def absolute(self, values):
        depth = values.shape[1] // self.size
        count = self.size // 2
        starts = [(part * count + n) * depth for n in range(count) for part in range(2)]
        if depth % LANES == 0:

            def kernel(in_ref, out_ref):
                for n, start in enumerate(starts):
                    out_ref[:, n * depth : (n + 1) * depth] = in_ref[:, start : start + depth]

            return pl.pallas_call(
                kernel,
                out_shape=jax.ShapeDtypeStruct(values.shape, values.dtype),
                in_specs=[VMEM_SPEC],
                name="absolute",
            )(values)
        return jnp.concatenate([values[:, start : start + depth] for start in starts], axis=1)


def local(
    tokens_in,
    cotangent,
    routes,
    attn_gain,
    w_query,
    key_projection,
    value_projection,
    w_out,
    moe_gain,
    w_router,
    w_gate,
    w_up,
    w_down,
):
    rows_own, width = tokens_in.shape
    me = lax.axis_index("tensor")
    me_array = me.reshape(1).astype(jnp.int32)
    depth = w_query.shape[1]
    q_columns, kv_columns = w_query.shape[2], key_projection.shape[2]
    cos, sin = rope_tables(rows_own * lax.axis_size("tensor"))
    data = Data()
    share = EXPERTS // 2
    base = (data.odd * share).reshape(1).astype(jnp.int32)

    packs, mine = [], []
    for layer in range(LAYER_COUNT):
        small = jnp.concatenate(
            [
                w_router[layer],
                attn_gain[layer][:, None],
                moe_gain[layer][:, None],
                jnp.zeros((depth, PACK - OUT_END - EXPERTS - 2), BF16),
            ],
            axis=1,
        )
        packs.append(
            jnp.concatenate(
                [w_query[layer], key_projection[layer], value_projection[layer], w_out[layer].T, small], axis=1
            )
        )

    def shares(weight):
        return [lax.dynamic_slice_in_dim(weight, start * share, share, 0) for start in (data.odd, 1 - data.odd)]

    gathered = []
    for layer in range(LAYER_COUNT):
        gate, up, down = shares(w_gate[layer]), shares(w_up[layer]), shares(w_down[layer])
        other = swap(jnp.concatenate([gate[1], up[1]], axis=0), "x")
        other_down = swap(down[1], "x")
        columns = [
            part.transpose(1, 0, 2).reshape(depth, -1)
            for own, got in ((gate[0], other[:share]), (up[0], other[share:]))
            for part in data.by_parity(own, got)
        ]
        down_columns = [part.reshape(-1, depth).T for part in data.by_parity(down[0], other_down)]
        gathered.append(
            (
                data.gather(packs[layer]),
                data.gather(jnp.concatenate(columns, axis=1)),
                data.gather(jnp.concatenate(down_columns, axis=1)),
            )
        )

    partner_routes = swap(routes, "x")
    masks = []
    for layer in range(LAYER_COUNT):
        own = route_masks(routes[layer], me)
        partner = route_masks(partner_routes[layer], me)
        middle = own[0].shape[0] // 2
        masks.append(
            [jnp.concatenate([a[:middle], b[:middle], a[middle:], b[middle:]]) for a, b in zip(own, partner)]
        )

    tokens_in, cotangent = data.relative(tokens_in), data.relative(cotangent)
    residual = tokens_in.astype(F32)
    tokens_all = widen(tokens_in)
    weights, records = [], []
    for layer in range(LAYER_COUNT):
        own_pack, gate_up, down = gathered[layer]
        pack = data.by_parity(own_pack, swap(own_pack, "x"))
        gain_attn, gain_moe = (
            jnp.concatenate([part[:, OUT_END + EXPERTS + n].astype(F32) for part in pack])[None, :] for n in range(2)
        )
        weights.append((pack, gain_attn, gain_moe, gate_up, down))
        chosen, kept = masks[layer]
        if layer == 0:
            hidden_attn = normalize(tokens_all.astype(F32), gain_attn)[2]
        else:
            hidden_attn = widen(normalize(residual, gain_attn)[2])
        before_attn = residual
        q, k, v, mixed, lse, attn_part = attention_forward(me_array, hidden_attn, pack, cos, sin)
        residual = residual + narrow(attn_part)
        before_moe = residual
        low_moe = normalize(residual, gain_moe)[2]
        hidden_moe = widen_pair(low_moe)
        g, u, active, probs, gates = experts_up(base, hidden_moe, gate_up, pack, chosen, kept)
        far = experts_down(active, down, 1)
        near = experts_down(active, down, 0)
        residual = residual + narrow_pair(near, far)
        records.append(
            (before_attn, hidden_attn, q, k, v, mixed, lse, before_moe, low_moe, hidden_moe, probs, gates, g, u, active)
        )
    grad = cotangent.astype(F32)
    pieces = []
    for layer in reversed(range(LAYER_COUNT)):
        pack, gain_attn, gain_moe, gate_up, down = weights[layer]
        before_attn, hidden_attn, q, k, v, mixed, lse, before_moe, low_moe, hidden_moe, probs, gates, g, u, active = (
            records[layer]
        )
        kept = masks[layer][1]
        grad_pair = widen_pair(grad.astype(BF16))
        (grad_down,) = expert_weights(grad_pair, (active,))
        grad_down = data.scatter(grad_down)
        grad_gate, grad_up, moe_part = experts_backward(base, grad_pair, gate_up, down, g, u, gates)
        middle = moe_part.shape[0] // 2
        own = narrow_pair(moe_part[:middle], moe_part[middle:])
        grad_gate, grad_up = (data.scatter(part) for part in expert_weights(hidden_moe, (grad_gate, grad_up)))
        grad_moe_own, grad_pairs = own[:, :width], own[:, width:] * kept[:rows_own]
        own_probs = probs[:rows_own]
        grad_chosen = own_probs * (grad_pairs - jnp.sum(own_probs * grad_pairs, axis=-1, keepdims=True))
        grad_logits = grad_chosen.astype(BF16)
        grad_moe_own = grad_moe_own + jnp.concatenate(
            [dot_nt(grad_logits, part[:, OUT_END : OUT_END + LANES]) for part in pack], axis=1
        )
        normed_moe, scale_moe, _ = normalize(before_moe, gain_moe)
        grad = grad + normalize_back(grad_moe_own, normed_moe, scale_moe, gain_moe)
        grad_all = widen(grad.astype(BF16))
        grad_qkv, attn_part = attention_backward(me_array, grad_all, pack, q, k, v, lse, cos, sin)
        grad_pack = data.scatter(attention_weights(hidden_attn, grad_qkv, grad_all, mixed, low_moe, grad_logits))
        normed_attn, scale_attn, _ = normalize(before_attn, gain_attn)
        grad = grad + normalize_back(narrow(attn_part), normed_attn, scale_attn, gain_attn)
        pieces.insert(0, (grad_pack, grad_gate, grad_up, grad_down))

    outputs = []
    for layer in range(LAYER_COUNT):
        grad_pack, grad_gate, grad_up, grad_down = pieces[layer]
        grad_pack = added(grad_pack[0], swap(grad_pack[1], "x"))

        def experts_of(pair, turned):
            both = data.by_parity(pair[0], swap(pair[1], "x"))
            both = jnp.stack([part.T if turned else part for part in both]).astype(F32)
            if turned:
                return both.reshape(EXPERTS, -1, depth)
            return both.reshape(2, depth, share, -1).transpose(0, 2, 1, 3).reshape(EXPERTS, depth, -1)

        grad_gate, grad_up = experts_of(grad_gate, False), experts_of(grad_up, False)
        own_pack = packs[layer].astype(F32)
        attn_term = jnp.sum(own_pack[:, :QKV] * grad_pack[:, :QKV], axis=1)[:, None]
        moe_term = jnp.sum(
            w_gate[layer].astype(F32) * grad_gate + w_up[layer].astype(F32) * grad_up, axis=(0, 2)
        )[:, None]
        lane = lax.broadcasted_iota(jnp.int32, (depth, LANES), 1)
        stats = grad_pack[:, OUT_END:]
        stats = jnp.where(lane == EXPERTS, attn_term, jnp.where(lane == EXPERTS + 1, moe_term, stats))
        stats = sum_over_tensor(stats)
        router_grad = stats[:, :EXPERTS]
        router_own = own_pack[:, OUT_END : OUT_END + EXPERTS]
        attn_gain_grad = stats[:, EXPERTS] / attn_gain[layer].astype(F32)
        moe_gain_grad = (stats[:, EXPERTS + 1] + jnp.sum(router_own * router_grad, axis=1)) / moe_gain[layer].astype(
            F32
        )
        outputs.append(
            (
                attn_gain_grad,
                grad_pack[:, :q_columns],
                grad_pack[:, q_columns : q_columns + kv_columns],
                grad_pack[:, q_columns + kv_columns : QKV],
                grad_pack[:, QKV:OUT_END].T,
                moe_gain_grad,
                router_grad,
                grad_gate,
                grad_up,
                experts_of(grad_down, True),
            )
        )
    stacked = tuple(jnp.stack([terms[n] for terms in outputs]) for n in range(10))
    return (data.absolute(residual), data.absolute(grad)) + stacked


def solution(mesh):
    placed = (
        P(("dp", "tensor"), None),
        P(("dp", "tensor"), None),
        P(None, "dp", None),
        P(None, "dp"),
        P(None, "dp", "tensor"),
        P(None, "dp", "tensor"),
        P(None, "dp", "tensor"),
        P(None, "tensor", "dp"),
        P(None, "dp"),
        P(None, "dp", None),
        P(None, None, "dp", "tensor"),
        P(None, None, "dp", "tensor"),
        P(None, None, "tensor", "dp"),
    )
    return jax.shard_map(
        local,
        mesh=mesh,
        in_specs=placed,
        out_specs=(
            P(("dp", "tensor"), None),
            P(("dp", "tensor"), None),
            P(None, "dp"),
            P(None, "dp", "tensor"),
            P(None, "dp", "tensor"),
            P(None, "dp", "tensor"),
            P(None, "tensor", "dp"),
            P(None, "dp"),
            P(None, "dp", None),
            P(None, None, "dp", "tensor"),
            P(None, None, "dp", "tensor"),
            P(None, None, "tensor", "dp"),
        ),
        check_vma=False,
    )
```

time: 1390 us -> 842 us (0.61)
  waiting for transfers between devices: 1000 us -> 280 us
  other arithmetic: 57.7 us -> 130 us
  Pallas kernels: 136 us -> 208 us
  matrix products: 69.4 us -> 11.2 us
  local copies, waits for them, and re-layouts: 61.4 us -> 115 us
  starting transfers between devices: 33.9 us -> 74.5 us
    reduce_scatter x8, waiting for transfers between devices: 469 us -> 0.07 us  [scatter(): lax.psum_scatter(values, 'dp', scatter_dimension=0, tiled=True, axis_inde...]
    all_gather x8 -> x6, waiting for transfers between devices: 349 us -> 6.17 us  [gather(): lax.all_gather(own, 'dp', axis=0, tiled=True, axis_index_groups=self.groups)]
    ppermute x52 -> x99, waiting for transfers between devices: 183 us -> 274 us  [swap(): return lax.ppermute(values, axis, [(i, i ^ bit) for i in range(size)])]
    pallas_call x6 -> x20, Pallas kernels: 107 us -> 178 us  [the longest x2 54.7 us: experts_backward(): pl.pallas_call(experts_backward_kernel, grid=(steps,), in_specs=[SMEM_SPE...]
    dot_general x12 -> x0, matrix products: 55.4 us -> none  [dot_tn(): lax.dot_general(a, b, (((0,), (0,)), ((), ())), preferred_element_type=F32)]
    unnamed x254 -> x358, local copies, waits for them, and re-layouts: 20.9 us -> 69.7 us
    ppermute x52 -> x99, starting transfers between devices: 32.7 us -> 73.2 us  [swap(): return lax.ppermute(values, axis, [(i, i ^ bit) for i in range(size)])]
    convert_element_type x14 -> x24, other arithmetic: 11.1 us -> 31.5 us  [the longest x4 6.3 us: narrow_pair(): y_second = swap(added(piece(1, 0), x_first[half:]).astype(BF16), 'y')]
  transfers between devices with their start and end apart: 68 -> 113, of which waited for: 41 -> 43; matrix products, arithmetic and copies ran while one was open for 11% -> 26% of each run, Pallas kernels for 6% -> 21%
where the time goes in v3:
time: 842 us; the launch traced here: 836 us
  waiting for transfers between devices  280 us (33%)
  Pallas kernels  208 us (25%)
  other arithmetic  130 us (15%)
  local copies, waits for them, and re-layouts  115 us (14%)
  starting transfers between devices  74.5 us (9%)
  between operations  16.6 us (2%)
  matrix products  11.2 us (1%)
    ppermute x99, waiting for transfers between devices, swap(): return lax.ppermute(values, axis, [(i, i ^ bit) for i in range(size)])  274 us
    ppermute x99, starting transfers between devices, swap(): return lax.ppermute(values, axis, [(i, i ^ bit) for i in range(size)])  73.2 us
    unnamed x358, local copies, waits for them, and re-layouts  69.7 us
    pallas_call x2, Pallas kernels, experts_backward(): pl.pallas_call(experts_backward_kernel, grid=(steps,), in_specs=[SMEM_SPE...  54.7 us
    pallas_call x6, Pallas kernels, expert_weights(): pl.pallas_call(expert_weights_kernel, grid=(2, steps), in_specs=[pl.Block...  45.9 us
    pallas_call x2, Pallas kernels, experts_up(): pl.pallas_call(experts_up_kernel, grid=(steps,), in_specs=[SMEM_SPEC, pl....  35.3 us
    pallas_call x2, Pallas kernels, attention_backward(): pl.pallas_call(attention_backward_kernel, out_shape=(jax.ShapeDtypeStruct...  30.3 us
    pallas_call x2, Pallas kernels, attention_forward(): pl.pallas_call(attention_forward_kernel, out_shape=shapes, in_specs=[SMEM...  17.5 us
  transfers between devices with their start and end apart: 113, of which 43 were waited for; matrix products, arithmetic and copies ran while one was open for 26% of the time, Pallas kernels for 21%

profile of v3, /device:TPU:0, one launch (start us, length us, event | category | flops | bytes accessed | tf_op | source)
XLA Modules:
  0.0 836.0 jit_solution(9783674300466851233)
XLA Ops:
  20.0 12.1 %collective-permute-done.40 = bf16[16,128,128]{2,1,0:T(8,128)(2,1)S(1)} collective-permute-done((bf16[16,128,128]{2,1,0:T(8,128)(2,1)}, bf16[16,128,128]{2,1,0:T(8,128)(2,1)S(1)}, u32[]{:S(2)}, u32[]{:S(2)}) %collective-permute-start.40) | collective-permute-done | bytes 524320 | tf_op jit(solution)/shard_map/ppermute | solution.py:477
  32.1 10.4 %collective-permute-done.16 = bf16[16,128,128]{2,1,0:T(8,128)(2,1)S(1)} collective-permute-done((bf16[16,128,128]{2,1,0:T(8,128)(2,1)}, bf16[16,128,128]{2,1,0:T(8,128)(2,1)S(1)}, u32[]{:S(2)}, u32[]{:S(2)}) %collective-permute-start.16) | collective-permute-done | bytes 524320 | tf_op jit(solution)/shard_map/ppermute | solution.py:477
  78.4 20.7 %collective-permute-done.3 = bf16[512,1024]{1,0:T(8,128)(2,1)S(1)} collective-permute-done((bf16[512,1024]{1,0:T(8,128)(2,1)}, bf16[512,1024]{1,0:T(8,128)(2,1)S(1)}, u32[]{:S(2)}, u32[]{:S(2)}) %collective-permute-start.3) | collective-permute-done | bytes 1048608 | tf_op jit(solution)/shard_map/ppermute | solution.py:477
  105.1 8.6 %attention_forward.2 = (bf16[1024,256]{1,0:T(8,128)(2,1)S(1)}, bf16[1024,128]{1,0:T(8,128)(2,1)S(1)}, bf16[1024,128]{1,0:T(8,128)(2,1)S(1)}, bf16[1024,256]{1,0:...) custom-call(s32[1]{0:T(128)} %bitcast.me_ref, bf16[1024,1024]{1,0:T(8,128)(2,1)S(1)} %fusion.10.x_ref, ...), custom_call_target="tpu_custom_call" | custom-call | flops 2684354560 | bytes 12582912 | tf_op jit(solution)/shard_map/attention_forward/pallas_call | solution.py:131
  120.2 9.8 %collective-permute-done.6 = bf16[256,1024]{1,0:T(8,128)(2,1)S(1)} collective-permute-done((bf16[256,1024]{1,0:T(8,128)(2,1)S(1)}, bf16[256,1024]{1,0:T(8,128)(2,1)S(1)}, u32[]{:S(2)}, u32[]{:S(2)}) %collective-permute-start.6) | collective-permute-done | bytes 524320 | tf_op jit(solution)/shard_map/ppermute | solution.py:477
  134.1 10.9 %collective-permute-done.7 = bf16[256,1024]{1,0:T(8,128)(2,1)S(1)} collective-permute-done((bf16[256,1024]{1,0:T(8,128)(2,1)S(1)}, bf16[256,1024]{1,0:T(8,128)(2,1)S(1)}, u32[]{:S(2)}, u32[]{:S(2)}) %collective-permute-start.7) | collective-permute-done | bytes 524320 | tf_op jit(solution)/shard_map/ppermute | solution.py:477
  160.6 17.6 %experts_up.2 = (bf16[2048,1024]{1,0:T(8,128)(2,1)}, bf16[2048,1024]{1,0:T(8,128)(2,1)}, bf16[2048,1024]{1,0:T(8,128)(2,1)}, f32[2048,128]{1,0:T(8,128)S(1)}, f32[2048,128]{1,0:T(8,128)}) custom-call(s32[1]{0:T(128)} %bitcast.9.base_ref, bf16[2048,1024]{1,0:T(8,128)(2,1)} %constant_dynamic-update-slice_fusion.8.x_ref, ...), custom_call_target="tpu_custom_call" | custom-call | flops 8589934592 | bytes 23068672 | tf_op jit(solution)/shard_map/experts_up/pallas_call | solution.py:292
  211.7 26.0 %collective-permute-done.20 = bf16[256,1024]{1,0:T(8,128)(2,1)S(1)} collective-permute-done((bf16[256,1024]{1,0:T(8,128)(2,1)S(1)}, bf16[256,1024]{1,0:T(8,128)(2,1)S(1)}, u32[]{:S(2)}, u32[]{:S(2)}) %collective-permute-start.20) | collective-permute-done | bytes 524320 | tf_op jit(solution)/shard_map/ppermute | solution.py:477
  243.0 14.6 %collective-permute-done.21 = bf16[128,1024]{1,0:T(8,128)(2,1)S(1)} collective-permute-done((bf16[128,1024]{1,0:T(8,128)(2,1)S(1)}, bf16[128,1024]{1,0:T(8,128)(2,1)S(1)}, u32[]{:S(2)}, u32[]{:S(2)}) %collective-permute-start.21) | collective-permute-done | bytes 262176 | tf_op jit(solution)/shard_map/ppermute | solution.py:477
  283.4 9.0 %attention_forward.3 = (bf16[1024,256]{1,0:T(8,128)(2,1)S(1)}, bf16[1024,128]{1,0:T(8,128)(2,1)S(1)}, bf16[1024,128]{1,0:T(8,128)(2,1)S(1)}, bf16[1024,256]{1,0:...) custom-call(s32[1]{0:T(128)} %bitcast.me_ref, ...), custom_call_target="tpu_custom_call" | custom-call | flops 2684354560 | bytes 12582912 | tf_op jit(solution)/shard_map/attention_forward/pallas_call | solution.py:131
  350.7 17.7 %experts_up.3 = (bf16[2048,1024]{1,0:T(8,128)(2,1)}, bf16[2048,1024]{1,0:T(8,128)(2,1)}, bf16[2048,1024]{1,0:T(8,128)(2,1)}, f32[2048,128]{1,0:T(8,128)S(1)}, f32[2048,128]{1,0:T(8,128)}) custom-call(s32[1]{0:T(128)} %bitcast.9.base_ref, bf16[2048,1024]{1,0:T(8,128)(2,1)} %constant_dynamic-update-slice_fusion.18.x_ref, ...), custom_call_target="tpu_custom_call" | custom-call | flops 8589934592 | bytes 23068672 | tf_op jit(solution)/shard_map/experts_up/pallas_call | solution.py:292
  369.3 27.5 %experts_backward.2 = (bf16[2048,1024]{1,0:T(8,128)(2,1)}, bf16[2048,1024]{1,0:T(8,128)(2,1)}, bf16[2048,1152]{1,0:T(8,128)(2,1)}) custom-call(s32[1]{0:T(128)} %bitcast.9.base_ref, bf16[2048,1024]{1,0:T(8,128)(2,1)} %constant_dynamic-update-slice_fusion.36.dy_ref.x_ref, bf16[512,4096]{1,0:T(8,128)(2,1)} %all-gather.15.cloned.1.call-done.ga_ref.gb_ref.ua_ref.ub_ref, ...), custom_call_target="tpu_custom_call" | custom-call | flops 12884901888 | bytes 39845888 | tf_op jit(solution)/shard_map/experts_backward/pallas_call | solution.py:380
  437.0 11.2 %collective-permute-done.43 = bf16[256,1024]{1,0:T(8,128)(2,1)S(1)} collective-permute-done((bf16[256,1024]{1,0:T(8,128)(2,1)S(1)}, bf16[256,1024]{1,0:T(8,128)(2,1)S(1)}, u32[]{:S(2)}, u32[]{:S(2)}) %collective-permute-start.43) | collective-permute-done | bytes 524320 | tf_op jit(solution)/shard_map/ppermute | solution.py:477
  451.3 9.1 %collective-permute-done.57 = bf16[256,1152]{1,0:T(8,128)(2,1)S(1)} collective-permute-done((bf16[256,1152]{1,0:T(8,128)(2,1)S(1)}, bf16[256,1152]{1,0:T(8,128)(2,1)S(1)}, u32[]{:S(2)}, u32[]{:S(2)}) %collective-permute-start.57) | collective-permute-done | bytes 589856 | tf_op jit(solution)/shard_map/ppermute | solution.py:477
  465.8 18.3 %collective-permute-done.44 = bf16[128,1024]{1,0:T(8,128)(2,1)S(1)} collective-permute-done((bf16[128,1024]{1,0:T(8,128)(2,1)S(1)}, bf16[128,1024]{1,0:T(8,128)(2,1)S(1)}, u32[]{:S(2)}, u32[]{:S(2)}) %collective-permute-start.44) | collective-permute-done | bytes 262176 | tf_op jit(solution)/shard_map/ppermute | solution.py:477
  511.1 11.2 %collective-permute-done.61 = bf16[256,1024]{1,0:T(8,128)(2,1)S(1)} collective-permute-done((bf16[256,1024]{1,0:T(8,128)(2,1)S(1)}, bf16[256,1024]{1,0:T(8,128)(2,1)S(1)}, u32[]{:S(2)}, u32[]{:S(2)}) %collective-permute-start.61) | collective-permute-done | bytes 524320 | tf_op jit(solution)/shard_map/ppermute | solution.py:477
  525.8 15.1 %attention_backward.2 = (bf16[1024,512]{1,0:T(8,128)(2,1)S(1)}, bf16[1024,1024]{1,0:T(8,128)(2,1)}) custom-call(s32[1]{0:T(128)} %bitcast.me_ref, bf16[1024,1024]{1,0:T(8,128)(2,1)} %pad_maximum_fusion.2.dy_ref, bf16[512,1024]{1,0:T(8,128)(2,1)S(1)} %copy-done.25, bf16[512,1024]{1,0:T(8,128)(2,1)S(1)} %copy-done.27, bf16[1024,256]{1,0:T(8,128)(2,1)S(1)} %copy-done.47, ...), custom_call_target="tpu_custom_call" | custom-call | flops 4294967296 | bytes 12582912 | tf_op jit(solution)/shard_map/attention_backward/pallas_call | solution.py:204
  551.9 9.5 %collective-permute-done.66 = bf16[256,1024]{1,0:T(8,128)(2,1)} collective-permute-done((bf16[256,1024]{1,0:T(8,128)(2,1)}, bf16[256,1024]{1,0:T(8,128)(2,1)}, u32[]{:S(2)}, u32[]{:S(2)}) %collective-permute-start.66) | collective-permute-done | bytes 524320 | tf_op jit(solution)/shard_map/ppermute | solution.py:477
  568.5 11.2 %collective-permute-done.67 = bf16[256,1024]{1,0:T(8,128)(2,1)S(1)} collective-permute-done((bf16[256,1024]{1,0:T(8,128)(2,1)S(1)}, bf16[256,1024]{1,0:T(8,128)(2,1)S(1)}, u32[]{:S(2)}, u32[]{:S(2)}) %collective-permute-start.67) | collective-permute-done | bytes 524320 | tf_op jit(solution)/shard_map/ppermute | solution.py:477
  592.8 27.3 %experts_backward.3 = (bf16[2048,1024]{1,0:T(8,128)(2,1)}, bf16[2048,1024]{1,0:T(8,128)(2,1)}, bf16[2048,1152]{1,0:T(8,128)(2,1)}) custom-call(s32[1]{0:T(128)} %bitcast.9.base_ref, bf16[2048,1024]{1,0:T(8,128)(2,1)} %constant_dynamic-update-slice_fusion.53.dy_ref.x_ref, bf16[512,4096]{1,0:T(8,128)(2,1)} %all-gather.9.cloned.1.call-done.ga_ref.gb_ref.ua_ref.ub_ref, ...), custom_call_target="tpu_custom_call" | custom-call | flops 12884901888 | bytes 39845888 | tf_op jit(solution)/shard_map/experts_backward/pallas_call | solution.py:380
  646.7 8.5 %expert_weights.7 = bf16[512,2048]{1,0:T(8,128)(2,1)} custom-call(bf16[2048,1024]{1,0:T(8,128)(2,1)} %constant_dynamic-update-slice_fusion.8.x_ref, bf16[2048,1024]{1,0:T(8,128)(2,1)S(1)} %copy-done.38), custom_call_target="tpu_custom_call" | custom-call | flops 4294967296 | bytes 12582912 | tf_op jit(solution)/shard_map/expert_weights/pallas_call | solution.py:414
  667.7 11.5 %collective-permute-done.77 = bf16[256,1152]{1,0:T(8,128)(2,1)} collective-permute-done((bf16[256,1152]{1,0:T(8,128)(2,1)}, bf16[256,1152]{1,0:T(8,128)(2,1)}, u32[]{:S(2)}, u32[]{:S(2)}) %collective-permute-start.77) | collective-permute-done | bytes 589856 | tf_op jit(solution)/shard_map/ppermute | solution.py:477
  688.1 12.2 %collective-permute-done.78 = bf16[128,1152]{1,0:T(8,128)(2,1)S(1)} collective-permute-done((bf16[128,1152]{1,0:T(8,128)(2,1)S(1)}, bf16[128,1152]{1,0:T(8,128)(2,1)S(1)}, u32[]{:S(2)}, u32[]{:S(2)}) %collective-permute-start.78) | collective-permute-done | bytes 294944 | tf_op jit(solution)/shard_map/ppermute | solution.py:477
  750.1 15.1 %attention_backward.3 = (bf16[1024,512]{1,0:T(8,128)(2,1)S(1)}, bf16[1024,1024]{1,0:T(8,128)(2,1)}) custom-call(s32[1]{0:T(128)} %bitcast.me_ref, bf16[1024,1024]{1,0:T(8,128)(2,1)} %pad_maximum_fusion.3.dy_ref, bf16[512,1024]{1,0:T(8,128)(2,1)S(1)} %copy-done.21, bf16[512,1024]{1,0:T(8,128)(2,1)S(1)} %copy-done.23, bf16[1024,256]{1,0:T(8,128)(2,1)S(1)} %copy-done.43, ...), custom_call_target="tpu_custom_call" | custom-call | flops 4294967296 | bytes 12582912 | tf_op jit(solution)/shard_map/attention_backward/pallas_call | solution.py:204
  (837 shorter events, 474.2 us)
Async XLA Ops:
  7.2 66.4 %all-gather.7.cloned.1.call-start = ((), (), s32[]{:S(2)}) async-start(), calls=%async_computation.8 | async-start | bytes 1310720 | tf_op jit(solution)/shard_map/all_gather | solution.py:545
  13.5 147.2 %all-gather.9.cloned.1.call-start = ((), (), s32[]{:S(2)}) async-start(), calls=%async_computation.9 | async-start | bytes 5242880 | tf_op jit(solution)/shard_map/all_gather | solution.py:545
  44.9 134.3 %all-gather.11.cloned.1.call-start = ((), (), s32[]{:S(2)}) async-start(), calls=%async_computation.10 | async-start | bytes 2621440 | tf_op jit(solution)/shard_map/all_gather | solution.py:545
  56.0 145.4 %all-gather.13.cloned.1.call-start = ((), (), s32[]{:S(2)}) async-start(), calls=%async_computation.11 | async-start | bytes 1310720 | tf_op jit(solution)/shard_map/all_gather | solution.py:545
  57.9 56.0 %collective-permute-start.17 = (s32[2,1024,8]{1,2,0:T(8,128)S(1)}, s32[2,1024,8]{1,2,0:T(8,128)}, u32[]{:S(2)}, u32[]{:S(2)}) collective-permute-start(s32[2,1024,8]{1,2,0:T(8,128)S(1)} %copy-done.133), channel_id=1, source_target_pairs={{0,4},{4,0},{8,12},{12,8},{16,20},{20,16},{24,28},{28,24},{1,5},{5... | collective-permute-start | bytes 196616 | tf_op jit(solution)/shard_map/ppermute | solution.py:477
  60.8 289.9 %all-gather.15.cloned.1.call-start = ((), (), s32[]{:S(2)}) async-start(), calls=%async_computation.12 | async-start | bytes 5242880 | tf_op jit(solution)/shard_map/all_gather | solution.py:545
  73.6 25.6 %collective-permute-start.3 = (bf16[512,1024]{1,0:T(8,128)(2,1)}, bf16[512,1024]{1,0:T(8,128)(2,1)S(1)}, u32[]{:S(2)}, u32[]{:S(2)}) collective-permute-start(bf16[512,1024]{1,0:T(8,128)(2,1)} %all-gather.7.cloned.1.call-done), channel_id=1, source_target_pairs={{0,4},{4,0},{8,12},{12,8},{16,20},{20,16},{24,28},{28,24},{1,5},{5... | collective-permute-start | bytes 3145736 | tf_op jit(solution)/shard_map/ppermute | solution.py:477
  151.8 147.9 %collective-permute-start.47 = (bf16[256,1024]{1,0:T(8,128)(2,1)}, bf16[256,1024]{1,0:T(8,128)(2,1)}, u32[]{:S(2)}, u32[]{:S(2)}) collective-permute-start(bf16[256,1024]{1,0:T(8,128)(2,1)} %get-tuple-element.232), channel_id=1, source_target_pairs={{0,2},{1,3},{2,0},{3,1},{4,6},{5,7},{6,4},{7,5},{8,10},{9,11},{10,... | collective-permute-start | bytes 1572872 | tf_op jit(solution)/shard_map/ppermute | solution.py:477
  153.9 153.4 %collective-permute-start.48 = (bf16[256,1024]{1,0:T(8,128)(2,1)}, bf16[256,1024]{1,0:T(8,128)(2,1)}, u32[]{:S(2)}, u32[]{:S(2)}) collective-permute-start(bf16[256,1024]{1,0:T(8,128)(2,1)} %get-tuple-element.232), channel_id=1, source_target_pairs={{0,4},{4,0},{8,12},{12,8},{16,20},{20,16},{24,28},{28,24},{1,5},{5... | collective-permute-start | bytes 1572872 | tf_op jit(solution)/shard_map/ppermute | solution.py:477
  158.4 168.0 %collective-permute-start.51 = (bf16[256,1024]{1,0:T(8,128)(2,1)}, bf16[256,1024]{1,0:T(8,128)(2,1)}, u32[]{:S(2)}, u32[]{:S(2)}) collective-permute-start(bf16[256,1024]{1,0:T(8,128)(2,1)} %get-tuple-element.232), channel_id=1, source_target_pairs={{0,1},{1,0},{2,3},{3,2},{4,5},{5,4},{6,7},{7,6},{8,9},{9,8},{10,11... | collective-permute-start | bytes 1572872 | tf_op jit(solution)/shard_map/ppermute | solution.py:477
  195.3 174.0 %all-gather.17.cloned.1.call-start = ((), (), s32[]{:S(2)}) async-start(), calls=%async_computation.13 | async-start | bytes 2621440 | tf_op jit(solution)/shard_map/all_gather | solution.py:545
  201.5 40.8 %collective-permute-start.24 = (bf16[512,1024]{1,0:T(8,128)(2,1)}, bf16[512,1024]{1,0:T(8,128)(2,1)S(1)}, u32[]{:S(2)}, u32[]{:S(2)}) collective-permute-start(bf16[512,1024]{1,0:T(8,128)(2,1)} %all-gather.13.cloned.1.call-done), channel_id=1, source_target_pairs={{0,4},{4,0},{8,12},{12,8},{16,20},{20,16},{24,28},{28,24},{1,5},{5... | collective-permute-start | bytes 3145736 | tf_op jit(solution)/shard_map/ppermute | solution.py:477
  209.5 28.2 %collective-permute-start.20 = (bf16[256,1024]{1,0:T(8,128)(2,1)S(1)}, bf16[256,1024]{1,0:T(8,128)(2,1)S(1)}, u32[]{:S(2)}, u32[]{:S(2)}) collective-permute-start(bf16[256,1024]{1,0:T(8,128)(2,1)S(1)} %pad_maximum_fusion.20), channel_id=1, source_target_pairs={{0,4},{4,0},{8,12},{12,8},{16,20},{20,16},{24,28},{28,24},{1,5},{5... | collective-permute-start | bytes 1572872 | tf_op jit(solution)/shard_map/ppermute | solution.py:477
  307.2 334.5 %reduce-scatter.17.cloned.1.call-start = ((), (), s32[]{:S(2)}) async-start(), calls=%async_computation.18 | async-start | bytes 2621440 | tf_op jit(solution)/shard_map/reduce_scatter | solution.py:548
  407.7 247.6 %reduce-scatter.19.cloned.1.call-start = ((), (), s32[]{:S(2)}) async-start(), calls=%async_computation.19 | async-start | bytes 2621440 | tf_op jit(solution)/shard_map/reduce_scatter | solution.py:548
  426.7 234.7 %reduce-scatter.23.cloned.1.call-start = ((), (), s32[]{:S(2)}) async-start(), calls=%async_computation.21 | async-start | bytes 2621440 | tf_op jit(solution)/shard_map/reduce_scatter | solution.py:548
  449.7 34.3 %collective-permute-start.45 = (bf16[256,1024]{1,0:T(8,128)(2,1)S(1)}, bf16[256,1024]{1,0:T(8,128)(2,1)S(1)}, u32[]{:S(2)}, u32[]{:S(2)}) collective-permute-start(bf16[256,1024]{1,0:T(8,128)(2,1)S(1)} %pad_maximum_fusion.25), channel_id=1, source_target_pairs={{0,2},{1,3},{2,0},{3,1},{4,6},{5,7},{6,4},{7,5},{8,10},{9,11},{10,... | collective-permute-start | bytes 1572872 | tf_op jit(solution)/shard_map/ppermute | solution.py:477
  462.2 27.0 %collective-permute-start.59 = (bf16[256,1152]{1,0:T(8,128)(2,1)S(1)}, bf16[256,1152]{1,0:T(8,128)(2,1)S(1)}, u32[]{:S(2)}, u32[]{:S(2)}) collective-permute-start(bf16[256,1152]{1,0:T(8,128)(2,1)S(1)} %pad_maximum_fusion.13), channel_id=1, source_target_pairs={{0,2},{1,3},{2,0},{3,1},{4,6},{5,7},{6,4},{7,5},{8,10},{9,11},{10,... | collective-permute-start | bytes 1769480 | tf_op jit(solution)/shard_map/ppermute | solution.py:477
  464.3 25.0 %collective-permute-start.58 = (bf16[128,1152]{1,0:T(8,128)(2,1)S(1)}, bf16[128,1152]{1,0:T(8,128)(2,1)S(1)}, u32[]{:S(2)}, u32[]{:S(2)}) collective-permute-start(bf16[128,1152]{1,0:T(8,128)(2,1)S(1)} %get-tuple-element.168), channel_id=1, source_target_pairs={{0,2},{1,3},{2,0},{3,1},{4,6},{5,7},{6,4},{7,5},{8,10},{9,11},{10,... | collective-permute-start | bytes 884744 | tf_op jit(solution)/shard_map/ppermute | solution.py:477
  500.4 212.3 %reduce-scatter.15.cloned.1.call-start = ((), (), s32[]{:S(2)}) async-start(), calls=%async_computation.17 | async-start | bytes 2293760 | tf_op jit(solution)/shard_map/reduce_scatter | solution.py:548
  551.8 216.8 %reduce-scatter.11.cloned.1.call-start = ((), (), s32[]{:S(2)}) async-start(), calls=%async_computation.15 | async-start | bytes 2621440 | tf_op jit(solution)/shard_map/reduce_scatter | solution.py:548
  630.4 140.5 %reduce-scatter.13.cloned.1.call-start = ((), (), s32[]{:S(2)}) async-start(), calls=%async_computation.16 | async-start | bytes 2621440 | tf_op jit(solution)/shard_map/reduce_scatter | solution.py:548
  655.2 117.8 %reduce-scatter.21.cloned.1.call-start = ((), (), s32[]{:S(2)}) async-start(), calls=%async_computation.20 | async-start | bytes 2621440 | tf_op jit(solution)/shard_map/reduce_scatter | solution.py:548
  712.5 97.1 %reduce-scatter.9.cloned.1.call-start = ((), (), s32[]{:S(2)}) async-start(), calls=%async_computation.14 | async-start | bytes 2293760 | tf_op jit(solution)/shard_map/reduce_scatter | solution.py:548
  (235 other events, 2985.7 us)
Sparse Core Ops, SparseCore 0:
  13.6 30.6 all-gather.6
  46.4 80.8 all-gather.8
  128.9 44.4 all-gather.10
  174.8 26.6 all-gather.12
  203.5 80.2 all-gather.14
  307.4 45.6 all-gather.16
  407.8 44.6 reduce-scatter.16
  454.9 43.1 reduce-scatter.18
  500.5 43.8 reduce-scatter.22
  551.9 38.4 reduce-scatter.14
  630.5 44.3 reduce-scatter.10
  677.0 43.1 reduce-scatter.12
  722.7 43.1 reduce-scatter.20
  768.6 40.6 reduce-scatter.8

commit v4 on v3

--- a/solution.py
+++ b/solution.py
@@ -214,30 +214,28 @@
     )(me, dy, *pack, q, k, v, lse, cos, sin)
 
 
-def attention_weights_kernel(x_ref, dqkv_ref, dy_ref, o_ref, low_ref, dl_ref, out_ref):
+def attention_weights_kernel(odd_ref, x_ref, dqkv_ref, dy_ref, o_ref, low_ref, dl_ref, own_ref, partner_ref):
     half = x_ref.shape[1] // 2
-    count = OUT_END + LANES
-    for n in range(2):
-        at = slice(n * half, (n + 1) * half)
-        to = n * count
-        out_ref[:, to : to + QKV] = dot_tn(x_ref[:, at], dqkv_ref[...]).astype(BF16)
-        out_ref[:, to + QKV : to + OUT_END] = dot_tn(dy_ref[:, at], o_ref[...]).astype(BF16)
-        out_ref[:, to + OUT_END : to + count] = dot_tn(low_ref[:, at], dl_ref[...]).astype(BF16)
-
-
-def attention_weights(x, dqkv, dy, o, low, dl):
+    for n, out_ref in enumerate((own_ref, partner_ref)):
+        at = pl.ds(pl.multiple_of((odd_ref[0] ^ n) * half, half), half)
+        out_ref[:, :QKV] = dot_tn(x_ref[:, at], dqkv_ref[...]).astype(BF16)
+        out_ref[:, QKV:OUT_END] = dot_tn(dy_ref[:, at], o_ref[...]).astype(BF16)
+        out_ref[:, OUT_END:] = dot_tn(low_ref[:, at], dl_ref[...]).astype(BF16)
+
+
+def attention_weights(odd, x, dqkv, dy, o, low, dl):
     rows, width = x.shape
     return pl.pallas_call(
         attention_weights_kernel,
-        out_shape=jax.ShapeDtypeStruct((width // 2, 2 * (OUT_END + LANES)), BF16),
-        in_specs=[VMEM_SPEC] * 6,
+        out_shape=(jax.ShapeDtypeStruct((width // 2, OUT_END + LANES), BF16),) * 2,
+        in_specs=[SMEM_SPEC] + [VMEM_SPEC] * 6,
         compiler_params=pltpu.CompilerParams(vmem_limit_bytes=32 * MIB),
         cost_estimate=pl.CostEstimate(flops=2 * rows * width * 800, bytes_accessed=9 * MIB, transcendentals=0),
         name="attention_weights",
-    )(x, dqkv, dy, o, low, dl)
-
-
-UP_STEP = 256
+    )(odd, x, dqkv, dy, o, low, dl)
+
+
+UP_STEP = 512
 BACK_STEP = 512
 
 
@@ -295,7 +293,7 @@
         in_specs=[SMEM_SPEC, pl.BlockSpec((rows, width), whole)] + weights + [router] * 2 + [wide] * 2,
         out_specs=[saved] * 3 + [wide] * 2,
         out_shape=(jax.ShapeDtypeStruct((rows, hidden), BF16),) * 3 + (jax.ShapeDtypeStruct((rows, LANES), F32),) * 2,
-        compiler_params=pltpu.CompilerParams(vmem_limit_bytes=52 * MIB),
+        compiler_params=pltpu.CompilerParams(vmem_limit_bytes=60 * MIB),
         cost_estimate=pl.CostEstimate(
             flops=4 * rows * width * hidden, bytes_accessed=22 * MIB, transcendentals=rows * hidden
         ),
@@ -305,22 +303,21 @@
 
 def experts_down_kernel(a_ref, da_ref, db_ref, out_ref):
     half = out_ref.shape[1] // 2
-    out_ref[:, :half] = dot_nt(a_ref[...], da_ref[...]).astype(BF16)
-    out_ref[:, half:] = dot_nt(a_ref[...], db_ref[...]).astype(BF16)
-
-
-def experts_down(active, down, part):
-    rows, hidden = active.shape[0] // 2, active.shape[1]
-    half = down.shape[0]
-    steps = rows // (2 * BLOCK)
-    weights = [pl.BlockSpec((half, hidden), lambda s, n=n: (0, n)) for n in range(2)]
+    out_ref[:, :half] = dot_nn(a_ref[...], da_ref[...]).astype(BF16)
+    out_ref[:, half:] = dot_nn(a_ref[...], db_ref[...]).astype(BF16)
+
+
+def experts_down(active, down):
+    rows, hidden = active.shape
+    half = down.shape[1]
+    weights = [pl.BlockSpec((hidden, half), lambda s, n=n: (n, 0)) for n in range(2)]
     return pl.pallas_call(
         experts_down_kernel,
-        grid=(steps,),
-        in_specs=[pl.BlockSpec((2 * BLOCK, hidden), lambda s: (s + part * steps, 0))] + weights,
+        grid=(rows // (2 * BLOCK),),
+        in_specs=[pl.BlockSpec((2 * BLOCK, hidden), lambda s: (s, 0))] + weights,
         out_specs=pl.BlockSpec((2 * BLOCK, 2 * half), lambda s: (s, 0)),
         out_shape=jax.ShapeDtypeStruct((rows, 2 * half), BF16),
-        compiler_params=pltpu.CompilerParams(vmem_limit_bytes=32 * MIB),
+        compiler_params=pltpu.CompilerParams(vmem_limit_bytes=60 * MIB),
         cost_estimate=pl.CostEstimate(flops=4 * rows * half * hidden, bytes_accessed=6 * MIB, transcendentals=0),
         name="experts_down",
     )(active, down, down)
@@ -341,7 +338,7 @@
     for n in range(count // 2):
         at = slice(2 * n * LANES, (2 * n + 2) * LANES)
         gate = pair_columns(columns, n)
-        da = dot_nn(dya, da_ref[:, at]) + dot_nn(dyb, db_ref[:, at])
+        da = dot_nt(dya, da_ref[at, :]) + dot_nt(dyb, db_ref[at, :])
         g = g_ref[:, at].astype(F32)
         u = u_ref[:, at].astype(F32)
         logistic = jax.nn.sigmoid(g)
@@ -382,7 +379,7 @@
         grid=(steps,),
         in_specs=[SMEM_SPEC, pl.BlockSpec((rows, width), whole, pipeline_mode=once)]
         + weights
-        + weights[:2]
+        + [pl.BlockSpec((BACK_STEP, width // 2), lambda s, n=n: (s + n * steps, 0)) for n in range(2)]
         + [saved] * 2
         + [pl.BlockSpec((rows, LANES), whole, pipeline_mode=once)],
         out_specs=[saved, saved, pl.BlockSpec((rows, width + LANES), whole, pipeline_mode=once)],
@@ -400,34 +397,118 @@
     )(base, dy, gate_up, gate_up, gate_up, gate_up, down, down, g, u, gates)
 
 
-def expert_weights_kernel(x_ref, r_ref, out_ref):
-    out_ref[...] = dot_tn(x_ref[...], r_ref[...]).astype(BF16)
-
-
-def expert_weights(x, rights):
-    rows, width = x.shape
-    hidden = rights[0].shape[1]
-    steps = hidden // BACK_STEP
-    outs = []
-    for right in rights:
-        outs.append(
-            pl.pallas_call(
-                expert_weights_kernel,
-                grid=(2, steps),
-                in_specs=[
-                    pl.BlockSpec((rows, width // 2), lambda h, s: (0, h)),
-                    pl.BlockSpec((rows, BACK_STEP), lambda h, s: (0, s)),
-                ],
-                out_specs=pl.BlockSpec((width // 2, BACK_STEP), lambda h, s: (0, h * steps + s)),
-                out_shape=jax.ShapeDtypeStruct((width // 2, 2 * hidden), BF16),
-                compiler_params=pltpu.CompilerParams(vmem_limit_bytes=40 * MIB),
-                cost_estimate=pl.CostEstimate(
-                    flops=2 * rows * width * hidden, bytes_accessed=12 * MIB, transcendentals=0
-                ),
-                name="expert_weights",
-            )(x, right)
-        )
-    return outs
+def expert_weights_kernel(xn_ref, xf_ref, rn_ref, rf_ref, out_ref):
+    out_ref[...] = (dot_tn(xn_ref[...], rn_ref[...]) + dot_tn(xf_ref[...], rf_ref[...])).astype(BF16)
+
+
+def expert_weights(x, right):
+    rows, width = x[0].shape
+    hidden = right[0].shape[1]
+    return pl.pallas_call(
+        expert_weights_kernel,
+        grid=(2,),
+        in_specs=[pl.BlockSpec((rows, width // 2), lambda h: (0, h))] * 2
+        + [pl.BlockSpec((rows, hidden), lambda h: (0, 0))] * 2,
+        out_specs=pl.BlockSpec((width // 2, hidden), lambda h: (0, h)),
+        out_shape=jax.ShapeDtypeStruct((width // 2, 2 * hidden), BF16),
+        compiler_params=pltpu.CompilerParams(vmem_limit_bytes=60 * MIB),
+        cost_estimate=pl.CostEstimate(flops=4 * rows * width * hidden, bytes_accessed=12 * MIB, transcendentals=0),
+        name="expert_weights",
+    )(*x, *right)
+
+
+def gate_up_out_kernel(odd_ref, tg_ref, og_ref, tu_ref, ou_ref, wg_ref, wu_ref, *refs):
+    gate_ref, up_ref, term_ref = refs[-3:]
+    share = gate_ref.shape[1] // 2
+    total = jnp.zeros(term_ref.shape, F32)
+    for mine, start in ((True, odd_ref[0] * share), (False, (1 - odd_ref[0]) * share)):
+        for e in range(share):
+            at = slice(e * LANES, (e + 1) * LANES)
+            dg = (tg_ref if mine else og_ref)[:, at].astype(F32)
+            du = (tu_ref if mine else ou_ref)[:, at].astype(F32)
+            gate_ref[0, start + e] = dg
+            up_ref[0, start + e] = du
+            total += dg * wg_ref[0, start + e].astype(F32) + du * wu_ref[0, start + e].astype(F32)
+    term_ref[...] = total
+
+
+def gate_up_out(odd, layer, totals, others, w_gate, w_up, earlier):
+    layers, experts, depth, wide = w_gate.shape
+    own = pl.BlockSpec((depth, others[0].shape[1]), lambda i, odd: (0, odd[0]))
+    other = pl.BlockSpec(others[0].shape, lambda i, odd: (0, 0))
+    block = pl.BlockSpec((1, experts, depth, wide), lambda i, odd: (layer, 0, 0, 0))
+    return pl.pallas_call(
+        gate_up_out_kernel,
+        grid_spec=pltpu.PrefetchScalarGridSpec(
+            num_scalar_prefetch=1,
+            grid=(1,),
+            in_specs=[own, other, own, other, block, block] + [pl.BlockSpec(memory_space=pl.ANY)] * len(earlier),
+            out_specs=[block, block, pl.BlockSpec((depth, wide), lambda i, odd: (0, 0))],
+        ),
+        out_shape=(jax.ShapeDtypeStruct(w_gate.shape, F32),) * 2 + (jax.ShapeDtypeStruct((depth, wide), F32),),
+        input_output_aliases={7 + n: n for n in range(len(earlier))},
+        compiler_params=pltpu.CompilerParams(vmem_limit_bytes=24 * MIB),
+        name="gate_up_out",
+    )(odd, totals[0], others[0], totals[1], others[1], w_gate, w_up, *earlier)
+
+
+def down_out_kernel(odd_ref, t_ref, o_ref, *refs):
+    out_ref = refs[-1]
+    share, wide = out_ref.shape[1] // 2, out_ref.shape[2]
+    for e in range(share):
+        at = slice(e * wide, (e + 1) * wide)
+        out_ref[0, odd_ref[0] * share + e] = t_ref[:, at].astype(F32).T
+        out_ref[0, (1 - odd_ref[0]) * share + e] = o_ref[:, at].astype(F32).T
+
+
+def down_out(odd, layer, total, other, shape, earlier):
+    block = pl.BlockSpec((1,) + shape[1:], lambda i, odd: (layer, 0, 0, 0))
+    return pl.pallas_call(
+        down_out_kernel,
+        grid_spec=pltpu.PrefetchScalarGridSpec(
+            num_scalar_prefetch=1,
+            grid=(1,),
+            in_specs=[pl.BlockSpec(other.shape, lambda i, odd: (0, odd[0])), pl.BlockSpec(other.shape, lambda i, odd: (0, 0))]
+            + [pl.BlockSpec(memory_space=pl.ANY)] * len(earlier),
+            out_specs=block,
+        ),
+        out_shape=jax.ShapeDtypeStruct(shape, F32),
+        input_output_aliases={3 + n: n for n in range(len(earlier))},
+        compiler_params=pltpu.CompilerParams(vmem_limit_bytes=24 * MIB),
+        name="down_out",
+    )(odd, total, other, *earlier)
+
+
+def pack_out_kernel(t_ref, w_ref, *refs):
+    q_ref, k_ref, v_ref, wo_ref, stats_ref = refs[-5:]
+    total = t_ref[...].astype(F32)
+    q_ref[0] = total[:, : 2 * LANES]
+    k_ref[0] = total[:, 2 * LANES : 3 * LANES]
+    v_ref[0] = total[:, 3 * LANES : QKV]
+    wo_ref[0] = total[:, QKV:OUT_END].T
+    term = jnp.sum(total[:, :QKV] * w_ref[:, :QKV].astype(F32), axis=1, keepdims=True)
+    stats = total[:, OUT_END:]
+    lane = lax.broadcasted_iota(jnp.int32, stats.shape, 1)
+    stats_ref[...] = jnp.where(lane == EXPERTS, term, jnp.where(lane < EXPERTS, stats, 0.0))
+
+
+def pack_out(layer, total, pack, earlier):
+    depth, columns = total.shape
+    shapes = [(depth, 2 * LANES), (depth, LANES), (depth, LANES), (2 * LANES, depth)]
+    whole = lambda i: (0, 0)
+    return pl.pallas_call(
+        pack_out_kernel,
+        grid=(1,),
+        in_specs=[pl.BlockSpec(total.shape, whole), pl.BlockSpec(pack.shape, whole)]
+        + [pl.BlockSpec(memory_space=pl.ANY)] * len(earlier),
+        out_specs=[pl.BlockSpec((1,) + shape, lambda i: (layer, 0, 0)) for shape in shapes]
+        + [pl.BlockSpec((depth, LANES), whole)],
+        out_shape=tuple(jax.ShapeDtypeStruct((LAYER_COUNT,) + shape, F32) for shape in shapes)
+        + (jax.ShapeDtypeStruct((depth, LANES), F32),),
+        input_output_aliases={2 + n: n for n in range(len(earlier))},
+        compiler_params=pltpu.CompilerParams(vmem_limit_bytes=24 * MIB),
+        name="pack_out",
+    )(total, pack, *earlier)
 
 
 def normalize(residual, gain):
@@ -450,25 +531,34 @@
     return jnp.concatenate([cos] * 4, axis=1), jnp.concatenate([-sin, sin] * 2, axis=1)
 
 
-def place_codes(size):
-    return [(p % (size // 2)) * 2 + p // (size // 2) for p in range(size)]
-
-
-def route_masks(routes, me):
+def route_masks(routes, partner, me):
     rows = routes.shape[0]
-    size = lax.axis_size("tensor")
-    own = rows // size
-    starts = [(me ^ code) * own for code in place_codes(size)]
-    routes = jnp.concatenate([lax.dynamic_slice_in_dim(routes, start, own, 0) for start in starts], axis=0)
+    half = rows // (2 * lax.axis_size("tensor"))
     lane = lax.broadcasted_iota(jnp.int32, (rows, LANES), 1)
-    chosen = routes[:, 0:1] == lane
-    for k in range(1, TOPK):
-        chosen = chosen | (routes[:, k : k + 1] == lane)
-    position = jnp.concatenate([start + jnp.arange(own, dtype=jnp.int32) for start in starts])
-    earlier = (position[:, None] > position[None, :]).astype(BF16)
-    before = dot_nn(earlier, chosen.astype(BF16))
-    kept = chosen & (before < CAP)
-    return chosen.astype(F32), kept.astype(F32)
+    earlier = (
+        lax.broadcasted_iota(jnp.int32, (rows, rows), 0) > lax.broadcasted_iota(jnp.int32, (rows, rows), 1)
+    ).astype(BF16)
+    both = []
+    for named in (routes, partner):
+        chosen = named[:, 0:1] == lane
+        for k in range(1, TOPK):
+            chosen = chosen | (named[:, k : k + 1] == lane)
+        before = dot_nn(earlier, chosen.astype(BF16))
+        both.append((chosen.astype(F32), (chosen & (before < CAP)).astype(F32)))
+
+    def placed(which, core):
+        parts = []
+        for lower, places in ((0, ((0, 0), (0, 2), (1, 0), (1, 2))), (1, ((0, 0), (1, 0), (0, 2), (1, 2)))):
+            for x, y in places:
+                start = ((me ^ (y + core)) * 2 + lower) * half
+                parts.append(lax.dynamic_slice_in_dim(both[x][which], start, half, 0))
+        return jnp.concatenate(parts, axis=0)
+
+    return [[placed(which, core) for core in range(2)] for which in range(2)]
+
+
+def after(values, *earlier):
+    return lax.optimization_barrier((values,) + earlier)[0]
 
 
 def swap(values, which):
@@ -477,51 +567,63 @@
     return lax.ppermute(values, axis, [(i, i ^ bit) for i in range(size)])
 
 
-def widen(values):
+def widen(values, meanwhile=None):
     other = swap(values, "y")
-    near = [values, other]
-    return jnp.concatenate(near + [swap(piece, "core") for piece in near], axis=0)
+    sibling = swap(values, "core")
+    if meanwhile is not None:
+        other = after(other, *meanwhile(sibling))
+    return jnp.concatenate([values, other, sibling, swap(other, "core")], axis=0)
 
 
 def widen_pair(values):
     half = values.shape[0] // 2
     by_y, by_x = swap(values, "y"), swap(values, "x")
     first, second = swap(by_y[:half], "x"), swap(by_x[half:], "y")
-    near = [values, by_y, by_x, first, second]
-    return jnp.concatenate(near + [swap(piece, "core") for piece in near], axis=0)
+    near = jnp.concatenate(
+        [values[:half], by_y[:half], by_x[:half], first, values[half:], by_x[half:], by_y[half:], second], axis=0
+    )
+    return near, swap(near, "core")
 
 
 def added(left, right):
     return left.astype(F32) + right.astype(F32)
 
 
-def narrow(values):
+def narrow(values, meanwhile=None):
     rows = values.shape[0] // 4
     far, near = values[2 * rows :], values[: 2 * rows]
-    out = added(near[rows:], swap(far[rows:], "core")).astype(BF16)
-    out = swap(out, "y")
+    sent = added(near[rows:], swap(far[rows:], "core")).astype(BF16)
+    out = swap(sent, "y")
+    if meanwhile is not None:
+        out = after(out, *meanwhile(sent))
     return added(near[:rows], swap(far[:rows], "core")) + out.astype(F32)
 
 
-def narrow_pair(near, far):
-    rows = near.shape[0] // 4
-    half = rows // 2
+def pair_pieces(near, far):
+    half = near.shape[0] // 8
     received = swap(far, "core")
 
-    def piece(n, lower):
-        at = slice(n * rows + lower * half, n * rows + (lower + 1) * half)
-        return added(near[at], received[at])
-
-    def sent(*pieces):
-        return jnp.concatenate([p.astype(BF16) for p in pieces], axis=0)
-
-    x_first = swap(sent(piece(2, 0), piece(3, 0)), "x")
-    y_first = swap(sent(piece(1, 1), piece(3, 1)), "y")
-    y_second = swap(added(piece(1, 0), x_first[half:]).astype(BF16), "y")
-    x_second = swap(added(piece(2, 1), y_first[half:]).astype(BF16), "x")
-    upper = added(piece(0, 0), x_first[:half]) + y_second.astype(F32)
-    lower = added(piece(0, 1), y_first[:half]) + x_second.astype(F32)
+    def piece(start, end):
+        return added(near[start * half : end * half], received[start * half : end * half])
+
+    return piece, piece(2, 4).astype(BF16), piece(6, 8).astype(BF16)
+
+
+def pair_sum(piece, x_first, y_first):
+    half = x_first.shape[0] // 2
+    y_second = swap((piece(1, 2) + x_first[half:].astype(F32)).astype(BF16), "y")
+    x_second = swap((piece(5, 6) + y_first[half:].astype(F32)).astype(BF16), "x")
+    upper = piece(0, 1) + x_first[:half].astype(F32) + y_second.astype(F32)
+    lower = piece(4, 5) + y_first[:half].astype(F32) + x_second.astype(F32)
     return jnp.concatenate([upper, lower], axis=0)
+
+
+def narrow_pair(near, far, meanwhile=None):
+    piece, to_x, to_y = pair_pieces(near, far)
+    x_first, y_first = swap(to_x, "x"), swap(to_y, "y")
+    if meanwhile is not None:
+        x_first = after(x_first, *meanwhile(to_x))
+    return pair_sum(piece, x_first, y_first)
 
 
 def sum_over_tensor(values):
@@ -541,14 +643,16 @@
         even = self.odd == 0
         return jnp.where(even, mine, other), jnp.where(even, other, mine)
 
-    def gather(self, own):
-        return lax.all_gather(own, "dp", axis=0, tiled=True, axis_index_groups=self.groups)
-
-    def scatter(self, values):
-        total = lax.psum_scatter(values, "dp", scatter_dimension=0, tiled=True, axis_index_groups=self.groups)
-        n = total.shape[1] // 2
-        even, odd = total[:, :n], total[:, n:]
-        return self.by_parity(even, odd)
+    def gather(self, own, axis=0):
+        return lax.all_gather(own, "dp", axis=axis, tiled=True, axis_index_groups=self.groups)
+
+    def scatter(self, values, axis=0):
+        return lax.psum_scatter(values, "dp", scatter_dimension=axis, tiled=True, axis_index_groups=self.groups)
+
+    def from_partner(self, total, axis, *earlier):
+        size = total.shape[axis] // 2
+        sent = lax.dynamic_slice_in_dim(total, (1 - self.odd) * size, size, axis)
+        return swap(after(sent, *earlier) if earlier else sent, "x")
 
     def relative(self, values):
         depth = values.shape[1] // self.size
@@ -598,16 +702,17 @@
     cos, sin = rope_tables(rows_own * lax.axis_size("tensor"))
     data = Data()
     share = EXPERTS // 2
-    base = (data.odd * share).reshape(1).astype(jnp.int32)
-
-    packs, mine = [], []
+    odd = data.odd.reshape(1).astype(jnp.int32)
+    base = odd * share
+
+    packs = []
     for layer in range(LAYER_COUNT):
         small = jnp.concatenate(
             [
                 w_router[layer],
-                attn_gain[layer][:, None],
-                moe_gain[layer][:, None],
-                jnp.zeros((depth, PACK - OUT_END - EXPERTS - 2), BF16),
+                attn_gain.T,
+                moe_gain.T,
+                jnp.zeros((depth, PACK - OUT_END - EXPERTS - 2 * LAYER_COUNT), BF16),
             ],
             axis=1,
         )
@@ -620,81 +725,130 @@
     def shares(weight):
         return [lax.dynamic_slice_in_dim(weight, start * share, share, 0) for start in (data.odd, 1 - data.odd)]
 
-    gathered = []
-    for layer in range(LAYER_COUNT):
-        gate, up, down = shares(w_gate[layer]), shares(w_up[layer]), shares(w_down[layer])
-        other = swap(jnp.concatenate([gate[1], up[1]], axis=0), "x")
-        other_down = swap(down[1], "x")
+    def gate_up_columns(layer, *earlier):
+        gate, up = shares(w_gate[layer]), shares(w_up[layer])
+        sent = jnp.concatenate([gate[1], up[1]], axis=0)
+        other = swap(after(sent, *earlier) if earlier else sent, "x")
         columns = [
             part.transpose(1, 0, 2).reshape(depth, -1)
             for own, got in ((gate[0], other[:share]), (up[0], other[share:]))
             for part in data.by_parity(own, got)
         ]
-        down_columns = [part.reshape(-1, depth).T for part in data.by_parity(down[0], other_down)]
-        gathered.append(
-            (
-                data.gather(packs[layer]),
-                data.gather(jnp.concatenate(columns, axis=1)),
-                data.gather(jnp.concatenate(down_columns, axis=1)),
-            )
+        return jnp.concatenate(columns, axis=1)
+
+    def down_rows(layer, *earlier):
+        down = shares(w_down[layer])
+        sent = after(down[1], *earlier) if earlier else down[1]
+        return jnp.concatenate(
+            [part.reshape(-1, depth) for part in data.by_parity(down[0], swap(sent, "x"))], axis=0
         )
 
-    partner_routes = swap(routes, "x")
+    own_packs = [data.gather(packs[0])]
+    tokens_in = data.relative(after(tokens_in, packs[0]))
+    tokens_all = widen(tokens_in)
+    columns = gate_up_columns(0, packs[0])
+    gate_ups = [data.gather(columns)]
+    pack = data.by_parity(own_packs[0], swap(after(own_packs[0], columns), "x"))
+    rows = down_rows(0, pack[0])
+    downs = [data.gather(rows, 1)]
+    own_packs.append(data.gather(after(packs[1], rows)))
+    next_columns, next_rows = gate_up_columns(1, pack[0]), down_rows(1, pack[0])
+    gate_ups.append(data.gather(next_columns))
+    downs.append(data.gather(next_rows, 1))
     masks = []
-    for layer in range(LAYER_COUNT):
-        own = route_masks(routes[layer], me)
-        partner = route_masks(partner_routes[layer], me)
-        middle = own[0].shape[0] // 2
-        masks.append(
-            [jnp.concatenate([a[:middle], b[:middle], a[middle:], b[middle:]]) for a, b in zip(own, partner)]
-        )
-
-    tokens_in, cotangent = data.relative(tokens_in), data.relative(cotangent)
+
+    def mask(layer, point):
+        masks.append(route_masks(after(routes[layer], point), after(partner_routes[layer], point), me))
+        return [*masks[-1][0], *masks[-1][1]]
+
     residual = tokens_in.astype(F32)
-    tokens_all = widen(tokens_in)
     weights, records = [], []
     for layer in range(LAYER_COUNT):
-        own_pack, gate_up, down = gathered[layer]
-        pack = data.by_parity(own_pack, swap(own_pack, "x"))
-        gain_attn, gain_moe = (
-            jnp.concatenate([part[:, OUT_END + EXPERTS + n].astype(F32) for part in pack])[None, :] for n in range(2)
-        )
+        gate_up, down = gate_ups[layer], downs[layer]
+        if layer > 0:
+            pack = data.by_parity(own_packs[layer], swap(after(own_packs[layer], residual), "x"))
+        if layer == 0:
+            gains = [
+                jnp.concatenate([part[:, OUT_END + EXPERTS + n].astype(F32) for part in pack])[None, :]
+                for n in range(2 * LAYER_COUNT)
+            ]
+        gain_attn, gain_moe = gains[layer], gains[LAYER_COUNT + layer]
         weights.append((pack, gain_attn, gain_moe, gate_up, down))
-        chosen, kept = masks[layer]
         if layer == 0:
             hidden_attn = normalize(tokens_all.astype(F32), gain_attn)[2]
+            cotangent = data.relative(after(cotangent, hidden_attn))
+            partner_routes = swap(after(routes, pack[0]), "x")
         else:
             hidden_attn = widen(normalize(residual, gain_attn)[2])
         before_attn = residual
         q, k, v, mixed, lse, attn_part = attention_forward(me_array, hidden_attn, pack, cos, sin)
-        residual = residual + narrow(attn_part)
+        if layer == 0:
+            held = lambda point: mask(0, point) + [next_columns, next_rows]
+        else:
+            held = lambda point, layer=layer: mask(layer, point)
+        residual = residual + narrow(attn_part, held)
         before_moe = residual
         low_moe = normalize(residual, gain_moe)[2]
         hidden_moe = widen_pair(low_moe)
-        g, u, active, probs, gates = experts_up(base, hidden_moe, gate_up, pack, chosen, kept)
-        far = experts_down(active, down, 1)
-        near = experts_down(active, down, 0)
-        residual = residual + narrow_pair(near, far)
+        chosen, kept = masks[layer]
+        parts = [experts_up(base, hidden_moe[0], gate_up, pack, chosen[0], kept[0])]
+        parts.append(experts_up(base, after(hidden_moe[1], parts[0][2]), gate_up, pack, chosen[1], kept[1]))
+        g, u, active, probs, gates = zip(*parts)
         records.append(
-            (before_attn, hidden_attn, q, k, v, mixed, lse, before_moe, low_moe, hidden_moe, probs, gates, g, u, active)
+            (before_attn, hidden_attn, q, k, v, mixed, lse, before_moe, low_moe, hidden_moe, probs[0], gates, g, u, active)
         )
+        if layer < LAYER_COUNT - 1:
+            active = after(active, *active)
+            far, near = (experts_down(active[n], down) for n in (1, 0))
+            residual = residual + narrow_pair(near, far)
     grad = cotangent.astype(F32)
     pieces = []
+    half = rows_own // 2
+
+    def own_of(values):
+        return jnp.concatenate([values[:half], values[4 * half : 5 * half]], axis=0)
+
     for layer in reversed(range(LAYER_COUNT)):
         pack, gain_attn, gain_moe, gate_up, down = weights[layer]
         before_attn, hidden_attn, q, k, v, mixed, lse, before_moe, low_moe, hidden_moe, probs, gates, g, u, active = (
             records[layer]
         )
-        kept = masks[layer][1]
+        kept = masks[layer][1][0]
         grad_pair = widen_pair(grad.astype(BF16))
-        (grad_down,) = expert_weights(grad_pair, (active,))
+        if layer == LAYER_COUNT - 1:
+            grad_down = expert_weights(grad_pair, active)
+            grad_pair = after(grad_pair, grad_down)
+        parts = [experts_backward(base, grad_pair[0], gate_up, down, g[0], u[0], gates[0])]
+        grad_far = after(grad_pair[1], parts[0][0])
+        if layer < LAYER_COUNT - 1:
+            grad_down = expert_weights((grad_pair[0], grad_far), active)
+            grad_far = after(grad_far, grad_down)
         grad_down = data.scatter(grad_down)
-        grad_gate, grad_up, moe_part = experts_backward(base, grad_pair, gate_up, down, g, u, gates)
-        middle = moe_part.shape[0] // 2
-        own = narrow_pair(moe_part[:middle], moe_part[middle:])
-        grad_gate, grad_up = (data.scatter(part) for part in expert_weights(hidden_moe, (grad_gate, grad_up)))
-        grad_moe_own, grad_pairs = own[:, :width], own[:, width:] * kept[:rows_own]
-        own_probs = probs[:rows_own]
+        parts.append(experts_backward(base, grad_far, gate_up, down, g[1], u[1], gates[1]))
+        grad_gate, grad_up, moe_part = zip(*parts)
+        if layer == 0:
+            result_first = swap(result_x, "x"), swap(result_y, "y")
+            moe_part = after(moe_part, *result_first)
+        made = []
+
+        def meanwhile(point, active=active, down=down, made=made, last=layer == LAYER_COUNT - 1, right=grad_gate):
+            if last:
+                held = after(active, point)
+                made.extend(experts_down(held[n], down) for n in (1, 0))
+            else:
+                made.append(expert_weights(hidden_moe, after(right, point)))
+            return made
+
+        own = narrow_pair(*moe_part, meanwhile)
+        if layer == LAYER_COUNT - 1:
+            far, near = made
+            result_piece, result_x, result_y = pair_pieces(near, far)
+            grad_gate = expert_weights(hidden_moe, after(grad_gate, far, near))
+        else:
+            (grad_gate,) = made
+        grad_gate = data.scatter(grad_gate)
+        grad_moe_own, grad_pairs = own[:, :width], own[:, width:] * own_of(kept)
+        own_probs = own_of(probs)
         grad_chosen = own_probs * (grad_pairs - jnp.sum(own_probs * grad_pairs, axis=-1, keepdims=True))
         grad_logits = grad_chosen.astype(BF16)
         grad_moe_own = grad_moe_own + jnp.concatenate(
@@ -702,57 +856,85 @@
         )
         normed_moe, scale_moe, _ = normalize(before_moe, gain_moe)
         grad = grad + normalize_back(grad_moe_own, normed_moe, scale_moe, gain_moe)
-        grad_all = widen(grad.astype(BF16))
+        grad_low = grad.astype(BF16)
+        made = []
+
+        def meanwhile(point, made=made, right=grad_up):
+            made.append(expert_weights(hidden_moe, after(right, point)))
+            return made
+
+        if layer == 0:
+            later_pack, _, later_up, _ = pieces[0]
+
+            def meanwhile(point, made=made, first=meanwhile):
+                partners.append(data.from_partner(later_up, 1, point))
+                partners.append(data.from_partner(later_pack, 1, point))
+                return first(point) + partners[2:]
+
+        grad_all = widen(grad_low, meanwhile)
+        grad_up = data.scatter(made[0])
         grad_qkv, attn_part = attention_backward(me_array, grad_all, pack, q, k, v, lse, cos, sin)
-        grad_pack = data.scatter(attention_weights(hidden_attn, grad_qkv, grad_all, mixed, low_moe, grad_logits))
+        pack_product = attention_weights(odd, hidden_attn, grad_qkv, grad_all, mixed, low_moe, grad_logits)
+        if layer == LAYER_COUNT - 1:
+            partners = []
+
+            def meanwhile(point, grad_down=grad_down, grad_gate=grad_gate):
+                partners.extend(data.from_partner(part, 1, point) for part in (grad_down, grad_gate))
+                return [*pack_product, result_x, result_y, *partners]
+
+        else:
+            meanwhile = lambda point: pack_product
+        attn_own = narrow(attn_part, meanwhile)
+        own_product, partner_product = pack_product
+        if layer == 0:
+            own_product = added(own_product, swap(partner_product, "x")).astype(BF16)
+            grad_pack = data.scatter(own_product)
+        else:
+            halves = jnp.where(data.odd == 0, own_product, partner_product), jnp.where(
+                data.odd == 0, partner_product, own_product
+            )
+            grad_pack = data.scatter(jnp.concatenate(halves, axis=1))
         normed_attn, scale_attn, _ = normalize(before_attn, gain_attn)
-        grad = grad + normalize_back(narrow(attn_part), normed_attn, scale_attn, gain_attn)
+        grad = grad + normalize_back(attn_own, normed_attn, scale_attn, gain_attn)
         pieces.insert(0, (grad_pack, grad_gate, grad_up, grad_down))
-
-    outputs = []
-    for layer in range(LAYER_COUNT):
+    residual = residual + pair_sum(result_piece, *after(result_first, *pack_product))
+    result, input_grad = data.absolute(residual), data.absolute(grad)
+    stacked_experts, stacked_down, stacked_pack, stats = (), (), (), [None] * LAYER_COUNT
+    lane = lax.broadcasted_iota(jnp.int32, (depth, LANES), 1)
+    for layer in reversed(range(LAYER_COUNT)):
         grad_pack, grad_gate, grad_up, grad_down = pieces[layer]
-        grad_pack = added(grad_pack[0], swap(grad_pack[1], "x"))
-
-        def experts_of(pair, turned):
-            both = data.by_parity(pair[0], swap(pair[1], "x"))
-            both = jnp.stack([part.T if turned else part for part in both]).astype(F32)
-            if turned:
-                return both.reshape(EXPERTS, -1, depth)
-            return both.reshape(2, depth, share, -1).transpose(0, 2, 1, 3).reshape(EXPERTS, depth, -1)
-
-        grad_gate, grad_up = experts_of(grad_gate, False), experts_of(grad_up, False)
-        own_pack = packs[layer].astype(F32)
-        attn_term = jnp.sum(own_pack[:, :QKV] * grad_pack[:, :QKV], axis=1)[:, None]
-        moe_term = jnp.sum(
-            w_gate[layer].astype(F32) * grad_gate + w_up[layer].astype(F32) * grad_up, axis=(0, 2)
-        )[:, None]
-        lane = lax.broadcasted_iota(jnp.int32, (depth, LANES), 1)
-        stats = grad_pack[:, OUT_END:]
-        stats = jnp.where(lane == EXPERTS, attn_term, jnp.where(lane == EXPERTS + 1, moe_term, stats))
-        stats = sum_over_tensor(stats)
-        router_grad = stats[:, :EXPERTS]
-        router_own = own_pack[:, OUT_END : OUT_END + EXPERTS]
-        attn_gain_grad = stats[:, EXPERTS] / attn_gain[layer].astype(F32)
-        moe_gain_grad = (stats[:, EXPERTS + 1] + jnp.sum(router_own * router_grad, axis=1)) / moe_gain[layer].astype(
-            F32
+        if layer > 0:
+            others = partners
+            columns = grad_pack.shape[1] // 2
+            grad_pack = added(lax.dynamic_slice_in_dim(grad_pack, data.odd * columns, columns, 1), partners[3])
+        else:
+            others = [data.from_partner(part, 1, own_product) for part in (grad_down, grad_gate, grad_up)]
+        stacked_down = (down_out(odd, layer, grad_down, others[0], w_down.shape, stacked_down),)
+        *stacked_experts, term = gate_up_out(
+            odd, layer, (grad_gate, grad_up), others[1:3], w_gate, w_up, stacked_experts
         )
-        outputs.append(
-            (
-                attn_gain_grad,
-                grad_pack[:, :q_columns],
-                grad_pack[:, q_columns : q_columns + kv_columns],
-                grad_pack[:, q_columns + kv_columns : QKV],
-                grad_pack[:, QKV:OUT_END].T,
-                moe_gain_grad,
-                router_grad,
-                grad_gate,
-                grad_up,
-                experts_of(grad_down, True),
-            )
-        )
-    stacked = tuple(jnp.stack([terms[n] for terms in outputs]) for n in range(10))
-    return (data.absolute(residual), data.absolute(grad)) + stacked
+        if layer == 0:
+            grad_pack = after(grad_pack, term, result, input_grad, *stacked_experts, *stacked_down, stats[-1])
+        *stacked_pack, stat = pack_out(layer, grad_pack, packs[layer], stacked_pack)
+        stats[layer] = sum_over_tensor(jnp.where(lane == EXPERTS + 1, jnp.sum(term, axis=1, keepdims=True), stat))
+    stats = jnp.stack(stats)
+    router_grad = stats[:, :, :EXPERTS]
+    attn_gain_grad = stats[:, :, EXPERTS] / attn_gain.astype(F32)
+    moe_gain_grad = (stats[:, :, EXPERTS + 1] + jnp.sum(w_router.astype(F32) * router_grad, axis=2)) / moe_gain.astype(F32)
+    grad_query, grad_key, grad_value, grad_out = stacked_pack
+    return (
+        result,
+        input_grad,
+        attn_gain_grad,
+        grad_query,
+        grad_key,
+        grad_value,
+        grad_out,
+        moe_gain_grad,
+        router_grad,
+        *stacked_experts,
+        *stacked_down,
+    )
 
 
 def solution(mesh):

time: 842 us -> 772 us (0.917)
  other arithmetic: 130 us -> 84 us
  waiting for transfers between devices: 280 us -> 234 us
  Pallas kernels: 208 us -> 239 us
    ppermute x99 -> x83, waiting for transfers between devices: 274 us -> 231 us  [swap(): return lax.ppermute(values, axis, [(i, i ^ bit) for i in range(size)])]
    pallas_call x12 -> x18, Pallas kernels: 65.6 us -> 85.8 us  [the longest x6 52.1 us: expert_weights(): pl.pallas_call(expert_weights_kernel, grid=(2,), in_specs=[pl.BlockSpec((...]
    another operation x18 -> x2, other arithmetic: 15.5 us -> 0.13 us  [local(): stats = jnp.stack(stats)]
    dynamic_slice x2 -> x7, local copies, waits for them, and re-layouts: 0.03 us -> 10.4 us  [from_partner(): sent = lax.dynamic_slice_in_dim(total, (1 - self.odd) * size, size, axis)]
    select_n x12 -> x4, other arithmetic: 11.3 us -> 2.54 us  [by_parity(): return (jnp.where(even, mine, other), jnp.where(even, other, mine))]
    pallas_call x2 -> x4, Pallas kernels: 35.3 us -> 42 us  [experts_up(): pl.pallas_call(experts_up_kernel, grid=(steps,), in_specs=[SMEM_SPEC, pl....]
    pallas_call x2 -> x4, Pallas kernels: 54.7 us -> 59.4 us  [experts_backward(): pl.pallas_call(experts_backward_kernel, grid=(steps,), in_specs=[SMEM_SPE...]
    unnamed x358 -> x343, local copies, waits for them, and re-layouts: 69.7 us -> 65.1 us
  transfers between devices with their start and end apart: 113 -> 97, of which waited for: 43 -> 45; matrix products, arithmetic and copies ran while one was open for 26% -> 23% of each run, Pallas kernels for 21% -> 27%
where the time goes in v4:
time: 772 us; the launch traced here: 765 us
  Pallas kernels  239 us (31%)
  waiting for transfers between devices  234 us (30%)
  local copies, waits for them, and re-layouts  110 us (14%)
  other arithmetic  84 us (11%)
  starting transfers between devices  72 us (9%)
  between operations  16.5 us (2%)
  matrix products  9.87 us (1%)
    ppermute x83, waiting for transfers between devices, swap(): return lax.ppermute(values, axis, [(i, i ^ bit) for i in range(size)])  231 us
    ppermute x83, starting transfers between devices, swap(): return lax.ppermute(values, axis, [(i, i ^ bit) for i in range(size)])  70.3 us
    unnamed x343, local copies, waits for them, and re-layouts  65.1 us
    pallas_call x4, Pallas kernels, experts_backward(): pl.pallas_call(experts_backward_kernel, grid=(steps,), in_specs=[SMEM_SPE...  59.4 us
    pallas_call x6, Pallas kernels, expert_weights(): pl.pallas_call(expert_weights_kernel, grid=(2,), in_specs=[pl.BlockSpec((...  52.1 us
    pallas_call x4, Pallas kernels, experts_up(): pl.pallas_call(experts_up_kernel, grid=(steps,), in_specs=[SMEM_SPEC, pl....  42 us
    pallas_call x2, Pallas kernels, attention_backward(): pl.pallas_call(attention_backward_kernel, out_shape=(jax.ShapeDtypeStruct...  30.1 us
    pallas_call x4, Pallas kernels, experts_down(): pl.pallas_call(experts_down_kernel, grid=(rows // (2 * BLOCK),), in_specs...  21.5 us
  transfers between devices with their start and end apart: 97, of which 45 were waited for; matrix products, arithmetic and copies ran while one was open for 23% of the time, Pallas kernels for 27%

profile of v4, /device:TPU:0, one launch (start us, length us, event | category | flops | bytes accessed | tf_op | source)
XLA Modules:
  0.0 765.3 jit_solution(4262313217881694061)
XLA Ops:
  51.0 18.8 %collective-permute-done.4 = bf16[512,1024]{1,0:T(8,128)(2,1)} collective-permute-done((bf16[512,1024]{1,0:T(8,128)(2,1)}, bf16[512,1024]{1,0:T(8,128)(2,1)}, u32[]{:S(2)}, u32[]{:S(2)}) %collective-permute-start.4) | collective-permute-done | bytes 1048608 | tf_op jit(solution)/shard_map/ppermute | solution.py:567
  79.5 8.6 %attention_forward.2 = (bf16[1024,256]{1,0:T(8,128)(2,1)S(1)}, bf16[1024,128]{1,0:T(8,128)(2,1)S(1)}, bf16[1024,128]{1,0:T(8,128)(2,1)S(1)}, bf16[1024,256]{1,0:...) custom-call(s32[1]{0:T(128)} %bitcast.8.me_ref, bf16[1024,1024]{1,0:T(8,128)(2,1)S(1)} %fusion.2.x_ref, ...), custom_call_target="tpu_custom_call" | custom-call | flops 2684354560 | bytes 12582912 | tf_op jit(solution)/shard_map/attention_forward/pallas_call | solution.py:131
  122.6 8.7 %collective-permute-done.11 = bf16[256,1024]{1,0:T(8,128)(2,1)S(1)} collective-permute-done((bf16[256,1024]{1,0:T(8,128)(2,1)S(1)}, bf16[256,1024]{1,0:T(8,128)(2,1)S(1)}, u32[]{:S(2)}, u32[]{:S(2)}) %collective-permute-start.11) | collective-permute-done | bytes 524320 | tf_op jit(solution)/shard_map/ppermute | solution.py:567
  151.2 10.4 %experts_up.4 = (bf16[1024,1024]{1,0:T(8,128)(2,1)}, bf16[1024,1024]{1,0:T(8,128)(2,1)}, bf16[1024,1024]{1,0:T(8,128)(2,1)}, f32[1024,128]{1,0:T(8,128)}, f32[1024,128]{1,0:T(8,128)}) custom-call(s32[1]{0:T(128)S(6)} %mul.209.base_ref, bf16[1024,1024]{1,0:T(8,128)(2,1)} %constant_dynamic-update-slice_fusion.40.x_ref.xn_ref, ...), custom_call_target="tpu_custom_call" | custom-call | flops 4294967296 | bytes 23068672 | tf_op jit(solution)/shard_map/experts_up/pallas_call | solution.py:290
  162.9 10.4 %experts_up.5 = (bf16[1024,1024]{1,0:T(8,128)(2,1)}, bf16[1024,1024]{1,0:T(8,128)(2,1)}, bf16[1024,1024]{1,0:T(8,128)(2,1)}, f32[1024,128]{1,0:T(8,128)}, f32[1024,128]{1,0:T(8,128)}) custom-call(s32[1]{0:T(128)S(6)} %mul.209.base_ref, bf16[1024,1024]{1,0:T(8,128)(2,1)} %copy-done.84, ...), custom_call_target="tpu_custom_call" | custom-call | flops 4294967296 | bytes 23068672 | tf_op jit(solution)/shard_map/experts_up/pallas_call | solution.py:290
  192.0 11.3 %collective-permute-done.18 = bf16[256,1024]{1,0:T(8,128)(2,1)S(1)} collective-permute-done((bf16[256,1024]{1,0:T(8,128)(2,1)S(1)}, bf16[256,1024]{1,0:T(8,128)(2,1)S(1)}, u32[]{:S(2)}, u32[]{:S(2)}) %collective-permute-start.18) | collective-permute-done | bytes 524320 | tf_op jit(solution)/shard_map/ppermute | solution.py:567
  235.8 9.2 %collective-permute-done.25 = bf16[512,1024]{1,0:T(8,128)(2,1)S(1)} collective-permute-done((bf16[512,1024]{1,0:T(8,128)(2,1)}, bf16[512,1024]{1,0:T(8,128)(2,1)S(1)}, u32[]{:S(2)}, u32[]{:S(2)}) %collective-permute-start.25) | collective-permute-done | bytes 1048608 | tf_op jit(solution)/shard_map/ppermute | solution.py:567
  274.3 12.7 %collective-permute-done.28 = bf16[256,1024]{1,0:T(8,128)(2,1)S(1)} collective-permute-done((bf16[256,1024]{1,0:T(8,128)(2,1)S(1)}, bf16[256,1024]{1,0:T(8,128)(2,1)S(1)}, u32[]{:S(2)}, u32[]{:S(2)}) %collective-permute-start.28) | collective-permute-done | bytes 524320 | tf_op jit(solution)/shard_map/ppermute | solution.py:567
  335.3 10.8 %experts_up.6 = (bf16[1024,1024]{1,0:T(8,128)(2,1)}, bf16[1024,1024]{1,0:T(8,128)(2,1)}, bf16[1024,1024]{1,0:T(8,128)(2,1)}, f32[1024,128]{1,0:T(8,128)}, f32[1024,128]{1,0:T(8,128)}) custom-call(s32[1]{0:T(128)S(6)} %mul.209.base_ref, bf16[1024,1024]{1,0:T(8,128)(2,1)} %constant_dynamic-update-slice_fusion.76.x_ref.xn_ref, ...), custom_call_target="tpu_custom_call" | custom-call | flops 4294967296 | bytes 23068672 | tf_op jit(solution)/shard_map/experts_up/pallas_call | solution.py:290
  347.5 10.4 %experts_up.7 = (bf16[1024,1024]{1,0:T(8,128)(2,1)}, bf16[1024,1024]{1,0:T(8,128)(2,1)}, bf16[1024,1024]{1,0:T(8,128)(2,1)}, f32[1024,128]{1,0:T(8,128)}, f32[1024,128]{1,0:T(8,128)}) custom-call(s32[1]{0:T(128)S(6)} %mul.209.base_ref, bf16[1024,1024]{1,0:T(8,128)(2,1)} %copy-done.85, ...), custom_call_target="tpu_custom_call" | custom-call | flops 4294967296 | bytes 23068672 | tf_op jit(solution)/shard_map/experts_up/pallas_call | solution.py:290
  357.9 8.6 %expert_weights.6 = bf16[512,2048]{1,0:T(8,128)(2,1)} custom-call(bf16[1024,1024]{1,0:T(8,128)(2,1)} %constant_dynamic-update-slice_fusion.88.xn_ref.dy_ref, bf16[1024,1024]{1,0:T(8,128)(2,1)} %collective-permute-done.38.xf_ref.dy_ref, bf16[1024,1024]{1,0:T(8,128)(2,1)} %get-tuple-element.169.rn_ref.a_ref, bf16[1024,1024]{1,0:T(8,128)(2,1)} %get-tuple-element.170.rf_ref.a_ref), custom_call_target="tpu_custom_call" | custom-call | flops 4294967296 | bytes 12582912 | tf_op jit(solution)/shard_map/expert_weights/pallas_call | solution.py:407
  366.5 14.8 %experts_backward.4 = (bf16[1024,1024]{1,0:T(8,128)(2,1)}, bf16[1024,1024]{1,0:T(8,128)(2,1)}, bf16[1024,1152]{1,0:T(8,128)(2,1)}) custom-call(s32[1]{0:T(128)S(6)} %mul.209.base_ref, bf16[1024,1024]{1,0:T(8,128)(2,1)} %constant_dynamic-update-slice_fusion.88.xn_ref.dy_ref, bf16[512,4096]{1,0:T(8,128)(2,1)} %all-gather.15.cloned.1.call-done.ga_ref.gb_ref.ua_ref.ub_ref, ...), custom_call_target="tpu_custom_call" | custom-call | flops 6442450944 | bytes 39845888 | tf_op jit(solution)/shard_map/experts_backward/pallas_call | solution.py:377
  381.3 14.9 %experts_backward.5 = (bf16[1024,1024]{1,0:T(8,128)(2,1)}, bf16[1024,1024]{1,0:T(8,128)(2,1)}, bf16[1024,1152]{1,0:T(8,128)(2,1)}) custom-call(s32[1]{0:T(128)S(6)} %mul.209.base_ref, bf16[1024,1024]{1,0:T(8,128)(2,1)} %collective-permute-done.38.xf_ref.dy_ref, bf16[512,4096]{1,0:T(8,128)(2,1)} %all-gather.15.cloned.1.call-done.ga_ref.gb_ref.ua_ref.ub_ref, ...), custom_call_target="tpu_custom_call" | custom-call | flops 6442450944 | bytes 39845888 | tf_op jit(solution)/shard_map/experts_backward/pallas_call | solution.py:377
  423.3 8.7 %expert_weights.8 = bf16[512,2048]{1,0:T(8,128)(2,1)} custom-call(bf16[1024,1024]{1,0:T(8,128)(2,1)} %constant_dynamic-update-slice_fusion.76.x_ref.xn_ref, bf16[1024,1024]{1,0:T(8,128)(2,1)} %copy-done.85, bf16[1024,1024]{1,0:T(8,128)(2,1)} %get-tuple-element.189.rn_ref, bf16[1024,1024]{1,0:T(8,128)(2,1)} %get-tuple-element.190.rf_ref), custom_call_target="tpu_custom_call" | custom-call | flops 4294967296 | bytes 12582912 | tf_op jit(solution)/shard_map/expert_weights/pallas_call | solution.py:407
  453.7 8.7 %expert_weights.7 = bf16[512,2048]{1,0:T(8,128)(2,1)} custom-call(bf16[1024,1024]{1,0:T(8,128)(2,1)} %constant_dynamic-update-slice_fusion.76.x_ref.xn_ref, bf16[1024,1024]{1,0:T(8,128)(2,1)} %copy-done.85, bf16[1024,1024]{1,0:T(8,128)(2,1)} %get-tuple-element.175.rn_ref, bf16[1024,1024]{1,0:T(8,128)(2,1)} %get-tuple-element.176.rf_ref), custom_call_target="tpu_custom_call" | custom-call | flops 4294967296 | bytes 12582912 | tf_op jit(solution)/shard_map/expert_weights/pallas_call | solution.py:407
  471.4 14.9 %attention_backward.2 = (bf16[1024,512]{1,0:T(8,128)(2,1)S(1)}, bf16[1024,1024]{1,0:T(8,128)(2,1)}) custom-call(s32[1]{0:T(128)} %bitcast.8.me_ref, bf16[1024,1024]{1,0:T(8,128)(2,1)} %pad_maximum_fusion.2.dy_ref, bf16[512,1024]{1,0:T(8,128)(2,1)S(1)} %copy-done.7, bf16[512,1024]{1,0:T(8,128)(2,1)S(1)} %copy-done.5, bf16[1024,256]{1,0:T(8,128)(2,1)S(1)} %copy-done.52, ...), custom_call_target="tpu_custom_call" | custom-call | flops 4294967296 | bytes 12582912 | tf_op jit(solution)/shard_map/attention_backward/pallas_call | solution.py:204
  517.1 10.1 %collective-permute-done.55 = bf16[256,1024]{1,0:T(8,128)(2,1)S(1)} collective-permute-done((bf16[256,1024]{1,0:T(8,128)(2,1)}, bf16[256,1024]{1,0:T(8,128)(2,1)S(1)}, u32[]{:S(2)}, u32[]{:S(2)}) %collective-permute-start.55) | collective-permute-done | bytes 524320 | tf_op jit(solution)/shard_map/ppermute | solution.py:567
  546.4 14.8 %experts_backward.6 = (bf16[1024,1024]{1,0:T(8,128)(2,1)}, bf16[1024,1024]{1,0:T(8,128)(2,1)}, bf16[1024,1152]{1,0:T(8,128)(2,1)}) custom-call(s32[1]{0:T(128)S(6)} %mul.209.base_ref, bf16[1024,1024]{1,0:T(8,128)(2,1)} %copy-done.81, bf16[512,4096]{1,0:T(8,128)(2,1)} %all-gather.9.cloned.1.call-done.ga_ref.gb_ref.ua_ref.ub_ref, ...), custom_call_target="tpu_custom_call" | custom-call | flops 6442450944 | bytes 39845888 | tf_op jit(solution)/shard_map/experts_backward/pallas_call | solution.py:377
  561.3 8.7 %expert_weights.9 = bf16[512,2048]{1,0:T(8,128)(2,1)} custom-call(bf16[1024,1024]{1,0:T(8,128)(2,1)} %copy-done.81, bf16[1024,1024]{1,0:T(8,128)(2,1)} %collective-permute-done.59.xf_ref.dy_ref, bf16[1024,1024]{1,0:T(8,128)(2,1)} %get-tuple-element.144.a_ref.rn_ref, bf16[1024,1024]{1,0:T(8,128)(2,1)} %get-tuple-element.146.a_ref.rf_ref), custom_call_target="tpu_custom_call" | custom-call | flops 4294967296 | bytes 12582912 | tf_op jit(solution)/shard_map/expert_weights/pallas_call | solution.py:407
  570.2 14.9 %experts_backward.7 = (bf16[1024,1024]{1,0:T(8,128)(2,1)}, bf16[1024,1024]{1,0:T(8,128)(2,1)}, bf16[1024,1152]{1,0:T(8,128)(2,1)}) custom-call(s32[1]{0:T(128)S(6)} %mul.209.base_ref, bf16[1024,1024]{1,0:T(8,128)(2,1)} %collective-permute-done.59.xf_ref.dy_ref, bf16[512,4096]{1,0:T(8,128)(2,1)} %all-gather.9.cloned.1.call-done.ga_ref.gb_ref.ua_ref.ub_ref, ...), custom_call_target="tpu_custom_call" | custom-call | flops 6442450944 | bytes 39845888 | tf_op jit(solution)/shard_map/experts_backward/pallas_call | solution.py:377
  594.7 8.7 %expert_weights.10 = bf16[512,2048]{1,0:T(8,128)(2,1)} custom-call(bf16[1024,1024]{1,0:T(8,128)(2,1)} %constant_dynamic-update-slice_fusion.40.x_ref.xn_ref, bf16[1024,1024]{1,0:T(8,128)(2,1)} %copy-done.84, bf16[1024,1024]{1,0:T(8,128)(2,1)} %get-tuple-element.207.rn_ref, bf16[1024,1024]{1,0:T(8,128)(2,1)} %get-tuple-element.208.rf_ref), custom_call_target="tpu_custom_call" | custom-call | flops 4294967296 | bytes 12582912 | tf_op jit(solution)/shard_map/expert_weights/pallas_call | solution.py:407
  635.4 8.6 %expert_weights.11 = bf16[512,2048]{1,0:T(8,128)(2,1)} custom-call(bf16[1024,1024]{1,0:T(8,128)(2,1)} %constant_dynamic-update-slice_fusion.40.x_ref.xn_ref, bf16[1024,1024]{1,0:T(8,128)(2,1)} %copy-done.84, bf16[1024,1024]{1,0:T(8,128)(2,1)} %get-tuple-element.213.rn_ref, bf16[1024,1024]{1,0:T(8,128)(2,1)} %get-tuple-element.214.rf_ref), custom_call_target="tpu_custom_call" | custom-call | flops 4294967296 | bytes 12582912 | tf_op jit(solution)/shard_map/expert_weights/pallas_call | solution.py:407
  672.6 15.3 %attention_backward.3 = (bf16[1024,512]{1,0:T(8,128)(2,1)S(1)}, bf16[1024,1024]{1,0:T(8,128)(2,1)}) custom-call(s32[1]{0:T(128)} %bitcast.8.me_ref, bf16[1024,1024]{1,0:T(8,128)(2,1)} %pad_maximum_fusion.3.dy_ref, bf16[512,1024]{1,0:T(8,128)(2,1)S(1)} %copy-done.1, bf16[512,1024]{1,0:T(8,128)(2,1)S(1)} %copy-done.3, bf16[1024,256]{1,0:T(8,128)(2,1)S(1)} %copy-done.48, ...), custom_call_target="tpu_custom_call" | custom-call | flops 4294967296 | bytes 12582912 | tf_op jit(solution)/shard_map/attention_backward/pallas_call | solution.py:204
  701.5 10.7 %collective-permute-done.75 = bf16[512,896]{1,0:T(8,128)(2,1)} collective-permute-done((bf16[512,896]{1,0:T(8,128)(2,1)S(1)}, bf16[512,896]{1,0:T(8,128)(2,1)}, u32[]{:S(2)}, u32[]{:S(2)}) %collective-permute-start.75) | collective-permute-done | bytes 917536 | tf_op jit(solution)/shard_map/ppermute | solution.py:567
  (714 shorter events, 475.0 us)
Async XLA Ops:
  7.2 37.6 %all-gather.7.cloned.1.call-start = ((), (), s32[]{:S(2)}) async-start(), calls=%async_computation.8 | async-start | bytes 1310720 | tf_op jit(solution)/shard_map/all_gather | solution.py:647
  14.0 137.2 %all-gather.9.cloned.1.call-start = ((), (), s32[]{:S(2)}) async-start(), calls=%async_computation.9 | async-start | bytes 5242880 | tf_op jit(solution)/shard_map/all_gather | solution.py:647
  20.1 28.9 %collective-permute-start.1 = (bf16[256,1024]{1,0:T(8,128)(2,1)}, bf16[256,1024]{1,0:T(8,128)(2,1)}, u32[]{:S(2)}, u32[]{:S(2)}) collective-permute-start(bf16[256,1024]{1,0:T(8,128)(2,1)} %constant_dynamic-update-slice_fusion), channel_id=1, source_target_pairs={{0,1},{1,0},{2,3},{3,2},{4,5},{5,4},{6,7},{7,6},{8,9},{9,8},{10,11... | collective-permute-start | bytes 1572872 | tf_op jit(solution)/shard_map/ppermute | solution.py:567
  44.8 25.1 %collective-permute-start.4 = (bf16[512,1024]{1,0:T(8,128)(2,1)}, bf16[512,1024]{1,0:T(8,128)(2,1)}, u32[]{:S(2)}, u32[]{:S(2)}) collective-permute-start(bf16[512,1024]{1,0:T(8,128)(2,1)} %all-gather.7.cloned.1.call-done), channel_id=1, source_target_pairs={{0,4},{4,0},{8,12},{12,8},{16,20},{20,16},{24,28},{28,24},{1,5},{5... | collective-permute-start | bytes 3145736 | tf_op jit(solution)/shard_map/ppermute | solution.py:567
  48.8 126.6 %all-gather.11.cloned.1.call-start = ((), (), s32[]{:S(2)}) async-start(), calls=%async_computation.10 | async-start | bytes 2621440 | tf_op jit(solution)/shard_map/all_gather | solution.py:647
  75.4 42.9 %collective-permute-start.16 = (bf16[8,128,128]{2,1,0:T(8,128)(2,1)}, bf16[8,128,128]{2,1,0:T(8,128)(2,1)}, u32[]{:S(2)}, u32[]{:S(2)}) collective-permute-start(bf16[8,128,128]{2,1,0:T(8,128)(2,1)} %get-tuple-element.145), channel_id=1, source_target_pairs={{0,4},{4,0},{8,12},{12,8},{16,20},{20,16},{24,28},{28,24},{1,5},{5... | collective-permute-start | bytes 786440 | tf_op jit(solution)/shard_map/ppermute | solution.py:567
  76.8 33.6 %collective-permute-start.9 = (bf16[16,128,128]{2,1,0:T(8,128)(2,1)}, bf16[16,128,128]{2,1,0:T(8,128)(2,1)}, u32[]{:S(2)}, u32[]{:S(2)}) collective-permute-start(bf16[16,128,128]{2,1,0:T(8,128)(2,1)} %pad_maximum_fusion.8), channel_id=1, source_target_pairs={{0,4},{4,0},{8,12},{12,8},{16,20},{20,16},{24,28},{28,24},{1,5},{5... | collective-permute-start | bytes 1572872 | tf_op jit(solution)/shard_map/ppermute | solution.py:567
  121.9 99.7 %all-gather.13.cloned.1.call-start = ((), (), s32[]{:S(2)}) async-start(), calls=%async_computation.11 | async-start | bytes 1310720 | tf_op jit(solution)/shard_map/all_gather | solution.py:647
  151.1 184.2 %all-gather.15.cloned.1.call-start = ((), (), s32[]{:S(2)}) async-start(), calls=%async_computation.12 | async-start | bytes 5242880 | tf_op jit(solution)/shard_map/all_gather | solution.py:647
  180.8 185.8 %all-gather.17.cloned.1.call-start = ((), (), s32[]{:S(2)}) async-start(), calls=%async_computation.13 | async-start | bytes 2621440 | tf_op jit(solution)/shard_map/all_gather | solution.py:647
  260.3 31.1 %collective-permute-start.35 = (bf16[256,1024]{1,0:T(8,128)(2,1)S(1)}, bf16[256,1024]{1,0:T(8,128)(2,1)}, u32[]{:S(2)}, u32[]{:S(2)}) collective-permute-start(bf16[256,1024]{1,0:T(8,128)(2,1)S(1)} %constant_dynamic-update-slice_fusion.80), channel_id=1, source_target_pairs={{0,4},{4,0},{8,12},{12,8},{16,20},{20,16},{24,28},{28,24},{1,5},{5... | collective-permute-start | bytes 1572872 | tf_op jit(solution)/shard_map/ppermute | solution.py:567
  261.8 27.3 %collective-permute-start.34 = (bf16[256,1024]{1,0:T(8,128)(2,1)S(1)}, bf16[256,1024]{1,0:T(8,128)(2,1)}, u32[]{:S(2)}, u32[]{:S(2)}) collective-permute-start(bf16[256,1024]{1,0:T(8,128)(2,1)S(1)} %constant_dynamic-update-slice_fusion.80), channel_id=1, source_target_pairs={{0,2},{1,3},{2,0},{3,1},{4,6},{5,7},{6,4},{7,5},{8,10},{9,11},{10,... | collective-permute-start | bytes 1572872 | tf_op jit(solution)/shard_map/ppermute | solution.py:567
  264.0 225.4 %reduce-scatter.9.cloned.1.call-start = ((), (), s32[]{:S(2)}) async-start(), calls=%async_computation.14 | async-start | bytes 2621440 | tf_op jit(solution)/shard_map/reduce_scatter | solution.py:650
  396.8 100.2 %reduce-scatter.11.cloned.1.call-start = ((), (), s32[]{:S(2)}) async-start(), calls=%async_computation.15 | async-start | bytes 2621440 | tf_op jit(solution)/shard_map/reduce_scatter | solution.py:650
  432.0 213.7 %reduce-scatter.13.cloned.1.call-start = ((), (), s32[]{:S(2)}) async-start(), calls=%async_computation.16 | async-start | bytes 2621440 | tf_op jit(solution)/shard_map/reduce_scatter | solution.py:650
  466.1 32.8 %collective-permute-start.40 = (bf16[1024,1024]{1,0:T(8,128)(2,1)}, bf16[1024,1024]{1,0:T(8,128)(2,1)}, u32[]{:S(2)}, u32[]{:S(2)}) collective-permute-start(bf16[1024,1024]{1,0:T(8,128)(2,1)} %experts_down.7), channel_id=1, source_target_pairs={{0,1},{1,0},{2,3},{3,2},{4,5},{5,4},{6,7},{7,6},{8,9},{9,8},{10,11... | collective-permute-start | bytes 6291464 | tf_op jit(solution)/shard_map/ppermute | solution.py:567
  466.6 181.4 %reduce-scatter.15.cloned.1.call-start = ((), (), s32[]{:S(2)}) async-start(), calls=%async_computation.17 | async-start | bytes 2293760 | tf_op jit(solution)/shard_map/reduce_scatter | solution.py:650
  530.9 161.6 %reduce-scatter.23.cloned.1.call-start = ((), (), s32[]{:S(2)}) async-start(), calls=%async_computation.21 | async-start | bytes 2621440 | tf_op jit(solution)/shard_map/reduce_scatter | solution.py:650
  544.3 40.9 %collective-permute-start.42 = (bf16[256,1024]{1,0:T(8,128)(2,1)}, bf16[256,1024]{1,0:T(8,128)(2,1)}, u32[]{:S(2)}, u32[]{:S(2)}) collective-permute-start(bf16[256,1024]{1,0:T(8,128)(2,1)} %get-tuple-element.332), channel_id=1, source_target_pairs={{0,2},{1,3},{2,0},{3,1},{4,6},{5,7},{6,4},{7,5},{8,10},{9,11},{10,... | collective-permute-start | bytes 1572872 | tf_op jit(solution)/shard_map/ppermute | solution.py:567
  545.1 40.1 %collective-permute-start.41 = (bf16[256,1024]{1,0:T(8,128)(2,1)}, bf16[256,1024]{1,0:T(8,128)(2,1)}, u32[]{:S(2)}, u32[]{:S(2)}) collective-permute-start(bf16[256,1024]{1,0:T(8,128)(2,1)} %get-tuple-element.333), channel_id=1, source_target_pairs={{0,4},{4,0},{8,12},{12,8},{16,20},{20,16},{24,28},{28,24},{1,5},{5... | collective-permute-start | bytes 1572872 | tf_op jit(solution)/shard_map/ppermute | solution.py:567
  570.0 163.1 %reduce-scatter.17.cloned.1.call-start = ((), (), s32[]{:S(2)}) async-start(), calls=%async_computation.18 | async-start | bytes 2621440 | tf_op jit(solution)/shard_map/reduce_scatter | solution.py:650
  611.7 124.1 %reduce-scatter.19.cloned.1.call-start = ((), (), s32[]{:S(2)}) async-start(), calls=%async_computation.19 | async-start | bytes 2621440 | tf_op jit(solution)/shard_map/reduce_scatter | solution.py:650
  644.1 104.7 %reduce-scatter.21.cloned.1.call-start = ((), (), s32[]{:S(2)}) async-start(), calls=%async_computation.20 | async-start | bytes 1146880 | tf_op jit(solution)/shard_map/reduce_scatter | solution.py:650
  701.0 30.3 %collective-permute-start.72 = (bf16[256,1024]{1,0:T(8,128)(2,1)}, bf16[256,1024]{1,0:T(8,128)(2,1)}, u32[]{:S(2)}, u32[]{:S(2)}) collective-permute-start(bf16[256,1024]{1,0:T(8,128)(2,1)} %get-tuple-element.338), channel_id=1, source_target_pairs={{0,1},{1,0},{2,3},{3,2},{4,5},{5,4},{6,7},{7,6},{8,9},{9,8},{10,11... | collective-permute-start | bytes 1572872 | tf_op jit(solution)/shard_map/ppermute | solution.py:567
  (207 other events, 2537.9 us)
Sparse Core Ops, SparseCore 0:
  14.1 30.6 all-gather.6
  48.9 80.0 all-gather.8
  130.6 44.7 all-gather.10
  177.4 26.1 all-gather.12
  205.0 80.2 all-gather.14
  286.7 44.7 all-gather.16
  396.9 41.3 reduce-scatter.8
  440.7 43.1 reduce-scatter.10
  486.2 43.1 reduce-scatter.12
  531.7 38.7 reduce-scatter.14
  572.9 42.9 reduce-scatter.22
  618.1 43.2 reduce-scatter.16
  663.8 43.1 reduce-scatter.18
  714.7 21.7 reduce-scatter.20

commit v5 on v4

--- a/solution.py
+++ b/solution.py
@@ -609,21 +609,24 @@
     return piece, piece(2, 4).astype(BF16), piece(6, 8).astype(BF16)
 
 
-def pair_sum(piece, x_first, y_first):
+def pair_sum(piece, x_first, y_first, meanwhile=None):
     half = x_first.shape[0] // 2
-    y_second = swap((piece(1, 2) + x_first[half:].astype(F32)).astype(BF16), "y")
-    x_second = swap((piece(5, 6) + y_first[half:].astype(F32)).astype(BF16), "x")
+    to_y = (piece(1, 2) + x_first[half:].astype(F32)).astype(BF16)
+    to_x = (piece(5, 6) + y_first[half:].astype(F32)).astype(BF16)
+    y_second, x_second = swap(to_y, "y"), swap(to_x, "x")
+    if meanwhile is not None:
+        y_second = after(y_second, *meanwhile((to_x, to_y)))
     upper = piece(0, 1) + x_first[:half].astype(F32) + y_second.astype(F32)
     lower = piece(4, 5) + y_first[:half].astype(F32) + x_second.astype(F32)
     return jnp.concatenate([upper, lower], axis=0)
 
 
-def narrow_pair(near, far, meanwhile=None):
+def narrow_pair(near, far, meanwhile=None, later=None):
     piece, to_x, to_y = pair_pieces(near, far)
     x_first, y_first = swap(to_x, "x"), swap(to_y, "y")
     if meanwhile is not None:
-        x_first = after(x_first, *meanwhile(to_x))
-    return pair_sum(piece, x_first, y_first)
+        x_first = after(x_first, *meanwhile((to_x, to_y)))
+    return pair_sum(piece, x_first, y_first, later)
 
 
 def sum_over_tensor(values):
@@ -830,23 +833,29 @@
             result_first = swap(result_x, "x"), swap(result_y, "y")
             moe_part = after(moe_part, *result_first)
         made = []
-
-        def meanwhile(point, active=active, down=down, made=made, last=layer == LAYER_COUNT - 1, right=grad_gate):
+        last = layer == LAYER_COUNT - 1
+
+        def meanwhile(point, active=active, down=down, made=made, last=last, right=grad_gate):
             if last:
-                held = after(active, point)
+                held = after(active, *point)
                 made.extend(experts_down(held[n], down) for n in (1, 0))
             else:
-                made.append(expert_weights(hidden_moe, after(right, point)))
+                made.append(expert_weights(hidden_moe, after(right, point[0])))
             return made
 
-        own = narrow_pair(*moe_part, meanwhile)
-        if layer == LAYER_COUNT - 1:
-            far, near = made
+        def later(point, made=made, right=grad_gate if last else grad_up):
+            made.append(expert_weights(hidden_moe, after(right, *point)))
+            return made[-1:]
+
+        own = narrow_pair(*moe_part, meanwhile, later)
+        if last:
+            far, near, grad_gate = made
             result_piece, result_x, result_y = pair_pieces(near, far)
-            grad_gate = expert_weights(hidden_moe, after(grad_gate, far, near))
         else:
-            (grad_gate,) = made
+            grad_gate, grad_up = made
         grad_gate = data.scatter(grad_gate)
+        if not last:
+            grad_up = data.scatter(grad_up)
         grad_moe_own, grad_pairs = own[:, :width], own[:, width:] * own_of(kept)
         own_probs = own_of(probs)
         grad_chosen = own_probs * (grad_pairs - jnp.sum(own_probs * grad_pairs, axis=-1, keepdims=True))
@@ -858,21 +867,22 @@
         grad = grad + normalize_back(grad_moe_own, normed_moe, scale_moe, gain_moe)
         grad_low = grad.astype(BF16)
         made = []
-
-        def meanwhile(point, made=made, right=grad_up):
-            made.append(expert_weights(hidden_moe, after(right, point)))
-            return made
-
-        if layer == 0:
+        if last:
+
+            def meanwhile(point, made=made, right=grad_up):
+                made.append(expert_weights(hidden_moe, after(right, point)))
+                return made
+
+        else:
             later_pack, _, later_up, _ = pieces[0]
 
-            def meanwhile(point, made=made, first=meanwhile):
-                partners.append(data.from_partner(later_up, 1, point))
-                partners.append(data.from_partner(later_pack, 1, point))
-                return first(point) + partners[2:]
+            def meanwhile(point):
+                partners.extend(data.from_partner(part, 1, point) for part in (later_up, later_pack))
+                return partners[2:]
 
         grad_all = widen(grad_low, meanwhile)
-        grad_up = data.scatter(made[0])
+        if last:
+            grad_up = data.scatter(made[0])
         grad_qkv, attn_part = attention_backward(me_array, grad_all, pack, q, k, v, lse, cos, sin)
         pack_product = attention_weights(odd, hidden_attn, grad_qkv, grad_all, mixed, low_moe, grad_logits)
         if layer == LAYER_COUNT - 1:

time: 772 us -> 766 us (level)
  waiting for transfers between devices: 234 us -> 225 us
    ppermute x83, waiting for transfers between devices: 231 us -> 223 us  [swap(): return lax.ppermute(values, axis, [(i, i ^ bit) for i in range(size)])]
    unnamed x343 -> x353, local copies, waits for them, and re-layouts: 65.1 us -> 66.6 us
  transfers between devices with their start and end apart: 97 -> 97, of which waited for: 45 -> 44; matrix products, arithmetic and copies ran while one was open for 23% -> 22% of each run, Pallas kernels for 27% -> 28%
where the time goes in v5:
time: 766 us; the launch traced here: 759 us
  Pallas kernels  239 us (31%)
  waiting for transfers between devices  225 us (29%)
  local copies, waits for them, and re-layouts  111 us (14%)
  other arithmetic  83.3 us (11%)
  starting transfers between devices  73.3 us (10%)
  between operations  16.5 us (2%)
  matrix products  9.87 us (1%)
    ppermute x83, waiting for transfers between devices, swap(): return lax.ppermute(values, axis, [(i, i ^ bit) for i in range(size)])  223 us
    ppermute x83, starting transfers between devices, swap(): return lax.ppermute(values, axis, [(i, i ^ bit) for i in range(size)])  71.6 us
    unnamed x353, local copies, waits for them, and re-layouts  66.6 us
    pallas_call x4, Pallas kernels, experts_backward(): pl.pallas_call(experts_backward_kernel, grid=(steps,), in_specs=[SMEM_SPE...  59.5 us
    pallas_call x6, Pallas kernels, expert_weights(): pl.pallas_call(expert_weights_kernel, grid=(2,), in_specs=[pl.BlockSpec((...  51.9 us
    pallas_call x4, Pallas kernels, experts_up(): pl.pallas_call(experts_up_kernel, grid=(steps,), in_specs=[SMEM_SPEC, pl....  42 us
    pallas_call x2, Pallas kernels, attention_backward(): pl.pallas_call(attention_backward_kernel, out_shape=(jax.ShapeDtypeStruct...  30.2 us
    pallas_call x4, Pallas kernels, experts_down(): pl.pallas_call(experts_down_kernel, grid=(rows // (2 * BLOCK),), in_specs...  21.6 us
  transfers between devices with their start and end apart: 97, of which 44 were waited for; matrix products, arithmetic and copies ran while one was open for 22% of the time, Pallas kernels for 28%

profile of v5, /device:TPU:0, one launch (start us, length us, event | category | flops | bytes accessed | tf_op | source)
XLA Modules:
  0.0 758.8 jit_solution(17761469720758588527)
XLA Ops:
  50.9 19.0 %collective-permute-done.4 = bf16[512,1024]{1,0:T(8,128)(2,1)} collective-permute-done((bf16[512,1024]{1,0:T(8,128)(2,1)}, bf16[512,1024]{1,0:T(8,128)(2,1)}, u32[]{:S(2)}, u32[]{:S(2)}) %collective-permute-start.4) | collective-permute-done | bytes 1048608 | tf_op jit(solution)/shard_map/ppermute | solution.py:567
  123.2 8.8 %collective-permute-done.11 = bf16[256,1024]{1,0:T(8,128)(2,1)S(1)} collective-permute-done((bf16[256,1024]{1,0:T(8,128)(2,1)S(1)}, bf16[256,1024]{1,0:T(8,128)(2,1)S(1)}, u32[]{:S(2)}, u32[]{:S(2)}) %collective-permute-start.11) | collective-permute-done | bytes 524320 | tf_op jit(solution)/shard_map/ppermute | solution.py:567
  151.2 10.4 %experts_up.4 = (bf16[1024,1024]{1,0:T(8,128)(2,1)}, bf16[1024,1024]{1,0:T(8,128)(2,1)}, bf16[1024,1024]{1,0:T(8,128)(2,1)}, f32[1024,128]{1,0:T(8,128)}, f32[1024,128]{1,0:T(8,128)}) custom-call(s32[1]{0:T(128)S(6)} %mul.209.base_ref, bf16[1024,1024]{1,0:T(8,128)(2,1)} %constant_dynamic-update-slice_fusion.40.x_ref.xn_ref, ...), custom_call_target="tpu_custom_call" | custom-call | flops 4294967296 | bytes 23068672 | tf_op jit(solution)/shard_map/experts_up/pallas_call | solution.py:290
  163.0 10.4 %experts_up.5 = (bf16[1024,1024]{1,0:T(8,128)(2,1)}, bf16[1024,1024]{1,0:T(8,128)(2,1)}, bf16[1024,1024]{1,0:T(8,128)(2,1)}, f32[1024,128]{1,0:T(8,128)}, f32[1024,128]{1,0:T(8,128)}) custom-call(s32[1]{0:T(128)S(6)} %mul.209.base_ref, bf16[1024,1024]{1,0:T(8,128)(2,1)} %copy-done.89, ...), custom_call_target="tpu_custom_call" | custom-call | flops 4294967296 | bytes 23068672 | tf_op jit(solution)/shard_map/experts_up/pallas_call | solution.py:290
  191.5 11.3 %collective-permute-done.18 = bf16[256,1024]{1,0:T(8,128)(2,1)S(1)} collective-permute-done((bf16[256,1024]{1,0:T(8,128)(2,1)S(1)}, bf16[256,1024]{1,0:T(8,128)(2,1)S(1)}, u32[]{:S(2)}, u32[]{:S(2)}) %collective-permute-start.18) | collective-permute-done | bytes 524320 | tf_op jit(solution)/shard_map/ppermute | solution.py:567
  235.3 9.3 %collective-permute-done.25 = bf16[512,1024]{1,0:T(8,128)(2,1)S(1)} collective-permute-done((bf16[512,1024]{1,0:T(8,128)(2,1)}, bf16[512,1024]{1,0:T(8,128)(2,1)S(1)}, u32[]{:S(2)}, u32[]{:S(2)}) %collective-permute-start.25) | collective-permute-done | bytes 1048608 | tf_op jit(solution)/shard_map/ppermute | solution.py:567
  273.0 13.4 %collective-permute-done.28 = bf16[256,1024]{1,0:T(8,128)(2,1)S(1)} collective-permute-done((bf16[256,1024]{1,0:T(8,128)(2,1)S(1)}, bf16[256,1024]{1,0:T(8,128)(2,1)S(1)}, u32[]{:S(2)}, u32[]{:S(2)}) %collective-permute-start.28) | collective-permute-done | bytes 524320 | tf_op jit(solution)/shard_map/ppermute | solution.py:567
  334.7 10.8 %experts_up.6 = (bf16[1024,1024]{1,0:T(8,128)(2,1)}, bf16[1024,1024]{1,0:T(8,128)(2,1)}, bf16[1024,1024]{1,0:T(8,128)(2,1)}, f32[1024,128]{1,0:T(8,128)}, f32[1024,128]{1,0:T(8,128)}) custom-call(s32[1]{0:T(128)S(6)} %mul.209.base_ref, bf16[1024,1024]{1,0:T(8,128)(2,1)} %constant_dynamic-update-slice_fusion.76.x_ref.xn_ref, ...), custom_call_target="tpu_custom_call" | custom-call | flops 4294967296 | bytes 23068672 | tf_op jit(solution)/shard_map/experts_up/pallas_call | solution.py:290
  346.9 10.4 %experts_up.7 = (bf16[1024,1024]{1,0:T(8,128)(2,1)}, bf16[1024,1024]{1,0:T(8,128)(2,1)}, bf16[1024,1024]{1,0:T(8,128)(2,1)}, f32[1024,128]{1,0:T(8,128)}, f32[1024,128]{1,0:T(8,128)}) custom-call(s32[1]{0:T(128)S(6)} %mul.209.base_ref, bf16[1024,1024]{1,0:T(8,128)(2,1)} %copy-done.90, ...), custom_call_target="tpu_custom_call" | custom-call | flops 4294967296 | bytes 23068672 | tf_op jit(solution)/shard_map/experts_up/pallas_call | solution.py:290
  357.4 8.6 %expert_weights.6 = bf16[512,2048]{1,0:T(8,128)(2,1)} custom-call(bf16[1024,1024]{1,0:T(8,128)(2,1)} %constant_dynamic-update-slice_fusion.88.xn_ref.dy_ref, bf16[1024,1024]{1,0:T(8,128)(2,1)} %collective-permute-done.38.xf_ref.dy_ref, bf16[1024,1024]{1,0:T(8,128)(2,1)} %get-tuple-element.171.rn_ref.a_ref, bf16[1024,1024]{1,0:T(8,128)(2,1)} %get-tuple-element.172.rf_ref.a_ref), custom_call_target="tpu_custom_call" | custom-call | flops 4294967296 | bytes 12582912 | tf_op jit(solution)/shard_map/expert_weights/pallas_call | solution.py:407
  366.0 14.8 %experts_backward.4 = (bf16[1024,1024]{1,0:T(8,128)(2,1)}, bf16[1024,1024]{1,0:T(8,128)(2,1)}, bf16[1024,1152]{1,0:T(8,128)(2,1)}) custom-call(s32[1]{0:T(128)S(6)} %mul.209.base_ref, bf16[1024,1024]{1,0:T(8,128)(2,1)} %constant_dynamic-update-slice_fusion.88.xn_ref.dy_ref, bf16[512,4096]{1,0:T(8,128)(2,1)} %all-gather.15.cloned.1.call-done.ga_ref.gb_ref.ua_ref.ub_ref, ...), custom_call_target="tpu_custom_call" | custom-call | flops 6442450944 | bytes 39845888 | tf_op jit(solution)/shard_map/experts_backward/pallas_call | solution.py:377
  380.8 14.9 %experts_backward.5 = (bf16[1024,1024]{1,0:T(8,128)(2,1)}, bf16[1024,1024]{1,0:T(8,128)(2,1)}, bf16[1024,1152]{1,0:T(8,128)(2,1)}) custom-call(s32[1]{0:T(128)S(6)} %mul.209.base_ref, bf16[1024,1024]{1,0:T(8,128)(2,1)} %collective-permute-done.38.xf_ref.dy_ref, bf16[512,4096]{1,0:T(8,128)(2,1)} %all-gather.15.cloned.1.call-done.ga_ref.gb_ref.ua_ref.ub_ref, ...), custom_call_target="tpu_custom_call" | custom-call | flops 6442450944 | bytes 39845888 | tf_op jit(solution)/shard_map/experts_backward/pallas_call | solution.py:377
  422.4 8.7 %expert_weights.7 = bf16[512,2048]{1,0:T(8,128)(2,1)} custom-call(bf16[1024,1024]{1,0:T(8,128)(2,1)} %constant_dynamic-update-slice_fusion.76.x_ref.xn_ref, bf16[1024,1024]{1,0:T(8,128)(2,1)} %copy-done.90, bf16[1024,1024]{1,0:T(8,128)(2,1)} %get-tuple-element.175.rn_ref, bf16[1024,1024]{1,0:T(8,128)(2,1)} %get-tuple-element.176.rf_ref), custom_call_target="tpu_custom_call" | custom-call | flops 4294967296 | bytes 12582912 | tf_op jit(solution)/shard_map/expert_weights/pallas_call | solution.py:407
  466.2 14.9 %attention_backward.2 = (bf16[1024,512]{1,0:T(8,128)(2,1)S(1)}, bf16[1024,1024]{1,0:T(8,128)(2,1)}) custom-call(s32[1]{0:T(128)} %bitcast.8.me_ref, bf16[1024,1024]{1,0:T(8,128)(2,1)} %pad_maximum_fusion.2.dy_ref, bf16[512,1024]{1,0:T(8,128)(2,1)S(1)} %copy-done.7, bf16[512,1024]{1,0:T(8,128)(2,1)S(1)} %copy-done.5, bf16[1024,256]{1,0:T(8,128)(2,1)S(1)} %copy-done.56, ...), custom_call_target="tpu_custom_call" | custom-call | flops 4294967296 | bytes 12582912 | tf_op jit(solution)/shard_map/attention_backward/pallas_call | solution.py:204
  518.8 9.2 %collective-permute-done.55 = bf16[256,1024]{1,0:T(8,128)(2,1)S(1)} collective-permute-done((bf16[256,1024]{1,0:T(8,128)(2,1)}, bf16[256,1024]{1,0:T(8,128)(2,1)S(1)}, u32[]{:S(2)}, u32[]{:S(2)}) %collective-permute-start.55) | collective-permute-done | bytes 524320 | tf_op jit(solution)/shard_map/ppermute | solution.py:567
  545.0 14.8 %experts_backward.6 = (bf16[1024,1024]{1,0:T(8,128)(2,1)}, bf16[1024,1024]{1,0:T(8,128)(2,1)}, bf16[1024,1152]{1,0:T(8,128)(2,1)}) custom-call(s32[1]{0:T(128)S(6)} %mul.209.base_ref, bf16[1024,1024]{1,0:T(8,128)(2,1)} %copy-done.86, bf16[512,4096]{1,0:T(8,128)(2,1)} %all-gather.9.cloned.1.call-done.ga_ref.gb_ref.ua_ref.ub_ref, ...), custom_call_target="tpu_custom_call" | custom-call | flops 6442450944 | bytes 39845888 | tf_op jit(solution)/shard_map/experts_backward/pallas_call | solution.py:377
  559.8 8.6 %expert_weights.9 = bf16[512,2048]{1,0:T(8,128)(2,1)} custom-call(bf16[1024,1024]{1,0:T(8,128)(2,1)} %copy-done.86, bf16[1024,1024]{1,0:T(8,128)(2,1)} %collective-permute-done.59.xf_ref.dy_ref, bf16[1024,1024]{1,0:T(8,128)(2,1)} %get-tuple-element.146.a_ref.rn_ref, bf16[1024,1024]{1,0:T(8,128)(2,1)} %get-tuple-element.148.a_ref.rf_ref), custom_call_target="tpu_custom_call" | custom-call | flops 4294967296 | bytes 12582912 | tf_op jit(solution)/shard_map/expert_weights/pallas_call | solution.py:407
  570.8 15.0 %experts_backward.7 = (bf16[1024,1024]{1,0:T(8,128)(2,1)}, bf16[1024,1024]{1,0:T(8,128)(2,1)}, bf16[1024,1152]{1,0:T(8,128)(2,1)}) custom-call(s32[1]{0:T(128)S(6)} %mul.209.base_ref, bf16[1024,1024]{1,0:T(8,128)(2,1)} %collective-permute-done.59.xf_ref.dy_ref, bf16[512,4096]{1,0:T(8,128)(2,1)} %all-gather.9.cloned.1.call-done.ga_ref.gb_ref.ua_ref.ub_ref, ...), custom_call_target="tpu_custom_call" | custom-call | flops 6442450944 | bytes 39845888 | tf_op jit(solution)/shard_map/experts_backward/pallas_call | solution.py:377
  593.4 8.7 %expert_weights.10 = bf16[512,2048]{1,0:T(8,128)(2,1)} custom-call(bf16[1024,1024]{1,0:T(8,128)(2,1)} %constant_dynamic-update-slice_fusion.40.x_ref.xn_ref, bf16[1024,1024]{1,0:T(8,128)(2,1)} %copy-done.89, bf16[1024,1024]{1,0:T(8,128)(2,1)} %get-tuple-element.210.rn_ref, bf16[1024,1024]{1,0:T(8,128)(2,1)} %get-tuple-element.211.rf_ref), custom_call_target="tpu_custom_call" | custom-call | flops 4294967296 | bytes 12582912 | tf_op jit(solution)/shard_map/expert_weights/pallas_call | solution.py:407
  605.7 12.1 %collective-permute-done.61 = bf16[256,1152]{1,0:T(8,128)(2,1)S(1)} collective-permute-done((bf16[256,1152]{1,0:T(8,128)(2,1)}, bf16[256,1152]{1,0:T(8,128)(2,1)S(1)}, u32[]{:S(2)}, u32[]{:S(2)}) %collective-permute-start.61) | collective-permute-done | bytes 589856 | tf_op jit(solution)/shard_map/ppermute | solution.py:567
  622.7 8.7 %expert_weights.11 = bf16[512,2048]{1,0:T(8,128)(2,1)} custom-call(bf16[1024,1024]{1,0:T(8,128)(2,1)} %constant_dynamic-update-slice_fusion.40.x_ref.xn_ref, bf16[1024,1024]{1,0:T(8,128)(2,1)} %copy-done.89, bf16[1024,1024]{1,0:T(8,128)(2,1)} %get-tuple-element.215.rn_ref, bf16[1024,1024]{1,0:T(8,128)(2,1)} %get-tuple-element.216.rf_ref), custom_call_target="tpu_custom_call" | custom-call | flops 4294967296 | bytes 12582912 | tf_op jit(solution)/shard_map/expert_weights/pallas_call | solution.py:407
  643.6 8.6 %collective-permute-done.65 = bf16[256,1024]{1,0:T(8,128)(2,1)} collective-permute-done((bf16[256,1024]{1,0:T(8,128)(2,1)}, bf16[256,1024]{1,0:T(8,128)(2,1)}, u32[]{:S(2)}, u32[]{:S(2)}) %collective-permute-start.65) | collective-permute-done | bytes 524320 | tf_op jit(solution)/shard_map/ppermute | solution.py:567
  665.9 15.3 %attention_backward.3 = (bf16[1024,512]{1,0:T(8,128)(2,1)S(1)}, bf16[1024,1024]{1,0:T(8,128)(2,1)}) custom-call(s32[1]{0:T(128)} %bitcast.8.me_ref, bf16[1024,1024]{1,0:T(8,128)(2,1)} %pad_maximum_fusion.3.dy_ref, bf16[512,1024]{1,0:T(8,128)(2,1)S(1)} %copy-done.1, bf16[512,1024]{1,0:T(8,128)(2,1)S(1)} %copy-done.3, bf16[1024,256]{1,0:T(8,128)(2,1)S(1)} %copy-done.52, ...), custom_call_target="tpu_custom_call" | custom-call | flops 4294967296 | bytes 12582912 | tf_op jit(solution)/shard_map/attention_backward/pallas_call | solution.py:204
  696.0 9.7 %collective-permute-done.75 = bf16[512,896]{1,0:T(8,128)(2,1)} collective-permute-done((bf16[512,896]{1,0:T(8,128)(2,1)S(1)}, bf16[512,896]{1,0:T(8,128)(2,1)}, u32[]{:S(2)}, u32[]{:S(2)}) %collective-permute-start.75) | collective-permute-done | bytes 917536 | tf_op jit(solution)/shard_map/ppermute | solution.py:567
  (722 shorter events, 465.9 us)
Async XLA Ops:
  7.2 37.6 %all-gather.7.cloned.1.call-start = ((), (), s32[]{:S(2)}) async-start(), calls=%async_computation.8 | async-start | bytes 1310720 | tf_op jit(solution)/shard_map/all_gather | solution.py:650
  14.0 137.2 %all-gather.9.cloned.1.call-start = ((), (), s32[]{:S(2)}) async-start(), calls=%async_computation.9 | async-start | bytes 5242880 | tf_op jit(solution)/shard_map/all_gather | solution.py:650
  20.1 28.3 %collective-permute-start.1 = (bf16[256,1024]{1,0:T(8,128)(2,1)}, bf16[256,1024]{1,0:T(8,128)(2,1)}, u32[]{:S(2)}, u32[]{:S(2)}) collective-permute-start(bf16[256,1024]{1,0:T(8,128)(2,1)} %constant_dynamic-update-slice_fusion), channel_id=1, source_target_pairs={{0,1},{1,0},{2,3},{3,2},{4,5},{5,4},{6,7},{7,6},{8,9},{9,8},{10,11... | collective-permute-start | bytes 1572872 | tf_op jit(solution)/shard_map/ppermute | solution.py:567
  44.8 25.1 %collective-permute-start.4 = (bf16[512,1024]{1,0:T(8,128)(2,1)}, bf16[512,1024]{1,0:T(8,128)(2,1)}, u32[]{:S(2)}, u32[]{:S(2)}) collective-permute-start(bf16[512,1024]{1,0:T(8,128)(2,1)} %all-gather.7.cloned.1.call-done), channel_id=1, source_target_pairs={{0,4},{4,0},{8,12},{12,8},{16,20},{20,16},{24,28},{28,24},{1,5},{5... | collective-permute-start | bytes 3145736 | tf_op jit(solution)/shard_map/ppermute | solution.py:567
  48.2 126.6 %all-gather.11.cloned.1.call-start = ((), (), s32[]{:S(2)}) async-start(), calls=%async_computation.10 | async-start | bytes 2621440 | tf_op jit(solution)/shard_map/all_gather | solution.py:650
  75.4 43.5 %collective-permute-start.16 = (bf16[8,128,128]{2,1,0:T(8,128)(2,1)}, bf16[8,128,128]{2,1,0:T(8,128)(2,1)}, u32[]{:S(2)}, u32[]{:S(2)}) collective-permute-start(bf16[8,128,128]{2,1,0:T(8,128)(2,1)} %get-tuple-element.147), channel_id=1, source_target_pairs={{0,4},{4,0},{8,12},{12,8},{16,20},{20,16},{24,28},{28,24},{1,5},{5... | collective-permute-start | bytes 786440 | tf_op jit(solution)/shard_map/ppermute | solution.py:567
  76.8 34.2 %collective-permute-start.9 = (bf16[16,128,128]{2,1,0:T(8,128)(2,1)}, bf16[16,128,128]{2,1,0:T(8,128)(2,1)}, u32[]{:S(2)}, u32[]{:S(2)}) collective-permute-start(bf16[16,128,128]{2,1,0:T(8,128)(2,1)} %pad_maximum_fusion.8), channel_id=1, source_target_pairs={{0,4},{4,0},{8,12},{12,8},{16,20},{20,16},{24,28},{28,24},{1,5},{5... | collective-permute-start | bytes 1572872 | tf_op jit(solution)/shard_map/ppermute | solution.py:567
  90.5 25.1 %collective-permute-start.5 = (bf16[256,1024]{1,0:T(8,128)(2,1)}, bf16[256,1024]{1,0:T(8,128)(2,1)}, u32[]{:S(2)}, u32[]{:S(2)}) collective-permute-start(bf16[256,1024]{1,0:T(8,128)(2,1)} %get-tuple-element.354), channel_id=1, source_target_pairs={{0,1},{1,0},{2,3},{3,2},{4,5},{5,4},{6,7},{7,6},{8,9},{9,8},{10,11... | collective-permute-start | bytes 1572872 | tf_op jit(solution)/shard_map/ppermute | solution.py:567
  122.5 98.6 %all-gather.13.cloned.1.call-start = ((), (), s32[]{:S(2)}) async-start(), calls=%async_computation.11 | async-start | bytes 1310720 | tf_op jit(solution)/shard_map/all_gather | solution.py:650
  151.1 183.6 %all-gather.15.cloned.1.call-start = ((), (), s32[]{:S(2)}) async-start(), calls=%async_computation.12 | async-start | bytes 5242880 | tf_op jit(solution)/shard_map/all_gather | solution.py:650
  180.2 185.8 %all-gather.17.cloned.1.call-start = ((), (), s32[]{:S(2)}) async-start(), calls=%async_computation.13 | async-start | bytes 2621440 | tf_op jit(solution)/shard_map/all_gather | solution.py:650
  259.8 31.0 %collective-permute-start.35 = (bf16[256,1024]{1,0:T(8,128)(2,1)S(1)}, bf16[256,1024]{1,0:T(8,128)(2,1)}, u32[]{:S(2)}, u32[]{:S(2)}) collective-permute-start(bf16[256,1024]{1,0:T(8,128)(2,1)S(1)} %constant_dynamic-update-slice_fusion.80), channel_id=1, source_target_pairs={{0,4},{4,0},{8,12},{12,8},{16,20},{20,16},{24,28},{28,24},{1,5},{5... | collective-permute-start | bytes 1572872 | tf_op jit(solution)/shard_map/ppermute | solution.py:567
  261.2 27.3 %collective-permute-start.34 = (bf16[256,1024]{1,0:T(8,128)(2,1)S(1)}, bf16[256,1024]{1,0:T(8,128)(2,1)}, u32[]{:S(2)}, u32[]{:S(2)}) collective-permute-start(bf16[256,1024]{1,0:T(8,128)(2,1)S(1)} %constant_dynamic-update-slice_fusion.80), channel_id=1, source_target_pairs={{0,2},{1,3},{2,0},{3,1},{4,6},{5,7},{6,4},{7,5},{8,10},{9,11},{10,... | collective-permute-start | bytes 1572872 | tf_op jit(solution)/shard_map/ppermute | solution.py:567
  263.5 221.1 %reduce-scatter.9.cloned.1.call-start = ((), (), s32[]{:S(2)}) async-start(), calls=%async_computation.14 | async-start | bytes 2621440 | tf_op jit(solution)/shard_map/reduce_scatter | solution.py:653
  396.3 100.8 %reduce-scatter.11.cloned.1.call-start = ((), (), s32[]{:S(2)}) async-start(), calls=%async_computation.15 | async-start | bytes 2621440 | tf_op jit(solution)/shard_map/reduce_scatter | solution.py:653
  431.2 207.8 %reduce-scatter.13.cloned.1.call-start = ((), (), s32[]{:S(2)}) async-start(), calls=%async_computation.16 | async-start | bytes 2621440 | tf_op jit(solution)/shard_map/reduce_scatter | solution.py:653
  460.8 38.4 %collective-permute-start.40 = (bf16[1024,1024]{1,0:T(8,128)(2,1)}, bf16[1024,1024]{1,0:T(8,128)(2,1)}, u32[]{:S(2)}, u32[]{:S(2)}) collective-permute-start(bf16[1024,1024]{1,0:T(8,128)(2,1)} %experts_down.7), channel_id=1, source_target_pairs={{0,1},{1,0},{2,3},{3,2},{4,5},{5,4},{6,7},{7,6},{8,9},{9,8},{10,11... | collective-permute-start | bytes 6291464 | tf_op jit(solution)/shard_map/ppermute | solution.py:567
  461.3 180.0 %reduce-scatter.15.cloned.1.call-start = ((), (), s32[]{:S(2)}) async-start(), calls=%async_computation.17 | async-start | bytes 2293760 | tf_op jit(solution)/shard_map/reduce_scatter | solution.py:653
  486.4 23.5 %collective-permute-start.50 = (bf16[256,1024]{1,0:T(8,128)(2,1)}, bf16[256,1024]{1,0:T(8,128)(2,1)}, u32[]{:S(2)}, u32[]{:S(2)}) collective-permute-start(bf16[256,1024]{1,0:T(8,128)(2,1)} %get-tuple-element.348), channel_id=1, source_target_pairs={{0,1},{1,0},{2,3},{3,2},{4,5},{5,4},{6,7},{7,6},{8,9},{9,8},{10,11... | collective-permute-start | bytes 1572872 | tf_op jit(solution)/shard_map/ppermute | solution.py:567
  530.6 157.9 %reduce-scatter.23.cloned.1.call-start = ((), (), s32[]{:S(2)}) async-start(), calls=%async_computation.21 | async-start | bytes 2621440 | tf_op jit(solution)/shard_map/reduce_scatter | solution.py:653
  568.5 158.1 %reduce-scatter.17.cloned.1.call-start = ((), (), s32[]{:S(2)}) async-start(), calls=%async_computation.18 | async-start | bytes 2621440 | tf_op jit(solution)/shard_map/reduce_scatter | solution.py:653
  602.1 127.4 %reduce-scatter.19.cloned.1.call-start = ((), (), s32[]{:S(2)}) async-start(), calls=%async_computation.19 | async-start | bytes 2621440 | tf_op jit(solution)/shard_map/reduce_scatter | solution.py:653
  631.5 110.7 %reduce-scatter.21.cloned.1.call-start = ((), (), s32[]{:S(2)}) async-start(), calls=%async_computation.20 | async-start | bytes 1146880 | tf_op jit(solution)/shard_map/reduce_scatter | solution.py:653
  695.5 29.3 %collective-permute-start.72 = (bf16[256,1024]{1,0:T(8,128)(2,1)}, bf16[256,1024]{1,0:T(8,128)(2,1)}, u32[]{:S(2)}, u32[]{:S(2)}) collective-permute-start(bf16[256,1024]{1,0:T(8,128)(2,1)} %get-tuple-element.346), channel_id=1, source_target_pairs={{0,1},{1,0},{2,3},{3,2},{4,5},{5,4},{6,7},{7,6},{8,9},{9,8},{10,11... | collective-permute-start | bytes 1572872 | tf_op jit(solution)/shard_map/ppermute | solution.py:567
  (212 other events, 2521.2 us)
Sparse Core Ops, SparseCore 0:
  14.1 30.6 all-gather.6
  48.3 80.0 all-gather.8
  130.0 44.7 all-gather.10
  176.8 26.1 all-gather.12
  204.5 80.2 all-gather.14
  286.2 44.7 all-gather.16
  396.5 41.4 reduce-scatter.8
  440.3 43.1 reduce-scatter.10
  485.8 43.1 reduce-scatter.12
  531.3 38.7 reduce-scatter.14
  572.5 42.9 reduce-scatter.22
  617.7 43.1 reduce-scatter.16
  663.3 43.0 reduce-scatter.18
  708.6 24.4 reduce-scatter.20
